TPU v7x, 256 devices: a whole 4x4x8 slice. The times are simulated.
256 devices in a mesh: req: 64 (over y, z, core), rep: 4 (over x).
Axes of the slice: x: 4, y: 4, z: 8, core: 2. Of those that a mesh axis runs over, the one named last changes fastest.
Arguments:
- hidden: bfloat16 [512, 64, 1152], P('rep', 'req'), may hold values from -6 to 6
- norm_gain: float32 [1152], replicated, may hold values from 0.1 to 1.9
- w_qkv: bfloat16 [1152, 1920], replicated, may hold values from -0.1875 to 0.1875
- w_out: bfloat16 [1152, 1152], replicated, may hold values from -0.1875 to 0.1875
- ffn_gain: float32 [1152], replicated, may hold values from 0.1 to 1.9
- w_gate: bfloat16 [1152, 1536], P(None, 'rep'), may hold values from -0.1875 to 0.1875
- w_up: bfloat16 [1152, 1536], P(None, 'rep'), may hold values from -0.1875 to 0.1875
- w_down: bfloat16 [1536, 1152], P('rep'), may hold values from -0.15625 to 0.15625
- cache: bfloat16 [4096, 2, 128, 384], P(('req', 'rep')), may hold values from -363 to 363, as said below
- page_table: int32 [512, 4, 5], P('req', 'rep'), may hold values from 0 to 15, as said below
- cache_len: int32 [512], P('req'), may hold values from 2049 to 2560, as said below
- parents: int32 [512, 64], P('req'), may hold values from 0 to 62, as said below
- accept_leaf: int32 [512], P('req'), may hold values from 0 to 63, as said below
- page_slot: int32 [512], P('req'), may hold values from 0 to 7, as said below
Outputs:
- out: bfloat16 [512, 64, 1152], P('rep', 'req')
- new_pages: bfloat16 [512, 2, 8, 384], P(('req', 'rep'))
Inputs may be any that keep to these rules, and one draw needn't show every extreme that they name: `cache`: no structure is promised. page_table[r, j, s] is the index, among the 16 pages of device j of request r's owner, of the request's logical page s * 4 + j; requests of one owner in aligned blocks of 4 share the pages of logical pages below 16; all other pages are distinct. `cache_len`: every owner holds a request of the largest length. parents[r, 0] = 0; node t >= 1 has depth (t * 7 + 62) // 63 and its parent is a node of the depth before. accept_leaf names a node of depth 8 - 1. `page_slot`: the 8 requests of each owner take each slot once.
All inputs are finite; a program needn't handle non-finite values.
Results may differ from a plain program's by a relative error of at most 0.019.
The roundings to bfloat16 on the way count: a program that leaves them out, or rounds other values in their place, can miss the bound.
Values may be sent and summed in bfloat16 or wider, within the bound.
A program may use at most 128 MiB of HBM per device.

v0:
```python
import jax
import jax.numpy as jnp
from jax import lax
from jax.sharding import PartitionSpec as P

QUERY_HEADS = 18
KEY_VALUE_HEADS = 6
ACC = 8


SCALE = 0.125
EPSILON = 1e-05
THETA = 10000.0


def apply_rotation(values, token_positions, head_count):
    head_columns = values.shape[-1] // head_count
    half_width = head_columns // 2
    shaped = values.reshape(values.shape[:-1] + (head_count, head_columns))
    frequency = THETA ** (-jnp.arange(half_width, dtype=jnp.float32) / half_width)
    angles = token_positions.astype(jnp.float32)[..., None] * frequency
    cosine = jnp.cos(angles)[..., None, :]
    sines = jnp.sin(angles)[..., None, :]
    front_half = shaped[..., :half_width]
    back_half = shaped[..., half_width:]
    turned = jnp.concatenate(
        [front_half * cosine - back_half * sines, back_half * cosine + front_half * sines], axis=-1
    )
    return turned.reshape(values.shape)


def ancestors(parents):
    tree_length = parents.shape[-1]
    identity = jnp.eye(tree_length, dtype=jnp.float32)
    linked = jax.nn.one_hot(parents, tree_length, dtype=jnp.float32)
    reached = jnp.minimum(identity + linked, 1.0)
    for doubling in range(tree_length.bit_length()):
        reached = jnp.minimum(
            jnp.einsum("rts,rsu->rtu", reached, reached, precision=lax.Precision.HIGHEST), 1.0
        )
    return reached


def rms_scaled(values_in, gain):
    scaling = lax.rsqrt(jnp.mean(values_in * values_in, axis=-1, keepdims=True) + EPSILON)
    return (values_in * scaling * gain).astype(jnp.bfloat16)


def project(hidden, norm_gain, w_qkv):
    normed = rms_scaled(hidden.astype(jnp.float32), norm_gain)
    product = jnp.dot(
        normed.reshape(-1, hidden.shape[-1]), w_qkv, preferred_element_type=jnp.float32
    )
    return product.astype(jnp.bfloat16).reshape(hidden.shape[:-1] + (w_qkv.shape[1],))


def attend_part(query_matrix, key_matrix, value_matrix, allowed):
    tree_length = query_matrix.shape[0]
    head_columns = key_matrix.shape[-1]
    grouped_queries = query_matrix.reshape(
        tree_length, KEY_VALUE_HEADS, QUERY_HEADS // KEY_VALUE_HEADS, head_columns
    )
    scores = (
        jnp.einsum(
            "tgrd,sgd->gtrs", grouped_queries, key_matrix, preferred_element_type=jnp.float32
        )
        * SCALE
    )
    scores = jnp.where(allowed[None, :, None, :], scores, -jnp.inf)
    peaks = jnp.max(scores, axis=-1)
    weights = jnp.exp(scores - peaks[..., None])
    totals = jnp.sum(weights, axis=-1)
    summed = jnp.einsum(
        "gtrs,sgd->tgrd",
        weights.astype(jnp.bfloat16),
        value_matrix,
        preferred_element_type=jnp.float32,
    )
    peaks = jnp.transpose(peaks, (1, 0, 2)).reshape(tree_length, QUERY_HEADS)
    totals = jnp.transpose(totals, (1, 0, 2)).reshape(tree_length, QUERY_HEADS)
    return (peaks, totals, summed.reshape(tree_length, QUERY_HEADS * head_columns))


def join_parts(front_part, back_part):
    highest = jnp.maximum(front_part[0], back_part[0])
    front_scale = jnp.exp(front_part[0] - highest)
    back_scale = jnp.exp(back_part[0] - highest)
    totals = front_part[1] * front_scale + back_part[1] * back_scale
    shape_sum = front_part[2].shape
    split_shape = shape_sum[:-1] + (QUERY_HEADS, -1)
    summed = (
        front_part[2].reshape(split_shape) * front_scale[..., None]
        + back_part[2].reshape(split_shape) * back_scale[..., None]
    )
    return (highest, totals, summed.reshape(shape_sum))


def owner_partials(
    queries_all, local_key_rows, local_value_rows, own_reach, cache, page_list, cache_len, own_start
):
    rep_index = lax.axis_index("rep")
    rep_count = lax.axis_size("rep")
    requests = queries_all.shape[0]
    tree_length = queries_all.shape[1]
    owner_page_count = local_key_rows.shape[0]
    slots_count = page_list.shape[1]
    page_length = cache.shape[2]
    head_columns = local_key_rows.shape[-1] // KEY_VALUE_HEADS
    logical = (
        jnp.arange(slots_count, dtype=jnp.int32)[:, None] * rep_count + rep_index
    ) * page_length + jnp.arange(page_length, dtype=jnp.int32)[None, :]
    logical = logical.reshape(slots_count * page_length)

    def per_request(request_item):
        query_matrix, page_ids, cache_end = request_item
        collected_pages = cache[page_ids]
        key_matrix = collected_pages[:, 0].reshape(
            slots_count * page_length, KEY_VALUE_HEADS, head_columns
        )
        value_matrix = collected_pages[:, 1].reshape(
            slots_count * page_length, KEY_VALUE_HEADS, head_columns
        )
        visible = jnp.broadcast_to(
            (logical < cache_end)[None, :], (tree_length, slots_count * page_length)
        )
        return attend_part(query_matrix, key_matrix, value_matrix, visible)

    cached = lax.map(per_request, (queries_all, page_list, cache_len))
    own_queries = lax.dynamic_slice_in_dim(queries_all, own_start, owner_page_count, 0)
    drafted = jax.vmap(attend_part)(
        own_queries,
        local_key_rows.reshape(owner_page_count, tree_length, KEY_VALUE_HEADS, head_columns),
        local_value_rows.reshape(owner_page_count, tree_length, KEY_VALUE_HEADS, head_columns),
        own_reach > 0.5,
    )
    blanks = (
        jnp.full((requests, tree_length, QUERY_HEADS), -jnp.inf, jnp.float32),
        jnp.zeros((requests, tree_length, QUERY_HEADS), jnp.float32),
        jnp.zeros((requests, tree_length, queries_all.shape[2]), jnp.float32),
    )
    placed = tuple(
        (
            lax.dynamic_update_slice_in_dim(blank_part, drafted_part, own_start, 0)
            for blank_part, drafted_part in zip(blanks, drafted)
        )
    )
    return join_parts(cached, placed)


def path_rows(key_matrix, value_matrix, reached, depths, leaf_ids):
    tree_length = reached.shape[-1]
    leaf_hot = jax.nn.one_hot(leaf_ids, tree_length, dtype=jnp.float32)
    on_path = jnp.einsum("rt,rts->rs", leaf_hot, reached, precision=lax.Precision.HIGHEST)
    level_hot = (depths[:, None, :] == jnp.arange(ACC, dtype=jnp.int32)[None, :, None]).astype(
        jnp.float32
    )
    selector = (on_path[:, None, :] * level_hot).astype(jnp.bfloat16)
    stacked = jnp.stack([key_matrix, value_matrix], axis=1)
    return jnp.einsum(
        "ras,rbsc->rbac", selector, stacked, preferred_element_type=jnp.float32
    ).astype(jnp.bfloat16)


def place_rows(rows, page_slot, own_start, owner_page_count):
    slot_ids = own_start + jnp.arange(owner_page_count, dtype=jnp.int32)
    chooser = (page_slot[None, :] == slot_ids[:, None]).astype(jnp.bfloat16)
    return jnp.einsum("pr,rbac->pbac", chooser, rows, preferred_element_type=jnp.float32).astype(
        jnp.bfloat16
    )


def scale_sums(peaks, peak_all, totals, summed):
    factors = jnp.exp(peaks - peak_all)
    split_shape = summed.shape[:-1] + (QUERY_HEADS, -1)
    scaled = (summed.reshape(split_shape) * factors[..., None]).reshape(summed.shape)
    return (scaled, totals * factors)


def body(
    hidden,
    norm_gain,
    w_qkv,
    w_out,
    ffn_gain,
    w_gate,
    w_up,
    w_down,
    cache,
    page_table,
    cache_len,
    parents,
    accept_leaf,
    page_slot,
):
    block_rows, draft_part, model_width = hidden.shape
    channels = w_qkv.shape[1]
    query_columns = w_out.shape[0]
    key_value_columns = (channels - query_columns) // 2
    req_count = lax.axis_size("req")
    rep_count = lax.axis_size("rep")
    rep_index = lax.axis_index("rep")
    requests = cache_len.shape[0]
    owner_page_count = requests // rep_count
    tree_length = parents.shape[1]
    own_start = rep_index * owner_page_count
    projected_rows = project(hidden, norm_gain, w_qkv)
    reached = ancestors(parents)
    depths = jnp.sum(reached, axis=-1).astype(jnp.int32) - 1
    token_positions = cache_len[:, None] + depths
    page_list = page_table[:, 0, :]
    own_reach = lax.dynamic_slice_in_dim(reached, own_start, owner_page_count, 0)
    fanned = lax.all_gather(projected_rows, "rep", axis=0, tiled=True)
    arranged = fanned.reshape(requests, req_count, draft_part, channels)
    owned_pages = lax.all_to_all(arranged, "req", split_axis=1, concat_axis=2, tiled=True).reshape(
        requests, tree_length, channels
    )
    queries_all = apply_rotation(
        owned_pages[..., :query_columns].astype(jnp.float32), token_positions, QUERY_HEADS
    ).astype(jnp.bfloat16)
    keys_all = apply_rotation(
        owned_pages[..., query_columns : query_columns + key_value_columns].astype(jnp.float32),
        token_positions,
        KEY_VALUE_HEADS,
    ).astype(jnp.bfloat16)
    values_all = owned_pages[..., query_columns + key_value_columns :]
    local_key_rows = lax.dynamic_slice_in_dim(keys_all, own_start, owner_page_count, 0)
    local_value_rows = lax.dynamic_slice_in_dim(values_all, own_start, owner_page_count, 0)
    peaks, totals, summed = owner_partials(
        queries_all,
        local_key_rows,
        local_value_rows,
        own_reach,
        cache,
        page_list,
        cache_len,
        own_start,
    )
    returned = (
        lax.all_to_all(
            peaks.reshape(requests, 1, tree_length, QUERY_HEADS),
            "req",
            split_axis=2,
            concat_axis=1,
            tiled=True,
        ),
        lax.all_to_all(
            totals.reshape(requests, 1, tree_length, QUERY_HEADS),
            "req",
            split_axis=2,
            concat_axis=1,
            tiled=True,
        ),
        lax.all_to_all(
            summed.reshape(requests, 1, tree_length, query_columns),
            "req",
            split_axis=2,
            concat_axis=1,
            tiled=True,
        ),
    )
    back_peaks = returned[0].reshape(requests * req_count, draft_part, QUERY_HEADS)
    back_totals = returned[1].reshape(requests * req_count, draft_part, QUERY_HEADS)
    back_sums = returned[2].reshape(requests * req_count, draft_part, query_columns)
    peak_all = lax.pmax(back_peaks, "rep")
    scaled, scaled_totals = scale_sums(back_peaks, peak_all, back_totals, back_sums)
    shared = (
        lax.psum_scatter(scaled, "rep", scatter_dimension=0, tiled=True),
        lax.psum_scatter(scaled_totals, "rep", scatter_dimension=0, tiled=True),
    )
    attended = (
        (shared[0].reshape(block_rows, draft_part, QUERY_HEADS, -1) / shared[1][..., None])
        .reshape(block_rows, draft_part, query_columns)
        .astype(jnp.bfloat16)
    )
    all_rows = path_rows(keys_all, values_all, reached, depths, accept_leaf)
    mixed = jnp.dot(attended.reshape(-1, query_columns), w_out, preferred_element_type=jnp.float32)
    residual = (mixed + hidden.reshape(-1, model_width).astype(jnp.float32)).astype(jnp.bfloat16)
    residual_wide = residual.astype(jnp.float32)
    ffn_in = rms_scaled(residual_wide, ffn_gain).reshape(hidden.shape)
    collected_pages = lax.all_gather(ffn_in, "rep", axis=0, tiled=True)
    rows_in = collected_pages.reshape(-1, model_width)
    gate = jnp.dot(rows_in, w_gate, preferred_element_type=jnp.float32)
    up = jnp.dot(rows_in, w_up, preferred_element_type=jnp.float32)
    activated = (jax.nn.silu(gate) * up).astype(jnp.bfloat16)
    ffn_sum = lax.psum_scatter(
        jnp.dot(activated, w_down, preferred_element_type=jnp.float32).reshape(
            block_rows * lax.axis_size("rep"), draft_part, model_width
        ),
        "rep",
        scatter_dimension=0,
        tiled=True,
    )
    out = (ffn_sum + residual_wide.reshape(hidden.shape)).astype(jnp.bfloat16)
    new_pages = place_rows(all_rows, page_slot, own_start, owner_page_count)
    return (out, new_pages)


def solution(mesh):
    placed = (
        P("rep", "req", None),
        P(),
        P(),
        P(),
        P(),
        P(None, "rep"),
        P(None, "rep"),
        P("rep", None),
        P(("req", "rep"), None, None, None),
        P("req", "rep", None),
        P("req"),
        P("req", None),
        P("req"),
        P("req"),
    )
    return jax.shard_map(
        body,
        mesh=mesh,
        in_specs=placed,
        out_specs=(P("rep", "req", None), P(("req", "rep"), None, None, None)),
        check_vma=False,
    )
```

profile of v0, /device:TPU:1, one launch (start us, length us, event | category | flops | bytes accessed | tf_op | source)
XLA Modules:
  0.0 617.9 jit_solution(11852952766045524678)
XLA Ops:
  8.5 4.1 convolution_convert_fusion
  12.6 36.0 %all-gather.5.cloned.1.call-done = bf16[512,1920]{1,0:T(8,128)(2,1)} async-done(((bf16[128,1920]{1,0:T(8,128)(2,1)}), bf16[512,1920]{1,0:T(8,128)(2,1)}) %all-gather.5.cloned.1.call-update) | async-done | bytes 1966096 | tf_op jit(solution)/shard_map/all_gather | solution.py:212
  48.6 4.0 copy.113
  52.5 11.8 %all-to-all-start = ((bf16[8,64,1,1920]{3,0,2,1:T(8,128)(2,1)}), bf16[8,64,1,1920]{3,0,2,1:T(8,128)(2,1)}, u32[]{:S(2)}, u32[]{:S(2)}) async-start(bf16[8,64,1,1920]{3,0,2,1:T(8,128)(2,1)} %copy.113), calls=%async_computation | async-start | bytes 3932160 | tf_op jit(solution)/shard_map/all_to_all | solution.py:214
  71.9 40.4 %all-to-all-done = bf16[8,64,1,1920]{3,0,2,1:T(8,128)(2,1)} async-done(((bf16[8,64,1,1920]{3,0,2,1:T(8,128)(2,1)}), bf16[8,64,1,1920]{3,0,2,1:T(8,128)(2,1)}, u32[]{:S(2)}, u32[]{:S(2)}) %all-to-all-start) | async-done | bytes 1966112 | tf_op jit(solution)/shard_map/all_to_all | solution.py:214
  125.6 5.5 reshape.319
  131.1 6.6 %subtract_convert_fusion = (bf16[8,64,18,32]{3,2,1,0:T(8,128)(2,1)S(1)}, bf16[8,64,18,32]{3,2,1,0:T(8,128)(2,1)S(1)}) fusion(f32[8,64,18,64]{3,2,1,0:T(8,128)} %reshape.319, f32[8,64,32]{2,1,0:T(8,128)S(1)} %copy-done.3, f32[8,64,32]{2,1,0:T(8,128)S(1)} %copy-done.2), kind=kLoop, calls=%fused_computation.28 | loop fusion | flops 2359296 | bytes 3670016 | tf_op jit(solution)/shard_map/convert.3
  141.2 4.7 convert_element_type.116
  157.6 225.7 %while.15 = (s32[]{:T(128)}, f32[8,64,18]{1,0,2:T(8,128)}, f32[8,64,18]{1,0,2:T(8,128)}, f32[8,64,1152]{2,1,0:T(8,128)}, s32[8]{0:T(128)}, /*index=5*/bf16[8,64,...) while((s32[]{:T(128)}, f32[8,64,18]{1,0,2:T(8,128)}, ...), condition=%wide.region_5.6_spmd.clone, body=%wide.region_2.5_spmd.clone.sunk | while | flops 196853776 | bytes 19970600 | solution.py:128
  387.7 6.1 all-to-all-start.2
  400.1 5.3 mul.245
  405.5 3.8 mul.248
  409.3 5.3 mul.249
  415.7 10.6 %all-to-all-start.3 = ((f32[64,1,144]{2,1,0:T(1,128)}), f32[64,1,144]{2,1,0:T(1,128)S(1)}, u32[]{:S(2)}, u32[]{:S(2)}) async-start(f32[64,1,144]{2,1,0:T(1,128)} %reshape.357), calls=%async_computation.4 | async-start | bytes 131072 | tf_op jit(solution)/shard_map/all_to_all | solution.py:246
  426.3 4.2 bitcast_add_fusion
  436.0 7.9 %all-to-all-start.1 = ((f32[8,1,64,1152]{3,0,1,2:T(8,128)}), f32[8,1,64,1152]{3,0,1,2:T(8,128)}, u32[]{:S(2)}, u32[]{:S(2)}) async-start(f32[8,1,64,1152]{3,0,1,2:T(8,128)} %copy.132), calls=%async_computation.1 | async-start | bytes 4718592 | tf_op jit(solution)/shard_map/all_to_all | solution.py:253
  446.9 13.3 %pmax.7 = f32[512,1,18]{0,1,2:T(1,128)S(1)} all-reduce(f32[512,1,18]{0,1,2:T(1,128)S(1)} %reshape.309), channel_id=1, replica_groups=mesh['req'=64,'rep'=4] {'rep'}, use_global_device_ids=true, to_apply=%region_7.8 | all-reduce | flops 9216 | bytes 73728 | tf_op jit(solution)/shard_map/pmax | solution.py:264
  465.1 4.1 copy.158
  469.3 5.2 bitcast_reduce_fusion
  474.5 25.9 %all-to-all-done.1 = f32[8,1,64,1152]{3,0,1,2:T(8,128)} async-done(((f32[8,1,64,1152]{3,0,1,2:T(8,128)}), f32[8,1,64,1152]{3,0,1,2:T(8,128)}, u32[]{:S(2)}, u32[]{:S(2)}) %all-to-all-start.1) | async-done | bytes 2359328 | tf_op jit(solution)/shard_map/all_to_all | solution.py:253
  510.0 26.1 %reduce-scatter.6.cloned.1.call-done = f32[128,1,1152]{2,0,1:T(8,128)} async-done(((f32[512,1,1152]{2,0,1:T(8,128)}), f32[128,1,1152]{2,0,1:T(8,128)}) %reduce-scatter.6.cloned.1.call-update) | async-done | bytes 589840 | tf_op jit(solution)/shard_map/reduce_scatter | solution.py:267
  539.1 24.7 %all-gather.7.cloned.1.call-done = bf16[512,1152]{1,0:T(8,128)(2,1)} async-done(((bf16[128,1152]{1,0:T(8,128)(2,1)}), bf16[512,1152]{1,0:T(8,128)(2,1)}) %all-gather.7.cloned.1.call-update) | async-done | bytes 1179664 | tf_op jit(solution)/shard_map/all_gather | solution.py:280
  567.0 5.0 convolution_bitcast_fusion
  577.9 31.4 %reduce-scatter.8.cloned.1.call-done = f32[128,1,1152]{2,0,1:T(8,128)} async-done(((f32[512,1,1152]{2,0,1:T(8,128)}), f32[128,1,1152]{2,0,1:T(8,128)}) %reduce-scatter.8.cloned.1.call-update) | async-done | bytes 589840 | tf_op jit(solution)/shard_map/reduce_scatter | solution.py:285
  (332 shorter events, 310.8 us)
Async XLA Ops:
  7.2 529.0 %copy-start = (bf16[1152,1152]{1,0:T(8,128)(2,1)S(1)}, bf16[1152,1152]{1,0:T(8,128)(2,1)}, u32[]{:S(2)}) copy-start(bf16[1152,1152]{1,0:T(8,128)(2,1)} %param.19) | copy-start | bytes 7962628
  7.2 41.4 %all-gather.5.cloned.1.call-start = ((), (), s32[]{:S(2)}) async-start(), calls=%async_computation.9 | async-start | bytes 2457600 | tf_op jit(solution)/shard_map/all_gather | solution.py:212
  52.5 11.8 %copy-start.16 = (s32[8,64]{1,0:T(8,128)S(1)}, s32[8,64]{1,0:T(8,128)}, u32[]{:S(2)}) copy-start(s32[8,64]{1,0:T(8,128)} %param.27) | copy-start | bytes 6148
  52.5 59.8 %all-to-all-start = ((bf16[8,64,1,1920]{3,0,2,1:T(8,128)(2,1)}), bf16[8,64,1,1920]{3,0,2,1:T(8,128)(2,1)}, u32[]{:S(2)}, u32[]{:S(2)}) async-start(bf16[8,64,1,1920]{3,0,2,1:T(8,128)(2,1)} %copy.113), calls=%async_computation | async-start | bytes 3932160 | tf_op jit(solution)/shard_map/all_to_all | solution.py:214
  157.6 10.0 %copy-start.13 = (s32[8,5]{1,0:T(8,128)}, s32[8,5]{1,0:T(8,128)S(1)}, u32[]{:S(2)}) copy-start(s32[8,5]{1,0:T(8,128)S(1)} %get-tuple-element.250) | copy-start | bytes 484 | tf_op jit(solution)/shard_map/while
  185.8 10.0 %copy-start.13 = (s32[8,5]{1,0:T(8,128)}, s32[8,5]{1,0:T(8,128)S(1)}, u32[]{:S(2)}) copy-start(s32[8,5]{1,0:T(8,128)S(1)} %get-tuple-element.250) | copy-start | bytes 484 | tf_op jit(solution)/shard_map/while
  214.0 10.0 %copy-start.13 = (s32[8,5]{1,0:T(8,128)}, s32[8,5]{1,0:T(8,128)S(1)}, u32[]{:S(2)}) copy-start(s32[8,5]{1,0:T(8,128)S(1)} %get-tuple-element.250) | copy-start | bytes 484 | tf_op jit(solution)/shard_map/while
  242.2 10.0 %copy-start.13 = (s32[8,5]{1,0:T(8,128)}, s32[8,5]{1,0:T(8,128)S(1)}, u32[]{:S(2)}) copy-start(s32[8,5]{1,0:T(8,128)S(1)} %get-tuple-element.250) | copy-start | bytes 484 | tf_op jit(solution)/shard_map/while
  270.4 10.0 %copy-start.13 = (s32[8,5]{1,0:T(8,128)}, s32[8,5]{1,0:T(8,128)S(1)}, u32[]{:S(2)}) copy-start(s32[8,5]{1,0:T(8,128)S(1)} %get-tuple-element.250) | copy-start | bytes 484 | tf_op jit(solution)/shard_map/while
  298.6 10.0 %copy-start.13 = (s32[8,5]{1,0:T(8,128)}, s32[8,5]{1,0:T(8,128)S(1)}, u32[]{:S(2)}) copy-start(s32[8,5]{1,0:T(8,128)S(1)} %get-tuple-element.250) | copy-start | bytes 484 | tf_op jit(solution)/shard_map/while
  326.8 10.0 %copy-start.13 = (s32[8,5]{1,0:T(8,128)}, s32[8,5]{1,0:T(8,128)S(1)}, u32[]{:S(2)}) copy-start(s32[8,5]{1,0:T(8,128)S(1)} %get-tuple-element.250) | copy-start | bytes 484 | tf_op jit(solution)/shard_map/while
  348.6 6.5 %copy-start.14 = (s32[8,5]{1,0:T(8,128)S(1)}, s32[8,5]{1,0:T(8,128)}, u32[]{:S(2)}) copy-start(s32[8,5]{1,0:T(8,128)} %copy-done.13) | copy-start | bytes 484 | tf_op jit(solution)/shard_map/while
  355.0 10.0 %copy-start.13 = (s32[8,5]{1,0:T(8,128)}, s32[8,5]{1,0:T(8,128)S(1)}, u32[]{:S(2)}) copy-start(s32[8,5]{1,0:T(8,128)S(1)} %get-tuple-element.250) | copy-start | bytes 484 | tf_op jit(solution)/shard_map/while
  383.3 12.1 %copy-start.4 = (f32[2,1,64,1152]{3,2,0,1:T(8,128)S(1)}, f32[2,1,64,1152]{3,2,0,1:T(8,128)}, u32[]{:S(2)}) copy-start(f32[2,1,64,1152]{3,2,0,1:T(8,128)} %copy.130) | copy-start | bytes 1769476
  387.7 8.5 %copy-start.10 = (f32[8,64,18]{1,0,2:T(8,128)S(1)}, f32[8,64,18]{1,0,2:T(8,128)}, u32[]{:S(2)}) copy-start(f32[8,64,18]{1,0,2:T(8,128)} %get-tuple-element.133) | copy-start | bytes 110596
  387.7 28.0 %all-to-all-start.2 = ((f32[64,1,144]{2,1,0:T(1,128)}), f32[64,1,144]{2,1,0:T(1,128)S(1)}, u32[]{:S(2)}, u32[]{:S(2)}) async-start(f32[64,1,144]{2,1,0:T(1,128)} %reshape.355), calls=%async_computation.2 | async-start | bytes 131072 | tf_op jit(solution)/shard_map/all_to_all | solution.py:239
  415.7 20.3 %all-to-all-start.3 = ((f32[64,1,144]{2,1,0:T(1,128)}), f32[64,1,144]{2,1,0:T(1,128)S(1)}, u32[]{:S(2)}, u32[]{:S(2)}) async-start(f32[64,1,144]{2,1,0:T(1,128)} %reshape.357), calls=%async_computation.4 | async-start | bytes 131072 | tf_op jit(solution)/shard_map/all_to_all | solution.py:246
  436.0 64.5 %all-to-all-start.1 = ((f32[8,1,64,1152]{3,0,1,2:T(8,128)}), f32[8,1,64,1152]{3,0,1,2:T(8,128)}, u32[]{:S(2)}, u32[]{:S(2)}) async-start(f32[8,1,64,1152]{3,0,1,2:T(8,128)} %copy.132), calls=%async_computation.1 | async-start | bytes 4718592 | tf_op jit(solution)/shard_map/all_to_all | solution.py:253
  443.9 60.7 %reduce-scatter.10.cloned.1.call-start = ((), (), s32[]{:S(2)}) async-start(), calls=%async_computation.11 | async-start | bytes 327680
  474.5 61.7 %reduce-scatter.6.cloned.1.call-start = ((), (), s32[]{:S(2)}) async-start(), calls=%async_computation.7 | async-start | bytes 2949120 | tf_op jit(solution)/shard_map/reduce_scatter | solution.py:267
  504.5 31.7 %copy-start.7 = (bf16[128,1,1152]{2,0,1:T(8,128)(2,1)S(1)}, bf16[128,1,1152]{2,0,1:T(8,128)(2,1)}, u32[]{:S(2)}) copy-start(bf16[128,1,1152]{2,0,1:T(8,128)(2,1)} %param.16) | copy-start | bytes 884740
  504.5 59.3 %all-gather.7.cloned.1.call-start = ((), (), s32[]{:S(2)}) async-start(), calls=%async_computation.10 | async-start | bytes 1474560 | tf_op jit(solution)/shard_map/all_gather | solution.py:280
  510.0 28.1 %copy-start.11 = (f32[1152]{0:T(1024)S(1)}, f32[1152]{0:T(1024)}, u32[]{:S(2)}) copy-start(f32[1152]{0:T(1024)} %param.20) | copy-start | bytes 13828
  539.0 70.2 %reduce-scatter.8.cloned.1.call-start = ((), (), s32[]{:S(2)}) async-start(), calls=%async_computation.8 | async-start | bytes 2949120 | tf_op jit(solution)/shard_map/reduce_scatter | solution.py:285
  (18 other events, 83.5 us)
Sparse Core Ops, SparseCore 0:
  12.7 35.8 all-gather.4
  474.6 23.4 reduce-scatter.9
  504.6 31.5 reduce-scatter.5
  539.1 24.6 all-gather.6
  572.2 37.0 reduce-scatter.7
where the time goes:
time: 625 us; the launch traced here: 618 us
  local copies, waits for them, and re-layouts  229 us (37%)
  waiting for transfers between devices  187 us (30%)
  matrix products  70.4 us (11%)
  other arithmetic  66.2 us (11%)
  starting transfers between devices  36.6 us (6%)
  between operations  14.5 us (2%)
  blocking collectives  13.3 us (2%)
    all_to_all x1, waiting for transfers between devices, body(): lax.all_to_all(arranged, 'req', split_axis=1, concat_axis=2, tiled=True)  40.4 us
    all_gather x1, waiting for transfers between devices, body(): fanned = lax.all_gather(projected_rows, 'rep', axis=0, tiled=True)  36 us
    dynamic_update_slice x32, local copies, waits for them, and re-layouts, owner_partials(): cached = lax.map(per_request, (queries_all, page_list, cache_len))  32.5 us
    reduce_scatter x1, waiting for transfers between devices, body(): lax.psum_scatter(jnp.dot(activated, w_down, preferred_element_type=jnp.fl...  31.4 us
    slice x16, local copies, waits for them, and re-layouts, per_request(): collected_pages[:, 1]  30.2 us
    gather x8, local copies, waits for them, and re-layouts, per_request(): collected_pages = cache[page_ids]  28.7 us
    dot_general x9, matrix products, attend_part(): jnp.einsum('tgrd,sgd->gtrs', grouped_queries, key_matrix, preferred_eleme...  26.9 us
    reduce_scatter x1, waiting for transfers between devices, body(): lax.psum_scatter(scaled, 'rep', scatter_dimension=0, tiled=True)  26.1 us
  transfers between devices with their start and end apart: 9, of which 7 were waited for; matrix products, arithmetic and copies ran while one was open for 11% of the time, Pallas kernels for 0%

commit v1 on v0

v1 whole, which is shorter than its diff:
```python
import functools

import jax
import jax.numpy as jnp
from jax import lax
from jax.experimental import pallas as pl
from jax.experimental.pallas import tpu as pltpu
from jax.sharding import PartitionSpec as P

QUERY_HEADS = 18
KEY_VALUE_HEADS = 6
ACC = 8


SCALE = 0.125
EPSILON = 1e-05
THETA = 10000.0


def apply_rotation(values, token_positions, head_count):
    head_columns = values.shape[-1] // head_count
    half_width = head_columns // 2
    shaped = values.reshape(values.shape[:-1] + (head_count, head_columns))
    frequency = THETA ** (-jnp.arange(half_width, dtype=jnp.float32) / half_width)
    angles = token_positions.astype(jnp.float32)[..., None] * frequency
    cosine = jnp.cos(angles)[..., None, :]
    sines = jnp.sin(angles)[..., None, :]
    front_half = shaped[..., :half_width]
    back_half = shaped[..., half_width:]
    turned = jnp.concatenate(
        [front_half * cosine - back_half * sines, back_half * cosine + front_half * sines], axis=-1
    )
    return turned.reshape(values.shape)


def ancestors(parents):
    tree_length = parents.shape[-1]
    identity = jnp.eye(tree_length, dtype=jnp.float32)
    linked = jax.nn.one_hot(parents, tree_length, dtype=jnp.float32)
    reached = jnp.minimum(identity + linked, 1.0)
    for doubling in range(tree_length.bit_length()):
        reached = jnp.minimum(
            jnp.einsum("rts,rsu->rtu", reached, reached, precision=lax.Precision.HIGHEST), 1.0
        )
    return reached


def rms_scaled(values_in, gain):
    scaling = lax.rsqrt(jnp.mean(values_in * values_in, axis=-1, keepdims=True) + EPSILON)
    return (values_in * scaling * gain).astype(jnp.bfloat16)


def path_rows(key_matrix, value_matrix, reached, depths, leaf_ids):
    tree_length = reached.shape[-1]
    leaf_hot = jax.nn.one_hot(leaf_ids, tree_length, dtype=jnp.float32)
    on_path = jnp.einsum("rt,rts->rs", leaf_hot, reached, precision=lax.Precision.HIGHEST)
    level_hot = (depths[:, None, :] == jnp.arange(ACC, dtype=jnp.int32)[None, :, None]).astype(
        jnp.float32
    )
    selector = (on_path[:, None, :] * level_hot).astype(jnp.bfloat16)
    stacked = jnp.stack([key_matrix, value_matrix], axis=1)
    return jnp.einsum(
        "ras,rbsc->rbac", selector, stacked, preferred_element_type=jnp.float32
    ).astype(jnp.bfloat16)


def place_rows(rows, page_slot, own_start, owner_page_count):
    slot_ids = own_start + jnp.arange(owner_page_count, dtype=jnp.int32)
    chooser = (page_slot[None, :] == slot_ids[:, None]).astype(jnp.bfloat16)
    return jnp.einsum("pr,rbac->pbac", chooser, rows, preferred_element_type=jnp.float32).astype(
        jnp.bfloat16
    )


def paged_kernel(slots, chunks, page_ref, limit_ref, *refs):
    q_ref = refs[0]
    page_refs = refs[1 : 1 + slots]
    dk_ref, dv_ref, dmask_ref = refs[1 + slots : 4 + slots]
    m_ref, l_ref, acc_ref = refs[4 + slots :]
    request = pl.program_id(0)
    rows = q_ref.shape[2]
    page_length = page_refs[0].shape[2]
    lane_ids = lax.broadcasted_iota(jnp.int32, (rows, page_length), 1)
    draft_open = dmask_ref[0] > 0.5
    nt = (((1,), (1,)), ((), ()))
    for c in range(chunks):
        lanes = pl.ds(c * 128, 128)
        qc = q_ref[0, c]
        parts = []
        for s in range(slots):
            kc = page_refs[s][0, 0, :, lanes]
            sc = lax.dot_general(qc, kc, nt, preferred_element_type=jnp.float32) * SCALE
            sc = jnp.where(lane_ids < limit_ref[request, s], sc, -jnp.inf)
            parts.append(sc)
        kd = dk_ref[0, :, lanes]
        sd = lax.dot_general(qc, kd, nt, preferred_element_type=jnp.float32) * SCALE
        sd = jnp.where(draft_open, sd, -jnp.inf)
        peak = jnp.max(sd, axis=-1, keepdims=True)
        for sc in parts:
            peak = jnp.maximum(peak, jnp.max(sc, axis=-1, keepdims=True))
        wd = jnp.exp(sd - peak)
        total = jnp.sum(wd, axis=-1, keepdims=True)
        acc = jnp.dot(
            wd.astype(jnp.bfloat16), dv_ref[0, :, lanes], preferred_element_type=jnp.float32
        )
        for s in range(slots):
            ws = jnp.exp(parts[s] - peak)
            total = total + jnp.sum(ws, axis=-1, keepdims=True)
            acc = acc + jnp.dot(
                ws.astype(jnp.bfloat16),
                page_refs[s][0, 1, :, lanes],
                preferred_element_type=jnp.float32,
            )
        m_ref[0, c] = peak
        l_ref[0, c] = total
        acc_ref[0, c] = acc


def paged_partials(q2, cache, page_list, limits, draft_keys, draft_values, draft_mask):
    requests, chunks, rows, lanes = q2.shape
    slots = page_list.shape[1]
    page_length = cache.shape[2]
    width = cache.shape[3]
    tree_length = draft_keys.shape[1]

    def page_map(s):
        return lambda k, pages, limit: (pages[k, s], 0, 0, 0)

    in_specs = [pl.BlockSpec((1, chunks, rows, lanes), lambda k, pages, limit: (k, 0, 0, 0))]
    in_specs += [pl.BlockSpec((1, 2, page_length, width), page_map(s)) for s in range(slots)]
    in_specs += [
        pl.BlockSpec((1, tree_length, width), lambda k, pages, limit: (k, 0, 0)),
        pl.BlockSpec((1, tree_length, width), lambda k, pages, limit: (k, 0, 0)),
        pl.BlockSpec((1, rows, tree_length), lambda k, pages, limit: (k, 0, 0)),
    ]
    out_specs = [
        pl.BlockSpec((1, chunks, rows, 1), lambda k, pages, limit: (k, 0, 0, 0)),
        pl.BlockSpec((1, chunks, rows, 1), lambda k, pages, limit: (k, 0, 0, 0)),
        pl.BlockSpec((1, chunks, rows, lanes), lambda k, pages, limit: (k, 0, 0, 0)),
    ]
    out_shape = [
        jax.ShapeDtypeStruct((requests, chunks, rows, 1), jnp.float32),
        jax.ShapeDtypeStruct((requests, chunks, rows, 1), jnp.float32),
        jax.ShapeDtypeStruct((requests, chunks, rows, lanes), jnp.float32),
    ]
    keys_seen = slots * page_length + tree_length
    cost = pl.CostEstimate(
        flops=requests * chunks * rows * lanes * keys_seen * 4,
        bytes_accessed=requests * (slots * 2 * page_length * width * 2 + chunks * rows * lanes * 6),
        transcendentals=requests * chunks * rows * keys_seen,
    )
    grid_spec = pltpu.PrefetchScalarGridSpec(
        num_scalar_prefetch=2,
        grid=(requests,),
        in_specs=in_specs,
        out_specs=out_specs,
    )
    return pl.pallas_call(
        functools.partial(paged_kernel, slots, chunks),
        grid_spec=grid_spec,
        out_shape=out_shape,
        cost_estimate=cost,
        compiler_params=pltpu.CompilerParams(dimension_semantics=("arbitrary",)),
        name="paged_partials",
    )(page_list, limits, q2, *([cache] * slots), draft_keys, draft_values, draft_mask)


def pair_queries(queries, requests, tree_length):
    head_columns = queries.shape[-1] // QUERY_HEADS
    group = QUERY_HEADS // KEY_VALUE_HEADS
    chunks = KEY_VALUE_HEADS // 2
    shaped = queries.reshape(requests, tree_length, chunks, 2, group, head_columns)
    shaped = shaped.transpose(0, 2, 3, 1, 4, 5).reshape(
        requests, chunks, 2, tree_length * group, head_columns
    )
    zeros = jnp.zeros_like(shaped[:, :, 0])
    top = jnp.concatenate([shaped[:, :, 0], zeros], axis=-1)
    bottom = jnp.concatenate([zeros, shaped[:, :, 1]], axis=-1)
    return jnp.concatenate([top, bottom], axis=2)


def unpair_rows(values, requests, tree_length):
    group = QUERY_HEADS // KEY_VALUE_HEADS
    chunks = KEY_VALUE_HEADS // 2
    shaped = values.reshape(requests, chunks, 2, tree_length, group)
    return shaped.transpose(0, 3, 1, 2, 4).reshape(requests, tree_length, QUERY_HEADS)


def unpair_sums(acc, requests, tree_length):
    group = QUERY_HEADS // KEY_VALUE_HEADS
    chunks = KEY_VALUE_HEADS // 2
    head_columns = acc.shape[-1] // 2
    shaped = acc.reshape(requests, chunks, 2, tree_length, group, 2, head_columns)
    diagonal = jnp.stack([shaped[:, :, 0, :, :, 0], shaped[:, :, 1, :, :, 1]], axis=2)
    return diagonal.transpose(0, 3, 1, 2, 4, 5).reshape(
        requests, tree_length, QUERY_HEADS * head_columns
    )


def body(
    hidden,
    norm_gain,
    w_qkv,
    w_out,
    ffn_gain,
    w_gate,
    w_up,
    w_down,
    cache,
    page_table,
    cache_len,
    parents,
    accept_leaf,
    page_slot,
):
    block_rows, draft_part, model_width = hidden.shape
    channels = w_qkv.shape[1]
    query_columns = w_out.shape[0]
    key_value_columns = (channels - query_columns) // 2
    req_count = lax.axis_size("req")
    rep_count = lax.axis_size("rep")
    rep_index = lax.axis_index("rep")
    requests = cache_len.shape[0]
    owner_page_count = requests // rep_count
    tree_length = parents.shape[1]
    own_start = rep_index * owner_page_count
    page_length = cache.shape[2]
    slots_count = page_table.shape[2]

    local_rows = hidden.reshape(owner_page_count, req_count, model_width)
    own_hidden = lax.all_to_all(local_rows, "req", split_axis=1, concat_axis=1, tiled=True)
    all_hidden = lax.all_gather(own_hidden, "rep", axis=0, tiled=True)

    normed = rms_scaled(all_hidden.astype(jnp.float32), norm_gain)
    projected = jnp.dot(
        normed.reshape(-1, model_width), w_qkv, preferred_element_type=jnp.float32
    ).astype(jnp.bfloat16).reshape(requests, tree_length, channels)

    reached = ancestors(parents)
    depths = jnp.sum(reached, axis=-1).astype(jnp.int32) - 1
    token_positions = cache_len[:, None] + depths
    queries = apply_rotation(
        projected[..., :query_columns].astype(jnp.float32), token_positions, QUERY_HEADS
    ).astype(jnp.bfloat16)
    keys_all = apply_rotation(
        projected[..., query_columns : query_columns + key_value_columns].astype(jnp.float32),
        token_positions,
        KEY_VALUE_HEADS,
    ).astype(jnp.bfloat16)
    values_all = projected[..., query_columns + key_value_columns :]

    group = QUERY_HEADS // KEY_VALUE_HEADS
    q2 = pair_queries(queries, requests, tree_length)
    page_list = page_table[:, 0, :]
    starts = (
        jnp.arange(slots_count, dtype=jnp.int32)[None, :] * rep_count + rep_index
    ) * page_length
    limits = cache_len[:, None] - starts
    mine = (jnp.arange(requests, dtype=jnp.int32) // owner_page_count) == rep_index
    open_rows = jnp.where(mine[:, None, None], reached, 0.0)
    open_rows = jnp.repeat(open_rows, group, axis=1)
    draft_mask = jnp.concatenate([open_rows, open_rows], axis=1)
    peaks, totals, sums = paged_partials(
        q2, cache, page_list, limits, keys_all, values_all, draft_mask
    )
    peaks = unpair_rows(peaks, requests, tree_length)
    totals = unpair_rows(totals, requests, tree_length)
    sums = unpair_sums(sums, requests, tree_length)

    peak_all = lax.pmax(peaks, "rep")
    factors = jnp.exp(peaks - peak_all)
    scaled = (sums.reshape(requests, tree_length, QUERY_HEADS, -1) * factors[..., None]).reshape(
        requests, tree_length, query_columns
    )
    joined = jnp.concatenate([scaled, totals * factors], axis=-1)
    shared = lax.psum_scatter(joined, "rep", scatter_dimension=0, tiled=True)
    attended = (
        (
            shared[..., :query_columns].reshape(owner_page_count, tree_length, QUERY_HEADS, -1)
            / shared[..., query_columns:][..., None]
        )
        .reshape(-1, query_columns)
        .astype(jnp.bfloat16)
    )

    mixed = jnp.dot(attended, w_out, preferred_element_type=jnp.float32)
    residual = (mixed + own_hidden.reshape(-1, model_width).astype(jnp.float32)).astype(
        jnp.bfloat16
    )
    residual_wide = residual.astype(jnp.float32)
    ffn_in = rms_scaled(residual_wide, ffn_gain).reshape(owner_page_count, tree_length, model_width)
    rows_in = lax.all_gather(ffn_in, "rep", axis=0, tiled=True).reshape(-1, model_width)
    gate = jnp.dot(rows_in, w_gate, preferred_element_type=jnp.float32)
    up = jnp.dot(rows_in, w_up, preferred_element_type=jnp.float32)
    activated = (jax.nn.silu(gate) * up).astype(jnp.bfloat16)
    ffn_sum = lax.psum_scatter(
        jnp.dot(activated, w_down, preferred_element_type=jnp.float32).reshape(
            requests, tree_length, model_width
        ),
        "rep",
        scatter_dimension=0,
        tiled=True,
    )
    out_own = (ffn_sum + residual_wide.reshape(owner_page_count, tree_length, model_width)).astype(
        jnp.bfloat16
    )
    out = lax.all_to_all(out_own, "req", split_axis=1, concat_axis=1, tiled=True)
    out = out.reshape(block_rows, draft_part, model_width)

    all_rows = path_rows(keys_all, values_all, reached, depths, accept_leaf)
    new_pages = place_rows(all_rows, page_slot, own_start, owner_page_count)
    return (out, new_pages)


def solution(mesh):
    placed = (
        P("rep", "req", None),
        P(),
        P(),
        P(),
        P(),
        P(None, "rep"),
        P(None, "rep"),
        P("rep", None),
        P(("req", "rep"), None, None, None),
        P("req", "rep", None),
        P("req"),
        P("req", None),
        P("req"),
        P("req"),
    )
    return jax.shard_map(
        body,
        mesh=mesh,
        in_specs=placed,
        out_specs=(P("rep", "req", None), P(("req", "rep"), None, None, None)),
        check_vma=False,
    )
```

time: 625 us -> 363 us (0.58)
  local copies, waits for them, and re-layouts: 229 us -> 90 us
  waiting for transfers between devices: 187 us -> 135 us
  matrix products: 70.4 us -> 21.2 us
  other arithmetic: 66.2 us -> 36.9 us
  Pallas kernels: 0 us -> 22.2 us
  starting transfers between devices: 36.6 us -> 24.8 us
    all_to_all x4 -> x2, waiting for transfers between devices: 68.9 us -> 17.2 us  [the longest x1 8.73 us: body(): lax.all_to_all(local_rows, 'req', split_axis=1, concat_axis=1, tiled=True)]
    dot_general x20 -> x2, matrix products: 57.5 us -> 7.07 us  [the longest x1 5.09 us: body(): jnp.dot(normed.reshape(-1, model_width), w_qkv, preferred_element_type=jn...]
    dynamic_update_slice x34 -> x0, local copies, waits for them, and re-layouts: 34.2 us -> none  [the longest x32 32.5 us: owner_partials(): cached = lax.map(per_request, (queries_all, page_list, cache_len))]
    slice x24 -> x5, local copies, waits for them, and re-layouts: 42.3 us -> 11.5 us  [the longest x1 8.66 us: unpair_sums(): shaped[:, :, 0, :, :, 0]]
    gather x8 -> x0, local copies, waits for them, and re-layouts: 28.7 us -> none  [per_request(): collected_pages = cache[page_ids]]
    pallas_call x0 -> x1, Pallas kernels: none -> 22.2 us  [paged_partials(): pl.pallas_call(functools.partial(paged_kernel, slots, chunks), grid_spec=...]
    squeeze x16 -> x1, local copies, waits for them, and re-layouts: 22 us -> 0.56 us  [pair_queries(): bottom = jnp.concatenate([zeros, shaped[:, :, 1]], axis=-1)]
    all_gather x2, waiting for transfers between devices: 60.7 us -> 39.4 us  [the longest x1 24.5 us: body(): lax.all_gather(ffn_in, 'rep', axis=0, tiled=True).reshape(-1, model_width)]
  transfers between devices with their start and end apart: 9 -> 6, of which waited for: 7 -> 6; matrix products, arithmetic and copies ran while one was open for 11% -> 4% of each run, Pallas kernels for 0% -> 0%
where the time goes in v1:
time: 363 us; the launch traced here: 359 us
  waiting for transfers between devices  135 us (37%)
  local copies, waits for them, and re-layouts  90 us (25%)
  other arithmetic  36.9 us (10%)
  starting transfers between devices  24.8 us (7%)
  Pallas kernels  22.2 us (6%)
  matrix products  21.2 us (6%)
  blocking collectives  14.5 us (4%)
  between operations  14.4 us (4%)
    reduce_scatter x1, waiting for transfers between devices, body(): shared = lax.psum_scatter(joined, 'rep', scatter_dimension=0, tiled=True)  41.4 us
    reduce_scatter x1, waiting for transfers between devices, body(): lax.psum_scatter(jnp.dot(activated, w_down, preferred_element_type=jnp.fl...  36.5 us
    all_gather x1, waiting for transfers between devices, body(): lax.all_gather(ffn_in, 'rep', axis=0, tiled=True).reshape(-1, model_width)  24.5 us
    pallas_call x1, Pallas kernels, paged_partials(): pl.pallas_call(functools.partial(paged_kernel, slots, chunks), grid_spec=...  22.2 us
    pallas_call x2, local copies, waits for them, and re-layouts, paged_partials(): pl.pallas_call(functools.partial(paged_kernel, slots, chunks), grid_spec=...  18.5 us
    all_gather x1, waiting for transfers between devices, body(): all_hidden = lax.all_gather(own_hidden, 'rep', axis=0, tiled=True)  14.9 us
    pmax x1, blocking collectives, body(): peak_all = lax.pmax(peaks, 'rep')  14.5 us
    all_to_all x1, starting transfers between devices, body(): lax.all_to_all(local_rows, 'req', split_axis=1, concat_axis=1, tiled=True)  13.1 us
  transfers between devices with their start and end apart: 6, of which 6 were waited for; matrix products, arithmetic and copies ran while one was open for 4% of the time, Pallas kernels for 0%

profile of v1, /device:TPU:1, one launch (start us, length us, event | category | flops | bytes accessed | tf_op | source)
XLA Modules:
  0.0 358.6 jit_solution(13897264977571488269)
XLA Ops:
  9.3 13.1 %all-to-all-start = ((bf16[2,64,1152]{2,0,1:T(2,128)(2,1)}), bf16[2,64,1152]{2,0,1:T(2,128)(2,1)S(1)}, u32[]{:S(2)}, u32[]{:S(2)}) async-start(bf16[2,64,1152]{2,0,1:T(2,128)(2,1)} %copy.131), calls=%async_computation | async-start | bytes 589824 | tf_op jit(solution)/shard_map/all_to_all | solution.py:231
  26.4 8.7 %all-to-all-done = bf16[2,64,1152]{2,0,1:T(2,128)(2,1)S(1)} async-done(((bf16[2,64,1152]{2,0,1:T(2,128)(2,1)}), bf16[2,64,1152]{2,0,1:T(2,128)(2,1)S(1)}, u32[]{:S(2)}, u32[]{:S(2)}) %all-to-all-start) | async-done | bytes 294944 | tf_op jit(solution)/shard_map/all_to_all | solution.py:231
  42.6 14.9 %all-gather.3.cloned.1.call-done = bf16[8,64,1152]{2,1,0:T(8,128)(2,1)} async-done(((bf16[2,64,1152]{2,1,0:T(8,128)(2,1)}), bf16[8,64,1152]{2,1,0:T(8,128)(2,1)}) %all-gather.3.cloned.1.call-update) | async-done | bytes 1179664 | tf_op jit(solution)/shard_map/all_gather | solution.py:232
  60.7 5.1 %convolution_convert_fusion = bf16[512,1920]{1,0:T(8,128)(2,1)S(1)} fusion(bf16[512,1152]{1,0:T(8,128)(2,1)S(1)} %bitcast.101, bf16[1152,1920]{1,0:T(8,128)(2,1)} %param.16), kind=kOutput, calls=%fused_computation.10 | convolution fusion | flops 2265907200 | bytes 7569408 | tf_op jit(solution)/shard_map/dot_general | solution.py:235
  70.3 3.1 multiply_subtract_fusion
  77.6 5.5 %reshape.203 = f32[8,64,18,64]{3,2,1,0:T(8,128)} reshape(f32[8,64,1152]{2,1,0:T(8,128)} %slice_convert_fusion) | data formatting | bytes 4718592 | tf_op jit(solution)/shard_map/reshape | solution.py:23
  83.1 6.8 %subtract_convert_fusion = (bf16[8,64,18,32]{3,2,1,0:T(8,128)(2,1)S(1)}, bf16[8,64,18,32]{3,2,1,0:T(8,128)(2,1)S(1)}) fusion(f32[8,64,18,64]{3,2,1,0:T(8,128)} %reshape.203, f32[8,64,32]{2,1,0:T(8,128)S(1)} %copy-done.3, f32[8,64,32]{2,1,0:T(8,128)S(1)} %copy-done.2), kind=kLoop, calls=%fused_computation.2 | loop fusion | flops 2359296 | bytes 3670016 | tf_op jit(solution)/shard_map/convert.3
  96.8 22.2 %paged_partials.1 = (f32[8,3,384,1]{3,2,1,0:T(8,128)}, f32[8,3,384,1]{3,2,1,0:T(8,128)}, f32[8,3,384,128]{3,2,1,0:T(8,128)}) custom-call(s32[8,5]{1,0:T(8,128)} %bitcast.105, s32[8,5]{1,0:T(8,128)} %broadcast_subtract_fusion.limit_ref, bf16[8,3,384,128]{3,2,1,0:T(8,128)(2,1)} %fusion.7.refs_0_, bf16[16,2,128,384]{3,2,1,0:T(8,128)(2,1)} %refs_5_.1, ...), custom_call_target="tpu_custom_call" | custom-call | flops 3321888768 | bytes 14942208 | tf_op jit(solution)/shard_map/paged_partials/pallas_call | solution.py:158
  119.0 9.3 %copy.144 = f32[8,3,384,1]{0,2,1,3:T(8,128)} copy(f32[8,3,384,1]{3,2,1,0:T(8,128)} %get-tuple-element.6) | data formatting | bytes 73728 | tf_op jit(solution)/shard_map/paged_partials/pallas_call | solution.py:158
  129.8 14.5 %pmax.7 = f32[8,64,18]{1,0,2:T(8,128)} all-reduce(f32[8,64,18]{1,0,2:T(8,128)S(1)} %bitcast.102), channel_id=1, replica_groups=mesh['req'=64,'rep'=4] {'rep'}, use_global_device_ids=true, to_apply=%region_2.3 | all-reduce | flops 9216 | bytes 73728 | tf_op jit(solution)/shard_map/pmax | solution.py:270
  144.4 9.2 %copy.147 = f32[8,3,384,1]{0,2,1,3:T(8,128)} copy(f32[8,3,384,1]{3,2,1,0:T(8,128)} %get-tuple-element.7) | data formatting | bytes 73728 | tf_op jit(solution)/shard_map/paged_partials/pallas_call | solution.py:158
  157.1 10.5 %reshape.191 = f32[8,3,2,64,3,2,64]{6,5,4,3,2,1,0:T(2,128)} reshape(f32[8,3,384,128]{3,2,1,0:T(8,128)} %get-tuple-element.5) | data formatting | bytes 9437184 | tf_op jit(solution)/shard_map/reshape | solution.py:193
  167.5 8.7 %fusion.42 = (f32[8,3,1,64,3,1,64]{6,5,4,3,2,1,0:T(1,128)S(1)}, f32[8,3,1,64,3,1,64]{6,5,4,3,2,1,0:T(1,128)S(1)}) fusion(f32[8,3,2,64,3,2,64]{6,5,4,3,2,1,0:T(2,128)} %reshape.191), kind=kLoop, calls=%fused_computation.100 | loop fusion | bytes 4718592 | tf_op jit(solution)/shard_map/slice | solution.py:194
  177.3 4.3 %maximum_bitcast_fusion = f32[8,64,3,2,3,64]{5,4,3,2,1,0:T(4,128)} fusion(f32[8,3,1,64,3,64]{5,4,2,1,3,0:T(4,128)S(1)} %bitcast.88, f32[8,3,1,64,3,64]{5,4,2,1,3,0:T(4,128)S(1)} %bitcast.87), kind=kLoop, calls=%fused_computation | loop fusion | flops 589824 | bytes 4718592 | tf_op jit(solution)/shard_map/transpose | solution.py:195
  181.6 7.5 %reshape_reshape.3 = f32[8,64,1152]{2,1,0:T(8,128)} reshape(f32[8,64,3,2,3,64]{5,4,3,2,1,0:T(4,128)} %maximum_bitcast_fusion) | data formatting | bytes 4718592 | tf_op jit(solution)/shard_map/reshape;reshape | solution.py:272
  189.1 3.8 %mul.191 = f32[8,64,18,64]{3,2,1,0:T(8,128)} broadcast(f32[8,64,18]{2,1,0:T(8,128)S(1)} %copy.146), dimensions={0,1,2} | broadcast | bytes 2396160 | tf_op jit(solution)/shard_map/mul | solution.py:272
  192.9 5.2 %mul.192 = f32[8,64,1152]{2,1,0:T(8,128)} reshape(f32[8,64,18,64]{3,2,1,0:T(8,128)} %mul.191) | data formatting | bytes 4718592 | tf_op jit(solution)/shard_map/mul | solution.py:272
  202.6 41.4 %reduce-scatter.3.cloned.1.call-done = f32[2,64,1170]{2,1,0:T(8,128)} async-done(((f32[8,64,1170]{2,1,0:T(8,128)}), f32[2,64,1170]{2,1,0:T(8,128)}) %reduce-scatter.3.cloned.1.call-update) | async-done | bytes 599056 | tf_op jit(solution)/shard_map/reduce_scatter | solution.py:276
  255.7 24.5 %all-gather.5.cloned.1.call-done = bf16[8,64,1152]{2,1,0:T(8,128)(2,1)} async-done(((bf16[2,64,1152]{2,1,0:T(8,128)(2,1)}), bf16[8,64,1152]{2,1,0:T(8,128)(2,1)}) %all-gather.5.cloned.1.call-update) | async-done | bytes 1179664 | tf_op jit(solution)/shard_map/all_gather | solution.py:292
  280.1 3.2 fusion.44
  283.3 5.0 %fusion.9 = f32[512,1152]{1,0:T(8,128)} fusion(bf16[384,1152]{1,0:T(8,128)(2,1)} %param.21, bf16[512,1152]{1,0:T(8,128)(2,1)} %bitcast.108, bf16[1152,384]{1,0:T(8,128)(2,1)} %param.20, f32[512,384]{1,0:T(8,128)} %fusion.44), kind=kOutput, calls=%fused_computation.27 | convolution fusion | flops 907149312 | bytes 6094848 | tf_op jit(solution)/shard_map/dot_general | solution.py:297
  289.0 36.5 %reduce-scatter.5.cloned.1.call-done = f32[2,64,1152]{2,1,0:T(8,128)} async-done(((f32[8,64,1152]{2,1,0:T(8,128)}), f32[2,64,1152]{2,1,0:T(8,128)}) %reduce-scatter.5.cloned.1.call-update) | async-done | bytes 589840 | tf_op jit(solution)/shard_map/reduce_scatter | solution.py:296
  327.7 10.7 %all-to-all-start.1 = ((bf16[2,64,1152]{2,0,1:T(2,128)(2,1)}), bf16[2,64,1152]{2,0,1:T(2,128)(2,1)S(1)}, u32[]{:S(2)}, u32[]{:S(2)}) async-start(bf16[2,64,1152]{2,0,1:T(2,128)(2,1)} %copy.153), calls=%async_computation.3 | async-start | bytes 589824 | tf_op jit(solution)/shard_map/all_to_all | solution.py:307
  342.6 8.4 %all-to-all-done.1 = bf16[2,64,1152]{2,0,1:T(2,128)(2,1)S(1)} async-done(((bf16[2,64,1152]{2,0,1:T(2,128)(2,1)}), bf16[2,64,1152]{2,0,1:T(2,128)(2,1)S(1)}, u32[]{:S(2)}, u32[]{:S(2)}) %all-to-all-start.1) | async-done | bytes 294944 | tf_op jit(solution)/shard_map/all_to_all | solution.py:307
  (93 shorter events, 62.0 us)
Async XLA Ops:
  7.2 245.3 %copy-start = (bf16[1152,1152]{1,0:T(8,128)(2,1)S(1)}, bf16[1152,1152]{1,0:T(8,128)(2,1)}, u32[]{:S(2)}) copy-start(bf16[1152,1152]{1,0:T(8,128)(2,1)} %param.17) | copy-start | bytes 7962628
  9.3 25.8 %all-to-all-start = ((bf16[2,64,1152]{2,0,1:T(2,128)(2,1)}), bf16[2,64,1152]{2,0,1:T(2,128)(2,1)S(1)}, u32[]{:S(2)}, u32[]{:S(2)}) async-start(bf16[2,64,1152]{2,0,1:T(2,128)(2,1)} %copy.131), calls=%async_computation | async-start | bytes 589824 | tf_op jit(solution)/shard_map/all_to_all | solution.py:231
  22.5 35.1 %all-gather.3.cloned.1.call-start = ((), (), s32[]{:S(2)}) async-start(), calls=%async_computation.4 | async-start | bytes 1474560 | tf_op jit(solution)/shard_map/all_gather | solution.py:232
  35.9 208.1 %reduce-scatter.3.cloned.1.call-start = ((), (), s32[]{:S(2)}) async-start(), calls=%async_computation.5 | async-start | bytes 3276800 | tf_op jit(solution)/shard_map/reduce_scatter | solution.py:276
  38.5 1.5 copy-start.7
  38.7 20.4 %copy-start.5 = (f32[1152]{0:T(1024)S(1)}, f32[1152]{0:T(1024)}, u32[]{:S(2)}) copy-start(f32[1152]{0:T(1024)} %param.15) | copy-start | bytes 13828
  77.6 5.5 %copy-start.2 = (f32[8,64,32]{2,1,0:T(8,128)S(1)}, f32[8,64,32]{2,1,0:T(8,128)}, u32[]{:S(2)}) copy-start(f32[8,64,32]{2,1,0:T(8,128)} %get-tuple-element.35) | copy-start | bytes 196612
  77.6 5.5 %copy-start.3 = (f32[8,64,32]{2,1,0:T(8,128)S(1)}, f32[8,64,32]{2,1,0:T(8,128)}, u32[]{:S(2)}) copy-start(f32[8,64,32]{2,1,0:T(8,128)} %get-tuple-element.36) | copy-start | bytes 196612
  202.5 77.6 %all-gather.5.cloned.1.call-start = ((), (), s32[]{:S(2)}) async-start(), calls=%async_computation.6 | async-start | bytes 1474560 | tf_op jit(solution)/shard_map/all_gather | solution.py:292
  246.6 5.9 %copy-start.1 = (bf16[2,64,1152]{2,1,0:T(8,128)(2,1)S(1)}, bf16[2,64,1152]{2,1,0:T(8,128)(2,1)}, u32[]{:S(2)}) copy-start(bf16[2,64,1152]{2,1,0:T(8,128)(2,1)} %copy.132) | copy-start | bytes 884740
  252.5 2.0 copy-start.6
  255.4 70.2 %reduce-scatter.5.cloned.1.call-start = ((), (), s32[]{:S(2)}) async-start(), calls=%async_computation.7 | async-start | bytes 2949120 | tf_op jit(solution)/shard_map/reduce_scatter | solution.py:296
  288.3 0.7 copy-start.8
  288.3 50.1 %copy-start.4 = (f32[8,64,64]{2,1,0:T(8,128)S(1)}, f32[8,64,64]{2,1,0:T(8,128)}, u32[]{:S(2)}) copy-start(f32[8,64,64]{2,1,0:T(8,128)} %get-tuple-element.39) | copy-start | bytes 393220
  326.7 15.1 %copy-start.9 = (s32[8]{0:T(128)S(1)}, s32[8]{0:T(128)}, u32[]{:S(2)}) copy-start(s32[8]{0:T(128)} %param.27) | copy-start | bytes 100
  327.7 23.4 %all-to-all-start.1 = ((bf16[2,64,1152]{2,0,1:T(2,128)(2,1)}), bf16[2,64,1152]{2,0,1:T(2,128)(2,1)S(1)}, u32[]{:S(2)}, u32[]{:S(2)}) async-start(bf16[2,64,1152]{2,0,1:T(2,128)(2,1)} %copy.153), calls=%async_computation.3 | async-start | bytes 589824 | tf_op jit(solution)/shard_map/all_to_all | solution.py:307
Sparse Core Ops, SparseCore 0:
  36.0 21.4 all-gather.2
  202.7 41.2 reduce-scatter.2
  255.5 24.6 all-gather.4
  288.4 37.0 reduce-scatter.4

commit v2 on v1

--- a/solution.py
+++ b/solution.py
@@ -76,21 +76,37 @@
     q_ref = refs[0]
     page_refs = refs[1 : 1 + slots]
     dk_ref, dv_ref, dmask_ref = refs[1 + slots : 4 + slots]
-    m_ref, l_ref, acc_ref = refs[4 + slots :]
+    acc_ref, stat_ref = refs[4 + slots :]
     request = pl.program_id(0)
-    rows = q_ref.shape[2]
+    tree_length = q_ref.shape[1]
     page_length = page_refs[0].shape[2]
-    lane_ids = lax.broadcasted_iota(jnp.int32, (rows, page_length), 1)
-    draft_open = dmask_ref[0] > 0.5
+    rows = 6 * tree_length
+    half = rows // 2
+    low_t = lax.broadcasted_iota(jnp.int32, (tree_length, 128), 1) < 64
+    low_h = lax.broadcasted_iota(jnp.int32, (half, 128), 1) < 64
+    key_lanes = lax.broadcasted_iota(jnp.int32, (rows, page_length), 1)
+    stat_lanes = lax.broadcasted_iota(jnp.int32, (rows, 128), 1)
+    draft_open = jnp.concatenate([dmask_ref[0]] * 6, axis=0) > 0.5
     nt = (((1,), (1,)), ((), ()))
     for c in range(chunks):
         lanes = pl.ds(c * 128, 128)
-        qc = q_ref[0, c]
+        tiles = [q_ref[0, :, pl.ds(c * 384 + 128 * j, 128)].astype(jnp.float32) for j in range(3)]
+        turned0 = pltpu.roll(tiles[0], 64, 1)
+        turned2 = pltpu.roll(tiles[2], 64, 1)
+        blocks = [
+            jnp.where(low_t, tiles[0], 0.0),
+            jnp.where(low_t, turned0, 0.0),
+            jnp.where(low_t, tiles[1], 0.0),
+            jnp.where(low_t, 0.0, tiles[1]),
+            jnp.where(low_t, 0.0, turned2),
+            jnp.where(low_t, 0.0, tiles[2]),
+        ]
+        qc = jnp.concatenate(blocks, axis=0).astype(jnp.bfloat16)
         parts = []
         for s in range(slots):
             kc = page_refs[s][0, 0, :, lanes]
             sc = lax.dot_general(qc, kc, nt, preferred_element_type=jnp.float32) * SCALE
-            sc = jnp.where(lane_ids < limit_ref[request, s], sc, -jnp.inf)
+            sc = jnp.where(key_lanes < limit_ref[request, s], sc, -jnp.inf)
             parts.append(sc)
         kd = dk_ref[0, :, lanes]
         sd = lax.dot_general(qc, kd, nt, preferred_element_type=jnp.float32) * SCALE
@@ -111,42 +127,41 @@
                 page_refs[s][0, 1, :, lanes],
                 preferred_element_type=jnp.float32,
             )
-        m_ref[0, c] = peak
-        l_ref[0, c] = total
-        acc_ref[0, c] = acc
-
-
-def paged_partials(q2, cache, page_list, limits, draft_keys, draft_values, draft_mask):
-    requests, chunks, rows, lanes = q2.shape
+        acc_ref[0, c] = jnp.where(low_h, acc[:half], acc[half:])
+        stats = jnp.where(stat_lanes == 0, peak, jnp.where(stat_lanes == 1, total, 0.0))
+        stat_ref[0, c] = jnp.transpose(stats)[0:8, :]
+
+
+def paged_partials(queries, cache, page_list, limits, draft_keys, draft_values, draft_mask):
+    requests, tree_length, query_columns = queries.shape
+    chunks = KEY_VALUE_HEADS // 2
+    rows = 6 * tree_length
     slots = page_list.shape[1]
     page_length = cache.shape[2]
     width = cache.shape[3]
-    tree_length = draft_keys.shape[1]
 
     def page_map(s):
         return lambda k, pages, limit: (pages[k, s], 0, 0, 0)
 
-    in_specs = [pl.BlockSpec((1, chunks, rows, lanes), lambda k, pages, limit: (k, 0, 0, 0))]
+    in_specs = [pl.BlockSpec((1, tree_length, query_columns), lambda k, pages, limit: (k, 0, 0))]
     in_specs += [pl.BlockSpec((1, 2, page_length, width), page_map(s)) for s in range(slots)]
     in_specs += [
         pl.BlockSpec((1, tree_length, width), lambda k, pages, limit: (k, 0, 0)),
         pl.BlockSpec((1, tree_length, width), lambda k, pages, limit: (k, 0, 0)),
-        pl.BlockSpec((1, rows, tree_length), lambda k, pages, limit: (k, 0, 0)),
+        pl.BlockSpec((1, tree_length, tree_length), lambda k, pages, limit: (k, 0, 0)),
     ]
     out_specs = [
-        pl.BlockSpec((1, chunks, rows, 1), lambda k, pages, limit: (k, 0, 0, 0)),
-        pl.BlockSpec((1, chunks, rows, 1), lambda k, pages, limit: (k, 0, 0, 0)),
-        pl.BlockSpec((1, chunks, rows, lanes), lambda k, pages, limit: (k, 0, 0, 0)),
+        pl.BlockSpec((1, chunks, rows // 2, 128), lambda k, pages, limit: (k, 0, 0, 0)),
+        pl.BlockSpec((1, chunks, 8, rows), lambda k, pages, limit: (k, 0, 0, 0)),
     ]
     out_shape = [
-        jax.ShapeDtypeStruct((requests, chunks, rows, 1), jnp.float32),
-        jax.ShapeDtypeStruct((requests, chunks, rows, 1), jnp.float32),
-        jax.ShapeDtypeStruct((requests, chunks, rows, lanes), jnp.float32),
+        jax.ShapeDtypeStruct((requests, chunks, rows // 2, 128), jnp.float32),
+        jax.ShapeDtypeStruct((requests, chunks, 8, rows), jnp.float32),
     ]
     keys_seen = slots * page_length + tree_length
     cost = pl.CostEstimate(
-        flops=requests * chunks * rows * lanes * keys_seen * 4,
-        bytes_accessed=requests * (slots * 2 * page_length * width * 2 + chunks * rows * lanes * 6),
+        flops=requests * chunks * rows * 128 * keys_seen * 4,
+        bytes_accessed=requests * (slots * 2 * page_length * width * 2 + chunks * rows * 128 * 3),
         transcendentals=requests * chunks * rows * keys_seen,
     )
     grid_spec = pltpu.PrefetchScalarGridSpec(
@@ -162,39 +177,70 @@
         cost_estimate=cost,
         compiler_params=pltpu.CompilerParams(dimension_semantics=("arbitrary",)),
         name="paged_partials",
-    )(page_list, limits, q2, *([cache] * slots), draft_keys, draft_values, draft_mask)
-
-
-def pair_queries(queries, requests, tree_length):
-    head_columns = queries.shape[-1] // QUERY_HEADS
+    )(page_list, limits, queries, *([cache] * slots), draft_keys, draft_values, draft_mask)
+
+
+def rescale_kernel(acc_ref, stat_ref, peak_ref, out_ref):
+    chunks, half = acc_ref.shape[1], acc_ref.shape[2]
+    rows = 2 * half
+    low_h = lax.broadcasted_iota(jnp.int32, (half, 128), 1) < 64
+    for c in range(chunks):
+        local_peak = stat_ref[0, c, 0:1, :]
+        factor = jnp.exp(local_peak - peak_ref[0, c : c + 1, :])
+        scaled_total = stat_ref[0, c, 1:2, :] * factor
+        column = jnp.transpose(jnp.broadcast_to(factor, (128, rows)))
+        out_ref[0, c, 0:half, :] = acc_ref[0, c] * jnp.where(low_h, column[:half], column[half:])
+        pieces = [scaled_total[:, 128 * j : 128 * (j + 1)] for j in range(rows // 128)]
+        pieces.append(jnp.zeros((8 - rows // 128, 128), jnp.float32))
+        out_ref[0, c, half : half + 8, :] = jnp.concatenate(pieces, axis=0)
+
+
+def rescale(acc, stats, peak_all):
+    requests, chunks, half, lanes = acc.shape
+    rows = 2 * half
+    return pl.pallas_call(
+        rescale_kernel,
+        grid=(requests,),
+        in_specs=[
+            pl.BlockSpec((1, chunks, half, lanes), lambda k: (k, 0, 0, 0)),
+            pl.BlockSpec((1, chunks, 8, rows), lambda k: (k, 0, 0, 0)),
+            pl.BlockSpec((1, chunks, rows), lambda k: (k, 0, 0)),
+        ],
+        out_specs=pl.BlockSpec((1, chunks, half + 8, lanes), lambda k: (k, 0, 0, 0)),
+        out_shape=jax.ShapeDtypeStruct((requests, chunks, half + 8, lanes), jnp.float32),
+        compiler_params=pltpu.CompilerParams(dimension_semantics=("arbitrary",)),
+        name="rescale_partials",
+    )(acc, stats, peak_all)
+
+
+def finish_attention(shared, requests, tree_length):
     group = QUERY_HEADS // KEY_VALUE_HEADS
-    chunks = KEY_VALUE_HEADS // 2
-    shaped = queries.reshape(requests, tree_length, chunks, 2, group, head_columns)
-    shaped = shaped.transpose(0, 2, 3, 1, 4, 5).reshape(
-        requests, chunks, 2, tree_length * group, head_columns
-    )
-    zeros = jnp.zeros_like(shaped[:, :, 0])
-    top = jnp.concatenate([shaped[:, :, 0], zeros], axis=-1)
-    bottom = jnp.concatenate([zeros, shaped[:, :, 1]], axis=-1)
-    return jnp.concatenate([top, bottom], axis=2)
-
-
-def unpair_rows(values, requests, tree_length):
-    group = QUERY_HEADS // KEY_VALUE_HEADS
-    chunks = KEY_VALUE_HEADS // 2
-    shaped = values.reshape(requests, chunks, 2, tree_length, group)
-    return shaped.transpose(0, 3, 1, 2, 4).reshape(requests, tree_length, QUERY_HEADS)
-
-
-def unpair_sums(acc, requests, tree_length):
-    group = QUERY_HEADS // KEY_VALUE_HEADS
-    chunks = KEY_VALUE_HEADS // 2
-    head_columns = acc.shape[-1] // 2
-    shaped = acc.reshape(requests, chunks, 2, tree_length, group, 2, head_columns)
-    diagonal = jnp.stack([shaped[:, :, 0, :, :, 0], shaped[:, :, 1, :, :, 1]], axis=2)
-    return diagonal.transpose(0, 3, 1, 2, 4, 5).reshape(
-        requests, tree_length, QUERY_HEADS * head_columns
-    )
+    chunks = shared.shape[1]
+    half = group * tree_length
+    sums = shared[:, :, :half, :].reshape(requests, chunks, group, tree_length, 2, 64)
+    totals = shared[:, :, half : half + 2 * group * tree_length // 128, :].reshape(
+        requests, chunks, 2, group, tree_length
+    )
+    totals = totals.transpose(0, 1, 3, 4, 2)[..., None]
+    result = (sums / totals).transpose(0, 3, 1, 4, 2, 5)
+    return result.reshape(requests * tree_length, chunks * 2 * group * 64).astype(jnp.bfloat16)
+
+
+def rotate_flat(values, token_positions, head_columns):
+    half_width = head_columns // 2
+    frequency = THETA ** (-jnp.arange(half_width, dtype=jnp.float32) / half_width)
+    angles = token_positions.astype(jnp.float32)[:, None] * frequency
+    cosine = jnp.cos(angles)
+    sines = jnp.sin(angles)
+    repeats = values.shape[-1] // head_columns
+    cosine = jnp.tile(jnp.concatenate([cosine, cosine], axis=-1), (1, repeats))
+    sines = jnp.tile(jnp.concatenate([-sines, sines], axis=-1), (1, repeats))
+    columns = jnp.arange(values.shape[-1], dtype=jnp.int32)
+    front = (columns % head_columns) < half_width
+    partner = jnp.where(
+        front[None, :], jnp.roll(values, -half_width, axis=-1), jnp.roll(values, half_width, axis=-1)
+    )
+    return values * cosine + partner * sines
 
 
 def body(
@@ -239,49 +285,33 @@
     reached = ancestors(parents)
     depths = jnp.sum(reached, axis=-1).astype(jnp.int32) - 1
     token_positions = cache_len[:, None] + depths
-    queries = apply_rotation(
-        projected[..., :query_columns].astype(jnp.float32), token_positions, QUERY_HEADS
-    ).astype(jnp.bfloat16)
-    keys_all = apply_rotation(
-        projected[..., query_columns : query_columns + key_value_columns].astype(jnp.float32),
-        token_positions,
-        KEY_VALUE_HEADS,
-    ).astype(jnp.bfloat16)
+    flat_positions = token_positions.reshape(-1)
+    head_columns = query_columns // QUERY_HEADS
+    flat = projected.reshape(requests * tree_length, channels)
+    queries = rotate_flat(
+        flat[:, :query_columns].astype(jnp.float32), flat_positions, head_columns
+    ).astype(jnp.bfloat16).reshape(requests, tree_length, query_columns)
+    keys_all = rotate_flat(
+        flat[:, query_columns : query_columns + key_value_columns].astype(jnp.float32),
+        flat_positions,
+        head_columns,
+    ).astype(jnp.bfloat16).reshape(requests, tree_length, key_value_columns)
     values_all = projected[..., query_columns + key_value_columns :]
 
-    group = QUERY_HEADS // KEY_VALUE_HEADS
-    q2 = pair_queries(queries, requests, tree_length)
     page_list = page_table[:, 0, :]
     starts = (
         jnp.arange(slots_count, dtype=jnp.int32)[None, :] * rep_count + rep_index
     ) * page_length
     limits = cache_len[:, None] - starts
     mine = (jnp.arange(requests, dtype=jnp.int32) // owner_page_count) == rep_index
-    open_rows = jnp.where(mine[:, None, None], reached, 0.0)
-    open_rows = jnp.repeat(open_rows, group, axis=1)
-    draft_mask = jnp.concatenate([open_rows, open_rows], axis=1)
-    peaks, totals, sums = paged_partials(
-        q2, cache, page_list, limits, keys_all, values_all, draft_mask
-    )
-    peaks = unpair_rows(peaks, requests, tree_length)
-    totals = unpair_rows(totals, requests, tree_length)
-    sums = unpair_sums(sums, requests, tree_length)
-
-    peak_all = lax.pmax(peaks, "rep")
-    factors = jnp.exp(peaks - peak_all)
-    scaled = (sums.reshape(requests, tree_length, QUERY_HEADS, -1) * factors[..., None]).reshape(
-        requests, tree_length, query_columns
-    )
-    joined = jnp.concatenate([scaled, totals * factors], axis=-1)
+    draft_mask = jnp.where(mine[:, None, None], reached, 0.0)
+    sums, stats = paged_partials(
+        queries, cache, page_list, limits, keys_all, values_all, draft_mask
+    )
+    peak_all = lax.pmax(stats[:, :, 0, :], "rep")
+    joined = rescale(sums, stats, peak_all)
     shared = lax.psum_scatter(joined, "rep", scatter_dimension=0, tiled=True)
-    attended = (
-        (
-            shared[..., :query_columns].reshape(owner_page_count, tree_length, QUERY_HEADS, -1)
-            / shared[..., query_columns:][..., None]
-        )
-        .reshape(-1, query_columns)
-        .astype(jnp.bfloat16)
-    )
+    attended = finish_attention(shared, owner_page_count, tree_length)
 
     mixed = jnp.dot(attended, w_out, preferred_element_type=jnp.float32)
     residual = (mixed + own_hidden.reshape(-1, model_width).astype(jnp.float32)).astype(

time: 363 us -> 279 us (0.77); the launches traced: 359 us -> 278 us
  local copies, waits for them, and re-layouts: 90 us -> 34.2 us
  other arithmetic: 36.9 us -> 12.4 us
  Pallas kernels: 22.2 us -> 35.2 us
  waiting for transfers between devices: 135 us -> 123 us
    reshape x7 -> x2, local copies, waits for them, and re-layouts: 21.7 us -> 1.8 us  [the longest x1 1.72 us: finish_attention(): shared[:, :, :half, :].reshape(requests, chunks, group, tree_length, 2, 64)]
    pallas_call x2 -> x1, local copies, waits for them, and re-layouts: 18.5 us -> 1.06 us  [paged_partials(): pl.pallas_call(functools.partial(paged_kernel, slots, chunks), grid_spec=...]
    all_gather x1, waiting for transfers between devices: 14.9 us -> 1.61 us  [body(): all_hidden = lax.all_gather(own_hidden, 'rep', axis=0, tiled=True)]
    another operation x1 -> x9, local copies, waits for them, and re-layouts: 7.54 us -> 17.3 us  [the longest x4 9.06 us: rotate_flat(): cosine = jnp.tile(jnp.concatenate([cosine, cosine], axis=-1), (1, repeats))]
    mul x3 -> x0, local copies, waits for them, and re-layouts: 9.16 us -> none  [the longest x2 9.01 us: body(): sums.reshape(requests, tree_length, QUERY_HEADS, -1) * factors[..., None]]
    slice x5 -> x6, local copies, waits for them, and re-layouts: 11.5 us -> 3.12 us  [the longest x4 1.27 us: rotate_flat(): jnp.roll(values, half_width, axis=-1)]
    another operation x2 -> x0, other arithmetic: 7.86 us -> none
    concatenate x4 -> x1, other arithmetic: 6.96 us -> 0.02 us  [rotate_flat(): cosine = jnp.tile(jnp.concatenate([cosine, cosine], axis=-1), (1, repeats))]
  transfers between devices with their start and end apart: 6 -> 6, of which waited for: 6 -> 6; matrix products, arithmetic and copies ran while one was open for 4% -> 9% of each run, Pallas kernels for 0% -> 0%
where the time goes in v2:
time: 279 us; the launch traced here: 278 us
  waiting for transfers between devices  123 us (44%)
  Pallas kernels  35.2 us (13%)
  local copies, waits for them, and re-layouts  34.2 us (12%)
  starting transfers between devices  24.6 us (9%)
  matrix products  21.2 us (8%)
  blocking collectives  14.2 us (5%)
  between operations  14.1 us (5%)
  other arithmetic  12.4 us (4%)
    reduce_scatter x1, waiting for transfers between devices, body(): shared = lax.psum_scatter(joined, 'rep', scatter_dimension=0, tiled=True)  39.7 us
    reduce_scatter x1, waiting for transfers between devices, body(): lax.psum_scatter(jnp.dot(activated, w_down, preferred_element_type=jnp.fl...  36.5 us
    pallas_call x1, Pallas kernels, paged_partials(): pl.pallas_call(functools.partial(paged_kernel, slots, chunks), grid_spec=...  28.5 us
    all_gather x1, waiting for transfers between devices, body(): lax.all_gather(ffn_in, 'rep', axis=0, tiled=True).reshape(-1, model_width)  24.7 us
    pmax x1, blocking collectives, body(): peak_all = lax.pmax(stats[:, :, 0, :], 'rep')  14.2 us
    all_to_all x1, starting transfers between devices, body(): lax.all_to_all(local_rows, 'req', split_axis=1, concat_axis=1, tiled=True)  13.3 us
    all_to_all x1, starting transfers between devices, body(): lax.all_to_all(out_own, 'req', split_axis=1, concat_axis=1, tiled=True)  10.8 us
    all_to_all x1, waiting for transfers between devices, body(): lax.all_to_all(out_own, 'req', split_axis=1, concat_axis=1, tiled=True)  10.2 us
  transfers between devices with their start and end apart: 6, of which 6 were waited for; matrix products, arithmetic and copies ran while one was open for 9% of the time, Pallas kernels for 0%

profile of v2, /device:TPU:1, one launch (start us, length us, event | category | flops | bytes accessed | tf_op | source)
XLA Modules:
  0.0 278.3 jit_solution(1756284272185771622)
XLA Ops:
  7.2 2.1 copy.88
  9.3 13.3 %all-to-all-start = ((bf16[2,64,1152]{2,0,1:T(2,128)(2,1)}), bf16[2,64,1152]{2,0,1:T(2,128)(2,1)S(1)}, u32[]{:S(2)}, u32[]{:S(2)}) async-start(bf16[2,64,1152]{2,0,1:T(2,128)(2,1)} %copy.88), calls=%async_computation | async-start | bytes 589824 | tf_op jit(solution)/shard_map/all_to_all | solution.py:277
  25.5 9.7 %all-to-all-done = bf16[2,64,1152]{2,0,1:T(2,128)(2,1)S(1)} async-done(((bf16[2,64,1152]{2,0,1:T(2,128)(2,1)}), bf16[2,64,1152]{2,0,1:T(2,128)(2,1)S(1)}, u32[]{:S(2)}, u32[]{:S(2)}) %all-to-all-start) | async-done | bytes 294944 | tf_op jit(solution)/shard_map/all_to_all | solution.py:277
  39.1 1.7 tile.18
  40.8 3.1 %copy.93 = f32[512,1152]{1,0:T(8,128)} copy(f32[512,1152]{0,1:T(8,128)} %bitcast.67) | data formatting | bytes 4718592 | tf_op jit(solution)/shard_map/tile | solution.py:237
  43.9 1.7 tile.16
  45.6 3.1 %copy.92 = f32[512,1152]{1,0:T(8,128)} copy(f32[512,1152]{0,1:T(8,128)} %bitcast.68) | data formatting | bytes 4718592 | tf_op jit(solution)/shard_map/tile | solution.py:236
  51.2 1.9 tile.40
  53.0 2.3 copy.94
  60.9 5.1 %convolution_convert_fusion = bf16[512,1920]{1,0:T(8,128)(2,1)S(1)} fusion(bf16[512,1152]{1,0:T(8,128)(2,1)S(1)} %bitcast.79, bf16[1152,1920]{1,0:T(8,128)(2,1)} %param.16), kind=kOutput, calls=%fused_computation | convolution fusion | flops 2265907200 | bytes 7569408 | tf_op jit(solution)/shard_map/dot_general | solution.py:281
  69.8 2.1 fusion.7
  73.1 28.5 %paged_partials.1 = (f32[8,3,192,128]{3,2,1,0:T(8,128)}, f32[8,3,8,384]{3,2,1,0:T(8,128)}) custom-call(s32[8,5]{1,0:T(8,128)} %bitcast.83, s32[8,5]{1,0:T(8,128)} %broadcast_subtract_fusion.limit_ref, bf16[8,64,1152]{2,1,0:T(8,128)(2,1)} %bitcast.71, bf16[16,2,128,384]{3,2,1,0:T(8,128)(2,1)} %refs_5_.1, bf16[16,2,128,384]{3,2,1,0:T(8,128)(2,1)} %refs_5_.1, ...), custom_call_target="tpu_custom_call" | custom-call | flops 3321888768 | bytes 11403264 | tf_op jit(solution)/shard_map/paged_partials/pallas_call | solution.py:173
  102.7 14.2 %pmax.7.peak_ref = f32[8,3,384]{2,1,0:T(4,128)} all-reduce(f32[8,3,384]{2,1,0:T(4,128)S(1)} %slice_bitcast_fusion), channel_id=1, replica_groups=mesh['req'=64,'rep'=4] {'rep'}, use_global_device_ids=true, to_apply=%region_2.3 | all-reduce | flops 9216 | bytes 73728 | tf_op jit(solution)/shard_map/pmax | solution.py:311
  116.8 6.7 %rescale_partials.1 = f32[8,3,200,128]{3,2,1,0:T(8,128)} custom-call(f32[8,3,192,128]{3,2,1,0:T(8,128)} %get-tuple-element.4.acc_ref, f32[8,3,8,384]{3,2,1,0:T(8,128)} %get-tuple-element.5.stat_ref, f32[8,3,384]{2,1,0:T(4,128)} %pmax.7.peak_ref), custom_call_target="tpu_custom_call" | custom-call | tf_op jit(solution)/shard_map/rescale_partials/pallas_call | solution.py:201
  123.8 39.7 %reduce-scatter.3.cloned.1.call-done = f32[2,3,200,128]{3,2,1,0:T(8,128)} async-done(((f32[8,3,200,128]{3,2,1,0:T(8,128)}), f32[2,3,200,128]{3,2,1,0:T(8,128)}) %reduce-scatter.3.cloned.1.call-update) | async-done | bytes 614416 | tf_op jit(solution)/shard_map/reduce_scatter | solution.py:313
  166.1 1.7 reshape.173
  167.8 2.5 fusion.21
  172.7 1.7 multiply_reduce_fusion
  175.3 24.7 %all-gather.5.cloned.1.call-done = bf16[8,64,1152]{2,1,0:T(8,128)(2,1)} async-done(((bf16[2,64,1152]{2,1,0:T(8,128)(2,1)}), bf16[8,64,1152]{2,1,0:T(8,128)(2,1)}) %all-gather.5.cloned.1.call-update) | async-done | bytes 1179664 | tf_op jit(solution)/shard_map/all_gather | solution.py:322
  200.0 3.2 %fusion.60 = f32[512,384]{1,0:T(8,128)} fusion(bf16[512,1152]{1,0:T(8,128)(2,1)} %bitcast.85, bf16[1152,384]{1,0:T(8,128)(2,1)} %param.19), kind=kOutput, calls=%fused_computation.110 | convolution fusion | flops 452984832 | bytes 2850816 | tf_op jit(solution)/shard_map/dot_general | solution.py:323
  203.3 5.0 %fusion.9 = f32[512,1152]{1,0:T(8,128)} fusion(bf16[384,1152]{1,0:T(8,128)(2,1)} %param.21, bf16[512,1152]{1,0:T(8,128)(2,1)} %bitcast.86, bf16[1152,384]{1,0:T(8,128)(2,1)} %param.20, f32[512,384]{1,0:T(8,128)} %fusion.60), kind=kOutput, calls=%fused_computation.15 | convolution fusion | flops 907149312 | bytes 6094848 | tf_op jit(solution)/shard_map/dot_general | solution.py:327
  209.0 36.5 %reduce-scatter.5.cloned.1.call-done = f32[2,64,1152]{2,1,0:T(8,128)} async-done(((f32[8,64,1152]{2,1,0:T(8,128)}), f32[2,64,1152]{2,1,0:T(8,128)}) %reduce-scatter.5.cloned.1.call-update) | async-done | bytes 589840 | tf_op jit(solution)/shard_map/reduce_scatter | solution.py:326
  247.7 10.8 %all-to-all-start.1 = ((bf16[2,64,1152]{2,0,1:T(2,128)(2,1)}), bf16[2,64,1152]{2,0,1:T(2,128)(2,1)S(1)}, u32[]{:S(2)}, u32[]{:S(2)}) async-start(bf16[2,64,1152]{2,0,1:T(2,128)(2,1)} %copy.101), calls=%async_computation.3 | async-start | bytes 589824 | tf_op jit(solution)/shard_map/all_to_all | solution.py:337
  260.9 10.2 %all-to-all-done.1 = bf16[2,64,1152]{2,0,1:T(2,128)(2,1)S(1)} async-done(((bf16[2,64,1152]{2,0,1:T(2,128)(2,1)}), bf16[2,64,1152]{2,0,1:T(2,128)(2,1)S(1)}, u32[]{:S(2)}, u32[]{:S(2)}) %all-to-all-start.1) | async-done | bytes 294944 | tf_op jit(solution)/shard_map/all_to_all | solution.py:337
  (87 shorter events, 32.7 us)
Async XLA Ops:
  7.2 165.5 %copy-start = (bf16[1152,1152]{1,0:T(8,128)(2,1)S(1)}, bf16[1152,1152]{1,0:T(8,128)(2,1)}, u32[]{:S(2)}) copy-start(bf16[1152,1152]{1,0:T(8,128)(2,1)} %param.17) | copy-start | bytes 7962628
  9.3 26.9 %copy-start.9 = (s32[8,1,5]{0,1,2:T(1,128)S(1)}, s32[8,1,5]{0,1,2:T(1,128)}, u32[]{:S(2)}) copy-start(s32[8,1,5]{0,1,2:T(1,128)} %param.23) | copy-start | bytes 484
  9.3 25.9 %all-to-all-start = ((bf16[2,64,1152]{2,0,1:T(2,128)(2,1)}), bf16[2,64,1152]{2,0,1:T(2,128)(2,1)S(1)}, u32[]{:S(2)}, u32[]{:S(2)}) async-start(bf16[2,64,1152]{2,0,1:T(2,128)(2,1)} %copy.88), calls=%async_computation | async-start | bytes 589824 | tf_op jit(solution)/shard_map/all_to_all | solution.py:277
  22.6 35.1 %all-gather.3.cloned.1.call-start = ((), (), s32[]{:S(2)}) async-start(), calls=%async_computation.4 | async-start | bytes 1474560 | tf_op jit(solution)/shard_map/all_gather | solution.py:278
  24.3 14.2 %copy-start.10 = (s32[8]{0:T(128)S(1)}, s32[8]{0:T(128)}, u32[]{:S(2)}) copy-start(s32[8]{0:T(128)} %param.24) | copy-start | bytes 100
  36.0 127.5 %reduce-scatter.3.cloned.1.call-start = ((), (), s32[]{:S(2)}) async-start(), calls=%async_computation.5 | async-start | bytes 3072000 | tf_op jit(solution)/shard_map/reduce_scatter | solution.py:313
  39.0 4.8 %copy-start.5 = (f32[512,64]{0,1:T(8,128)}, f32[512,64]{0,1:T(8,128)S(1)}, u32[]{:S(2)}) copy-start(f32[512,64]{0,1:T(8,128)S(1)} %get-tuple-element.38) | copy-start | bytes 393220
  49.7 9.5 %copy-start.7 = (f32[1152]{0:T(1024)S(1)}, f32[1152]{0:T(1024)}, u32[]{:S(2)}) copy-start(f32[1152]{0:T(1024)} %param.15) | copy-start | bytes 13828
  67.1 1.9 copy-start.2
  67.2 2.6 copy-start.1
  69.8 2.1 copy-start.3
  123.5 76.5 %all-gather.5.cloned.1.call-start = ((), (), s32[]{:S(2)}) async-start(), calls=%async_computation.6 | async-start | bytes 1474560 | tf_op jit(solution)/shard_map/all_gather | solution.py:322
  167.8 4.9 %copy-start.4 = (bf16[2,64,1152]{2,1,0:T(8,128)(2,1)S(1)}, bf16[2,64,1152]{2,1,0:T(8,128)(2,1)}, u32[]{:S(2)}) copy-start(bf16[2,64,1152]{2,1,0:T(8,128)(2,1)} %copy.89) | copy-start | bytes 884740
  171.7 2.7 copy-start.8
  175.3 70.2 %reduce-scatter.5.cloned.1.call-start = ((), (), s32[]{:S(2)}) async-start(), calls=%async_computation.7 | async-start | bytes 2949120 | tf_op jit(solution)/shard_map/reduce_scatter | solution.py:326
  208.3 0.7 copy-start.11
  208.3 50.2 %copy-start.6 = (f32[8,64,64]{2,1,0:T(8,128)S(1)}, f32[8,64,64]{2,1,0:T(8,128)}, u32[]{:S(2)}) copy-start(f32[8,64,64]{2,1,0:T(8,128)} %get-tuple-element.35) | copy-start | bytes 393220
  245.5 14.5 %copy-start.12 = (s32[8]{0:T(128)S(1)}, s32[8]{0:T(128)}, u32[]{:S(2)}) copy-start(s32[8]{0:T(128)} %param.27) | copy-start | bytes 100
  247.7 23.4 %all-to-all-start.1 = ((bf16[2,64,1152]{2,0,1:T(2,128)(2,1)}), bf16[2,64,1152]{2,0,1:T(2,128)(2,1)S(1)}, u32[]{:S(2)}, u32[]{:S(2)}) async-start(bf16[2,64,1152]{2,0,1:T(2,128)(2,1)} %copy.101), calls=%async_computation.3 | async-start | bytes 589824 | tf_op jit(solution)/shard_map/all_to_all | solution.py:337
Sparse Core Ops, SparseCore 0:
  36.1 21.4 all-gather.2
  123.6 39.8 reduce-scatter.2
  175.4 24.6 all-gather.4
  208.4 37.0 reduce-scatter.4

commit v3 on v2

--- a/solution.py
+++ b/solution.py
@@ -76,7 +76,7 @@
     q_ref = refs[0]
     page_refs = refs[1 : 1 + slots]
     dk_ref, dv_ref, dmask_ref = refs[1 + slots : 4 + slots]
-    acc_ref, stat_ref = refs[4 + slots :]
+    (part_ref,) = refs[4 + slots :]
     request = pl.program_id(0)
     tree_length = q_ref.shape[1]
     page_length = page_refs[0].shape[2]
@@ -127,9 +127,12 @@
                 page_refs[s][0, 1, :, lanes],
                 preferred_element_type=jnp.float32,
             )
-        acc_ref[0, c] = jnp.where(low_h, acc[:half], acc[half:])
-        stats = jnp.where(stat_lanes == 0, peak, jnp.where(stat_lanes == 1, total, 0.0))
-        stat_ref[0, c] = jnp.transpose(stats)[0:8, :]
+        part_ref[0, c, 0:half, :] = jnp.where(low_h, acc[:half], acc[half:])
+        stats = jnp.where(stat_lanes == 0, total, jnp.where(stat_lanes == 1, peak, 0.0))
+        flipped = jnp.transpose(stats)
+        pieces = [flipped[j : j + 1, 128 * p : 128 * (p + 1)] for j in range(2) for p in range(3)]
+        pieces.append(jnp.zeros((2, 128), jnp.float32))
+        part_ref[0, c, half : half + 8, :] = jnp.concatenate(pieces, axis=0)
 
 
 def paged_partials(queries, cache, page_list, limits, draft_keys, draft_values, draft_mask):
@@ -151,12 +154,10 @@
         pl.BlockSpec((1, tree_length, tree_length), lambda k, pages, limit: (k, 0, 0)),
     ]
     out_specs = [
-        pl.BlockSpec((1, chunks, rows // 2, 128), lambda k, pages, limit: (k, 0, 0, 0)),
-        pl.BlockSpec((1, chunks, 8, rows), lambda k, pages, limit: (k, 0, 0, 0)),
+        pl.BlockSpec((1, chunks, rows // 2 + 8, 128), lambda k, pages, limit: (k, 0, 0, 0)),
     ]
     out_shape = [
-        jax.ShapeDtypeStruct((requests, chunks, rows // 2, 128), jnp.float32),
-        jax.ShapeDtypeStruct((requests, chunks, 8, rows), jnp.float32),
+        jax.ShapeDtypeStruct((requests, chunks, rows // 2 + 8, 128), jnp.float32),
     ]
     keys_seen = slots * page_length + tree_length
     cost = pl.CostEstimate(
@@ -180,50 +181,56 @@
     )(page_list, limits, queries, *([cache] * slots), draft_keys, draft_values, draft_mask)
 
 
-def rescale_kernel(acc_ref, stat_ref, peak_ref, out_ref):
-    chunks, half = acc_ref.shape[1], acc_ref.shape[2]
+def combine_kernel(part_ref, out_ref):
+    holders, chunks = part_ref.shape[0], part_ref.shape[2]
+    half = out_ref.shape[2]
     rows = 2 * half
+    pieces = rows // 128
     low_h = lax.broadcasted_iota(jnp.int32, (half, 128), 1) < 64
+
+    def as_column(row):
+        column = jnp.transpose(jnp.broadcast_to(row, (128, rows)))
+        return jnp.where(low_h, column[:half], column[half:])
+
     for c in range(chunks):
-        local_peak = stat_ref[0, c, 0:1, :]
-        factor = jnp.exp(local_peak - peak_ref[0, c : c + 1, :])
-        scaled_total = stat_ref[0, c, 1:2, :] * factor
-        column = jnp.transpose(jnp.broadcast_to(factor, (128, rows)))
-        out_ref[0, c, 0:half, :] = acc_ref[0, c] * jnp.where(low_h, column[:half], column[half:])
-        pieces = [scaled_total[:, 128 * j : 128 * (j + 1)] for j in range(rows // 128)]
-        pieces.append(jnp.zeros((8 - rows // 128, 128), jnp.float32))
-        out_ref[0, c, half : half + 8, :] = jnp.concatenate(pieces, axis=0)
-
-
-def rescale(acc, stats, peak_all):
-    requests, chunks, half, lanes = acc.shape
-    rows = 2 * half
+        tails = [part_ref[h, 0, c, half : half + 8, :] for h in range(holders)]
+        totals = [jnp.concatenate([t[p : p + 1] for p in range(pieces)], axis=1) for t in tails]
+        peaks = [
+            jnp.concatenate([t[pieces + p : pieces + p + 1] for p in range(pieces)], axis=1)
+            for t in tails
+        ]
+        top = peaks[0]
+        for peak in peaks[1:]:
+            top = jnp.maximum(top, peak)
+        total = jnp.zeros_like(top)
+        acc = jnp.zeros((half, 128), jnp.float32)
+        for h in range(holders):
+            factor = jnp.exp(peaks[h] - top)
+            total = total + totals[h] * factor
+            acc = acc + part_ref[h, 0, c, 0:half, :] * as_column(factor)
+        out_ref[0, c] = (acc / as_column(total)).astype(out_ref.dtype)
+
+
+def combine(parts):
+    holders, requests, chunks, rows_in, lanes = parts.shape
+    half = rows_in - 8
     return pl.pallas_call(
-        rescale_kernel,
+        combine_kernel,
         grid=(requests,),
-        in_specs=[
-            pl.BlockSpec((1, chunks, half, lanes), lambda k: (k, 0, 0, 0)),
-            pl.BlockSpec((1, chunks, 8, rows), lambda k: (k, 0, 0, 0)),
-            pl.BlockSpec((1, chunks, rows), lambda k: (k, 0, 0)),
-        ],
-        out_specs=pl.BlockSpec((1, chunks, half + 8, lanes), lambda k: (k, 0, 0, 0)),
-        out_shape=jax.ShapeDtypeStruct((requests, chunks, half + 8, lanes), jnp.float32),
+        in_specs=[pl.BlockSpec((holders, 1, chunks, rows_in, lanes), lambda k: (0, k, 0, 0, 0))],
+        out_specs=pl.BlockSpec((1, chunks, half, lanes), lambda k: (k, 0, 0, 0)),
+        out_shape=jax.ShapeDtypeStruct((requests, chunks, half, lanes), jnp.bfloat16),
         compiler_params=pltpu.CompilerParams(dimension_semantics=("arbitrary",)),
-        name="rescale_partials",
-    )(acc, stats, peak_all)
-
-
-def finish_attention(shared, requests, tree_length):
+        name="combine_holders",
+    )(parts)
+
+
+def finish_attention(attended, requests, tree_length):
     group = QUERY_HEADS // KEY_VALUE_HEADS
-    chunks = shared.shape[1]
-    half = group * tree_length
-    sums = shared[:, :, :half, :].reshape(requests, chunks, group, tree_length, 2, 64)
-    totals = shared[:, :, half : half + 2 * group * tree_length // 128, :].reshape(
-        requests, chunks, 2, group, tree_length
-    )
-    totals = totals.transpose(0, 1, 3, 4, 2)[..., None]
-    result = (sums / totals).transpose(0, 3, 1, 4, 2, 5)
-    return result.reshape(requests * tree_length, chunks * 2 * group * 64).astype(jnp.bfloat16)
+    chunks = attended.shape[1]
+    shaped = attended.reshape(requests, chunks, group, tree_length, 2, 64)
+    result = shaped.transpose(0, 3, 1, 4, 2, 5)
+    return result.reshape(requests * tree_length, chunks * 2 * group * 64)
 
 
 def rotate_flat(values, token_positions, head_columns):
@@ -305,13 +312,12 @@
     limits = cache_len[:, None] - starts
     mine = (jnp.arange(requests, dtype=jnp.int32) // owner_page_count) == rep_index
     draft_mask = jnp.where(mine[:, None, None], reached, 0.0)
-    sums, stats = paged_partials(
+    (parts,) = paged_partials(
         queries, cache, page_list, limits, keys_all, values_all, draft_mask
     )
-    peak_all = lax.pmax(stats[:, :, 0, :], "rep")
-    joined = rescale(sums, stats, peak_all)
-    shared = lax.psum_scatter(joined, "rep", scatter_dimension=0, tiled=True)
-    attended = finish_attention(shared, owner_page_count, tree_length)
+    parts = parts.reshape((rep_count, owner_page_count) + parts.shape[1:])
+    gathered = lax.all_to_all(parts, "rep", split_axis=0, concat_axis=0, tiled=True)
+    attended = finish_attention(combine(gathered), owner_page_count, tree_length)
 
     mixed = jnp.dot(attended, w_out, preferred_element_type=jnp.float32)
     residual = (mixed + own_hidden.reshape(-1, model_width).astype(jnp.float32)).astype(

time: 279 us -> 252 us (0.903)
  waiting for transfers between devices: 123 us -> 85.6 us
  blocking collectives: 14.2 us -> 31.8 us
  Pallas kernels: 35.2 us -> 32.4 us
    reduce_scatter x1 -> x0, waiting for transfers between devices: 39.7 us -> none  [body(): shared = lax.psum_scatter(joined, 'rep', scatter_dimension=0, tiled=True)]
    all_to_all x0 -> x1, blocking collectives: none -> 31.8 us  [body(): lax.all_to_all(parts, 'rep', split_axis=0, concat_axis=0, tiled=True)]
    pmax x1 -> x0, blocking collectives: 14.2 us -> none  [body(): peak_all = lax.pmax(stats[:, :, 0, :], 'rep')]
    reshape x2 -> x3, local copies, waits for them, and re-layouts: 1.8 us -> 5.08 us  [the longest x2 2.96 us: finish_attention(): shaped = attended.reshape(requests, chunks, group, tree_length, 2, 64)]
    pallas_call x1, Pallas kernels: 6.69 us -> 3.72 us  [combine(): pl.pallas_call(combine_kernel, grid=(requests,), in_specs=[pl.BlockSpec((...]
    all_gather x1, waiting for transfers between devices: 24.7 us -> 27.5 us  [body(): lax.all_gather(ffn_in, 'rep', axis=0, tiled=True).reshape(-1, model_width)]
  transfers between devices with their start and end apart: 6 -> 5, of which waited for: 6 -> 5; matrix products, arithmetic and copies ran while one was open for 9% -> 10% of each run, Pallas kernels for 0% -> 0%
where the time goes in v3:
time: 252 us; the launch traced here: 251 us
  waiting for transfers between devices  85.6 us (34%)
  Pallas kernels  32.4 us (13%)
  blocking collectives  31.8 us (13%)
  local copies, waits for them, and re-layouts  31.6 us (13%)
  starting transfers between devices  24.3 us (10%)
  matrix products  21.2 us (8%)
  between operations  14 us (6%)
  other arithmetic  9.81 us (4%)
    reduce_scatter x1, waiting for transfers between devices, body(): lax.psum_scatter(jnp.dot(activated, w_down, preferred_element_type=jnp.fl...  36.5 us
    all_to_all x1, blocking collectives, body(): lax.all_to_all(parts, 'rep', split_axis=0, concat_axis=0, tiled=True)  31.8 us
    pallas_call x1, Pallas kernels, paged_partials(): pl.pallas_call(functools.partial(paged_kernel, slots, chunks), grid_spec=...  28.7 us
    all_gather x1, waiting for transfers between devices, body(): lax.all_gather(ffn_in, 'rep', axis=0, tiled=True).reshape(-1, model_width)  27.5 us
    all_to_all x1, starting transfers between devices, body(): lax.all_to_all(local_rows, 'req', split_axis=1, concat_axis=1, tiled=True)  13.3 us
    all_to_all x1, starting transfers between devices, body(): lax.all_to_all(out_own, 'req', split_axis=1, concat_axis=1, tiled=True)  10.8 us
    all_to_all x1, waiting for transfers between devices, body(): lax.all_to_all(out_own, 'req', split_axis=1, concat_axis=1, tiled=True)  10.2 us
    all_to_all x1, waiting for transfers between devices, body(): lax.all_to_all(local_rows, 'req', split_axis=1, concat_axis=1, tiled=True)  9.69 us
  transfers between devices with their start and end apart: 5, of which 5 were waited for; matrix products, arithmetic and copies ran while one was open for 10% of the time, Pallas kernels for 0%

profile of v3, /device:TPU:1, one launch (start us, length us, event | category | flops | bytes accessed | tf_op | source)
XLA Modules:
  0.0 250.8 jit_solution(12398893312126548553)
XLA Ops:
  7.2 2.1 copy.78
  9.3 13.3 %all-to-all-start = ((bf16[2,64,1152]{2,0,1:T(2,128)(2,1)}), bf16[2,64,1152]{2,0,1:T(2,128)(2,1)S(1)}, u32[]{:S(2)}, u32[]{:S(2)}) async-start(bf16[2,64,1152]{2,0,1:T(2,128)(2,1)} %copy.78), calls=%async_computation | async-start | bytes 589824 | tf_op jit(solution)/shard_map/all_to_all | solution.py:284
  25.5 9.7 %all-to-all-done = bf16[2,64,1152]{2,0,1:T(2,128)(2,1)S(1)} async-done(((bf16[2,64,1152]{2,0,1:T(2,128)(2,1)}), bf16[2,64,1152]{2,0,1:T(2,128)(2,1)S(1)}, u32[]{:S(2)}, u32[]{:S(2)}) %all-to-all-start) | async-done | bytes 294944 | tf_op jit(solution)/shard_map/all_to_all | solution.py:284
  39.1 1.7 tile.18
  40.8 3.1 %copy.83 = f32[512,1152]{1,0:T(8,128)} copy(f32[512,1152]{0,1:T(8,128)} %bitcast.65) | data formatting | bytes 4718592 | tf_op jit(solution)/shard_map/tile | solution.py:244
  43.9 1.7 tile.16
  45.6 3.1 %copy.82 = f32[512,1152]{1,0:T(8,128)} copy(f32[512,1152]{0,1:T(8,128)} %bitcast.66) | data formatting | bytes 4718592 | tf_op jit(solution)/shard_map/tile | solution.py:243
  51.1 1.9 tile.40
  53.0 2.3 copy.84
  56.0 1.6 all-gather.3.cloned.1.call-done
  60.9 5.1 %convolution_convert_fusion = bf16[512,1920]{1,0:T(8,128)(2,1)S(1)} fusion(bf16[512,1152]{1,0:T(8,128)(2,1)S(1)} %bitcast.78, bf16[1152,1920]{1,0:T(8,128)(2,1)} %param.16), kind=kOutput, calls=%fused_computation | convolution fusion | flops 2265907200 | bytes 7569408 | tf_op jit(solution)/shard_map/dot_general | solution.py:288
  69.8 2.0 fusion.7
  73.0 28.7 %paged_partials.1 = f32[8,3,200,128]{3,2,1,0:T(8,128)} custom-call(s32[8,5]{1,0:T(8,128)} %bitcast.81, s32[8,5]{1,0:T(8,128)} %broadcast_subtract_fusion.limit_ref, bf16[8,64,1152]{2,1,0:T(8,128)(2,1)} %bitcast.69, bf16[16,2,128,384]{3,2,1,0:T(8,128)(2,1)} %refs_5_.1, bf16[16,2,128,384]{3,2,1,0:T(8,128)(2,1)} %refs_5_.1, bf16[16,2,128,384]{3,2,1,0:T(8,128)(2,1)} %refs_5_.1, ...), custom_call_target="tpu_custom_call" | custom-call | flops 3321888768 | bytes 11403264 | tf_op jit(solution)/shard_map/paged_partials/pallas_call | solution.py:174
  101.7 31.8 %all_to_all.15.part_ref = f32[4,2,3,200,128]{4,3,2,1,0:T(8,128)} all-to-all(f32[4,2,3,200,128]{4,3,2,1,0:T(8,128)} %bitcast.64), channel_id=1, replica_groups=mesh['req'=64,'rep'=4] {'rep'}, dimensions={0} | all-to-all | bytes 4915200 | tf_op jit(solution)/shard_map/all_to_all | solution.py:319
  133.5 3.7 %combine_holders.1 = bf16[2,3,192,128]{3,2,1,0:T(8,128)(2,1)} custom-call(f32[4,2,3,200,128]{4,3,2,1,0:T(8,128)} %all_to_all.15.part_ref), custom_call_target="tpu_custom_call" | custom-call | tf_op jit(solution)/shard_map/combine_holders/pallas_call | solution.py:217
  138.5 1.7 copy.86
  140.2 2.1 reshape.175
  142.4 1.7 multiply_reduce_fusion
  145.0 27.5 %all-gather.5.cloned.1.call-done = bf16[8,64,1152]{2,1,0:T(8,128)(2,1)} async-done(((bf16[2,64,1152]{2,1,0:T(8,128)(2,1)}), bf16[8,64,1152]{2,1,0:T(8,128)(2,1)}) %all-gather.5.cloned.1.call-update) | async-done | bytes 1179664 | tf_op jit(solution)/shard_map/all_gather | solution.py:328
  172.5 3.2 %fusion.58 = f32[512,384]{1,0:T(8,128)} fusion(bf16[512,1152]{1,0:T(8,128)(2,1)} %bitcast.83, bf16[1152,384]{1,0:T(8,128)(2,1)} %param.19), kind=kOutput, calls=%fused_computation.106 | convolution fusion | flops 452984832 | bytes 2850816 | tf_op jit(solution)/shard_map/dot_general | solution.py:329
  175.7 5.0 %fusion.9 = f32[512,1152]{1,0:T(8,128)} fusion(bf16[384,1152]{1,0:T(8,128)(2,1)} %param.21, bf16[512,1152]{1,0:T(8,128)(2,1)} %bitcast.84, bf16[1152,384]{1,0:T(8,128)(2,1)} %param.20, f32[512,384]{1,0:T(8,128)} %fusion.58), kind=kOutput, calls=%fused_computation.15 | convolution fusion | flops 907149312 | bytes 6094848 | tf_op jit(solution)/shard_map/dot_general | solution.py:333
  181.4 36.5 %reduce-scatter.2.cloned.1.call-done = f32[2,64,1152]{2,1,0:T(8,128)} async-done(((f32[8,64,1152]{2,1,0:T(8,128)}), f32[2,64,1152]{2,1,0:T(8,128)}) %reduce-scatter.2.cloned.1.call-update) | async-done | bytes 589840 | tf_op jit(solution)/shard_map/reduce_scatter | solution.py:332
  220.1 10.8 %all-to-all-start.2 = ((bf16[2,64,1152]{2,0,1:T(2,128)(2,1)}), bf16[2,64,1152]{2,0,1:T(2,128)(2,1)S(1)}, u32[]{:S(2)}, u32[]{:S(2)}) async-start(bf16[2,64,1152]{2,0,1:T(2,128)(2,1)} %copy.88), calls=%async_computation.3 | async-start | bytes 589824 | tf_op jit(solution)/shard_map/all_to_all | solution.py:343
  233.3 10.2 %all-to-all-done.2 = bf16[2,64,1152]{2,0,1:T(2,128)(2,1)S(1)} async-done(((bf16[2,64,1152]{2,0,1:T(2,128)(2,1)}), bf16[2,64,1152]{2,0,1:T(2,128)(2,1)S(1)}, u32[]{:S(2)}, u32[]{:S(2)}) %all-to-all-start.2) | async-done | bytes 294944 | tf_op jit(solution)/shard_map/all_to_all | solution.py:343
  (77 shorter events, 26.1 us)
Async XLA Ops:
  7.2 135.2 %copy-start = (bf16[1152,1152]{1,0:T(8,128)(2,1)S(1)}, bf16[1152,1152]{1,0:T(8,128)(2,1)}, u32[]{:S(2)}) copy-start(bf16[1152,1152]{1,0:T(8,128)(2,1)} %param.17) | copy-start | bytes 7962628
  9.3 26.9 %copy-start.9 = (s32[8,1,5]{0,1,2:T(1,128)S(1)}, s32[8,1,5]{0,1,2:T(1,128)}, u32[]{:S(2)}) copy-start(s32[8,1,5]{0,1,2:T(1,128)} %param.23) | copy-start | bytes 484
  9.3 25.9 %all-to-all-start = ((bf16[2,64,1152]{2,0,1:T(2,128)(2,1)}), bf16[2,64,1152]{2,0,1:T(2,128)(2,1)S(1)}, u32[]{:S(2)}, u32[]{:S(2)}) async-start(bf16[2,64,1152]{2,0,1:T(2,128)(2,1)} %copy.78), calls=%async_computation | async-start | bytes 589824 | tf_op jit(solution)/shard_map/all_to_all | solution.py:284
  22.6 35.1 %all-gather.3.cloned.1.call-start = ((), (), s32[]{:S(2)}) async-start(), calls=%async_computation.4 | async-start | bytes 1474560 | tf_op jit(solution)/shard_map/all_gather | solution.py:285
  24.3 14.2 %copy-start.10 = (s32[8]{0:T(128)S(1)}, s32[8]{0:T(128)}, u32[]{:S(2)}) copy-start(s32[8]{0:T(128)} %param.24) | copy-start | bytes 100
  36.0 136.5 %all-gather.5.cloned.1.call-start = ((), (), s32[]{:S(2)}) async-start(), calls=%async_computation.5 | async-start | bytes 1474560 | tf_op jit(solution)/shard_map/all_gather | solution.py:328
  39.0 4.8 %copy-start.5 = (f32[512,64]{0,1:T(8,128)}, f32[512,64]{0,1:T(8,128)S(1)}, u32[]{:S(2)}) copy-start(f32[512,64]{0,1:T(8,128)S(1)} %get-tuple-element.34) | copy-start | bytes 393220
  49.7 9.5 %copy-start.7 = (f32[1152]{0:T(1024)S(1)}, f32[1152]{0:T(1024)}, u32[]{:S(2)}) copy-start(f32[1152]{0:T(1024)} %param.15) | copy-start | bytes 13828
  67.1 1.9 copy-start.2
  67.2 2.6 %copy-start.1 = (f32[512,1152]{1,0:T(8,128)S(1)}, f32[512,1152]{1,0:T(8,128)}, u32[]{:S(2)}) copy-start(f32[512,1152]{1,0:T(8,128)} %copy.83) | copy-start | bytes 7077892
  69.8 2.0 copy-start.3
  133.5 8.8 %copy-start.4 = (bf16[2,64,1152]{2,1,0:T(8,128)(2,1)S(1)}, bf16[2,64,1152]{2,1,0:T(8,128)(2,1)}, u32[]{:S(2)}) copy-start(bf16[2,64,1152]{2,1,0:T(8,128)(2,1)} %copy.79) | copy-start | bytes 884740
  140.2 3.8 %copy-start.8 = (f32[1152]{0:T(1024)S(1)}, f32[1152]{0:T(1024)}, u32[]{:S(2)}) copy-start(f32[1152]{0:T(1024)} %param.18) | copy-start | bytes 13828
  144.9 73.0 %reduce-scatter.2.cloned.1.call-start = ((), (), s32[]{:S(2)}) async-start(), calls=%async_computation.6 | async-start | bytes 2949120 | tf_op jit(solution)/shard_map/reduce_scatter | solution.py:332
  180.7 0.7 copy-start.11
  180.7 50.2 %copy-start.6 = (f32[8,64,64]{2,1,0:T(8,128)S(1)}, f32[8,64,64]{2,1,0:T(8,128)}, u32[]{:S(2)}) copy-start(f32[8,64,64]{2,1,0:T(8,128)} %get-tuple-element.31) | copy-start | bytes 393220
  217.9 14.5 %copy-start.12 = (s32[8]{0:T(128)S(1)}, s32[8]{0:T(128)}, u32[]{:S(2)}) copy-start(s32[8]{0:T(128)} %param.27) | copy-start | bytes 100
  220.1 23.4 %all-to-all-start.2 = ((bf16[2,64,1152]{2,0,1:T(2,128)(2,1)}), bf16[2,64,1152]{2,0,1:T(2,128)(2,1)S(1)}, u32[]{:S(2)}, u32[]{:S(2)}) async-start(bf16[2,64,1152]{2,0,1:T(2,128)(2,1)} %copy.88), calls=%async_computation.3 | async-start | bytes 589824 | tf_op jit(solution)/shard_map/all_to_all | solution.py:343
Sparse Core Ops, SparseCore 0:
  36.1 21.4 all-gather.2
  145.0 27.4 all-gather.4
  180.8 37.0 reduce-scatter.1

commit v4 on v3

--- a/solution.py
+++ b/solution.py
@@ -181,6 +181,67 @@
     )(page_list, limits, queries, *([cache] * slots), draft_keys, draft_values, draft_mask)
 
 
+def exchange_kernel(count, same, x_ref, out_ref, local_sem, send_sems, recv_sems):
+    me = lax.axis_index("rep")
+    row = lax.axis_index("req")
+    mesh_ids = pl.DeviceIdType.MESH
+    barrier = pltpu.get_barrier_semaphore()
+    for step in range(1, count):
+        peer = lax.rem(me + step, count)
+        pl.semaphore_signal(barrier, inc=1, device_id=(row, peer), device_id_type=mesh_ids)
+    pl.semaphore_wait(barrier, count - 1)
+    own = x_ref.at[0] if same else x_ref.at[me]
+    local = pltpu.make_async_copy(own, out_ref.at[me], local_sem)
+    local.start()
+    sends = []
+    for step in range(1, count):
+        peer = lax.rem(me + step, count)
+        source = x_ref.at[0] if same else x_ref.at[peer]
+        copy = pltpu.make_async_remote_copy(
+            src_ref=source,
+            dst_ref=out_ref.at[me],
+            send_sem=send_sems.at[step],
+            recv_sem=recv_sems.at[step],
+            device_id=(row, peer),
+            device_id_type=mesh_ids,
+        )
+        copy.start()
+        sends.append(copy)
+    local.wait()
+    for copy in sends:
+        copy.wait_send()
+    for step in range(1, count):
+        origin = lax.rem(me + count - step, count)
+        incoming = pltpu.make_async_remote_copy(
+            src_ref=x_ref.at[0],
+            dst_ref=out_ref.at[origin],
+            send_sem=send_sems.at[step],
+            recv_sem=recv_sems.at[step],
+            device_id=(row, origin),
+            device_id_type=mesh_ids,
+        )
+        incoming.wait_recv()
+
+
+def exchange(blocks, count, same, collective_id):
+    out_shape = jax.ShapeDtypeStruct((count,) + blocks.shape[1:], blocks.dtype)
+    moved = blocks[0].size * blocks.dtype.itemsize * (count - 1)
+    return pl.pallas_call(
+        functools.partial(exchange_kernel, count, same),
+        in_specs=[pl.BlockSpec(memory_space=pl.ANY)],
+        out_specs=pl.BlockSpec(memory_space=pl.ANY),
+        out_shape=out_shape,
+        scratch_shapes=[
+            pltpu.SemaphoreType.DMA(()),
+            pltpu.SemaphoreType.DMA((count,)),
+            pltpu.SemaphoreType.DMA((count,)),
+        ],
+        compiler_params=pltpu.CompilerParams(collective_id=collective_id, has_side_effects=True),
+        cost_estimate=pl.CostEstimate(flops=0, bytes_accessed=2 * moved, transcendentals=0),
+        name=f"exchange_{collective_id}",
+    )(blocks)
+
+
 def combine_kernel(part_ref, out_ref):
     holders, chunks = part_ref.shape[0], part_ref.shape[2]
     half = out_ref.shape[2]
@@ -316,7 +377,7 @@
         queries, cache, page_list, limits, keys_all, values_all, draft_mask
     )
     parts = parts.reshape((rep_count, owner_page_count) + parts.shape[1:])
-    gathered = lax.all_to_all(parts, "rep", split_axis=0, concat_axis=0, tiled=True)
+    gathered = exchange(parts, rep_count, False, 1)
     attended = finish_attention(combine(gathered), owner_page_count, tree_length)
 
     mixed = jnp.dot(attended, w_out, preferred_element_type=jnp.float32)
@@ -325,21 +386,18 @@
     )
     residual_wide = residual.astype(jnp.float32)
     ffn_in = rms_scaled(residual_wide, ffn_gain).reshape(owner_page_count, tree_length, model_width)
-    rows_in = lax.all_gather(ffn_in, "rep", axis=0, tiled=True).reshape(-1, model_width)
+    rows_in = exchange(ffn_in[None], rep_count, True, 2).reshape(-1, model_width)
     gate = jnp.dot(rows_in, w_gate, preferred_element_type=jnp.float32)
     up = jnp.dot(rows_in, w_up, preferred_element_type=jnp.float32)
     activated = (jax.nn.silu(gate) * up).astype(jnp.bfloat16)
-    ffn_sum = lax.psum_scatter(
-        jnp.dot(activated, w_down, preferred_element_type=jnp.float32).reshape(
-            requests, tree_length, model_width
-        ),
-        "rep",
-        scatter_dimension=0,
-        tiled=True,
-    )
-    out_own = (ffn_sum + residual_wide.reshape(owner_page_count, tree_length, model_width)).astype(
-        jnp.bfloat16
-    )
+    down = jnp.dot(activated, w_down, preferred_element_type=jnp.float32).reshape(
+        rep_count, owner_page_count, tree_length, model_width
+    )
+    ffn_terms = exchange(down, rep_count, False, 3)
+    out_own = (
+        jnp.sum(ffn_terms, axis=0)
+        + residual_wide.reshape(owner_page_count, tree_length, model_width)
+    ).astype(jnp.bfloat16)
     out = lax.all_to_all(out_own, "req", split_axis=1, concat_axis=1, tiled=True)
     out = out.reshape(block_rows, draft_part, model_width)
 

time: 252 us -> 235 us (0.933)
  Pallas kernels: 32.4 us -> 108 us
  waiting for transfers between devices: 85.6 us -> 21.6 us
  blocking collectives: 31.8 us -> 0 us
  other arithmetic: 9.81 us -> 12.5 us
    pallas_call x0 -> x3, Pallas kernels: none -> 76 us  [exchange(): pl.pallas_call(functools.partial(exchange_kernel, count, same), in_specs=...]
    reduce_scatter x1 -> x0, waiting for transfers between devices: 36.5 us -> none  [body(): lax.psum_scatter(jnp.dot(activated, w_down, preferred_element_type=jnp.fl...]
    all_to_all x1 -> x0, blocking collectives: 31.8 us -> none  [body(): lax.all_to_all(parts, 'rep', split_axis=0, concat_axis=0, tiled=True)]
    all_gather x1 -> x0, waiting for transfers between devices: 27.5 us -> none  [body(): lax.all_gather(ffn_in, 'rep', axis=0, tiled=True).reshape(-1, model_width)]
    reduce_sum x0 -> x1, other arithmetic: none -> 2.71 us  [body(): jnp.sum(ffn_terms, axis=0)]
  transfers between devices with their start and end apart: 5 -> 3, of which waited for: 5 -> 3; matrix products, arithmetic and copies ran while one was open for 10% -> 11% of each run, Pallas kernels for 0% -> 0%
where the time goes in v4:
time: 235 us; the launch traced here: 234 us
  Pallas kernels  108 us (46%)
  local copies, waits for them, and re-layouts  31 us (13%)
  starting transfers between devices  25 us (11%)
  waiting for transfers between devices  21.6 us (9%)
  matrix products  21.2 us (9%)
  between operations  14.4 us (6%)
  other arithmetic  12.5 us (5%)
    pallas_call x3, Pallas kernels, exchange(): pl.pallas_call(functools.partial(exchange_kernel, count, same), in_specs=...  76 us
    pallas_call x1, Pallas kernels, paged_partials(): pl.pallas_call(functools.partial(paged_kernel, slots, chunks), grid_spec=...  28.7 us
    all_to_all x1, starting transfers between devices, body(): lax.all_to_all(local_rows, 'req', split_axis=1, concat_axis=1, tiled=True)  13.1 us
    all_to_all x1, starting transfers between devices, body(): lax.all_to_all(out_own, 'req', split_axis=1, concat_axis=1, tiled=True)  11.8 us
    all_to_all x1, waiting for transfers between devices, body(): lax.all_to_all(out_own, 'req', split_axis=1, concat_axis=1, tiled=True)  10.2 us
    all_to_all x1, waiting for transfers between devices, body(): lax.all_to_all(local_rows, 'req', split_axis=1, concat_axis=1, tiled=True)  9.29 us
    another operation x4, local copies, waits for them, and re-layouts, rotate_flat(): cosine = jnp.tile(jnp.concatenate([cosine, cosine], axis=-1), (1, repeats))  9.11 us
    another operation x4, local copies, waits for them, and re-layouts, rotate_flat(): sines = jnp.tile(jnp.concatenate([-sines, sines], axis=-1), (1, repeats))  7.2 us
  transfers between devices with their start and end apart: 3, of which 3 were waited for; matrix products, arithmetic and copies ran while one was open for 11% of the time, Pallas kernels for 0%

profile of v4, /device:TPU:1, one launch (start us, length us, event | category | flops | bytes accessed | tf_op | source)
XLA Modules:
  0.0 234.1 jit_solution(2156920424385793442)
XLA Ops:
  7.2 2.1 copy.76
  9.3 13.1 %all-to-all-start = ((bf16[2,64,1152]{2,0,1:T(2,128)(2,1)}), bf16[2,64,1152]{2,0,1:T(2,128)(2,1)S(1)}, u32[]{:S(2)}, u32[]{:S(2)}) async-start(bf16[2,64,1152]{2,0,1:T(2,128)(2,1)} %copy.76), calls=%async_computation | async-start | bytes 589824 | tf_op jit(solution)/shard_map/all_to_all | solution.py:345
  25.8 9.3 %all-to-all-done = bf16[2,64,1152]{2,0,1:T(2,128)(2,1)S(1)} async-done(((bf16[2,64,1152]{2,0,1:T(2,128)(2,1)}), bf16[2,64,1152]{2,0,1:T(2,128)(2,1)S(1)}, u32[]{:S(2)}, u32[]{:S(2)}) %all-to-all-start) | async-done | bytes 294944 | tf_op jit(solution)/shard_map/all_to_all | solution.py:345
  38.3 1.7 tile.18
  40.0 3.1 %copy.81 = f32[512,1152]{1,0:T(8,128)} copy(f32[512,1152]{0,1:T(8,128)} %bitcast.65) | data formatting | bytes 4718592 | tf_op jit(solution)/shard_map/tile | solution.py:305
  43.1 1.7 tile.16
  44.8 3.1 %copy.80 = f32[512,1152]{1,0:T(8,128)} copy(f32[512,1152]{0,1:T(8,128)} %bitcast.66) | data formatting | bytes 4718592 | tf_op jit(solution)/shard_map/tile | solution.py:304
  50.4 1.9 tile.40
  52.3 2.3 copy.82
  55.4 2.1 all-gather.2.cloned.1.call-done
  60.7 5.1 %convolution_convert_fusion = bf16[512,1920]{1,0:T(8,128)(2,1)S(1)} fusion(bf16[512,1152]{1,0:T(8,128)(2,1)S(1)} %bitcast.77, bf16[1152,1920]{1,0:T(8,128)(2,1)} %param.16), kind=kOutput, calls=%fused_computation | convolution fusion | flops 2265907200 | bytes 7569408 | tf_op jit(solution)/shard_map/dot_general | solution.py:349
  69.6 2.1 fusion.7
  72.9 28.7 %paged_partials.1 = f32[8,3,200,128]{3,2,1,0:T(8,128)} custom-call(s32[8,5]{1,0:T(8,128)} %bitcast.83, s32[8,5]{1,0:T(8,128)} %broadcast_subtract_fusion.limit_ref, bf16[8,64,1152]{2,1,0:T(8,128)(2,1)} %bitcast.69, bf16[16,2,128,384]{3,2,1,0:T(8,128)(2,1)} %refs_5_.1, bf16[16,2,128,384]{3,2,1,0:T(8,128)(2,1)} %refs_5_.1, bf16[16,2,128,384]{3,2,1,0:T(8,128)(2,1)} %refs_5_.1, ...), custom_call_target="tpu_custom_call" | custom-call | flops 3321888768 | bytes 11403264 | tf_op jit(solution)/shard_map/paged_partials/pallas_call | solution.py:174
  101.6 29.3 %exchange_1.1.part_ref = f32[4,2,3,200,128]{4,3,2,1,0:T(8,128)} custom-call(f32[4,2,3,200,128]{4,3,2,1,0:T(8,128)} %bitcast.64), custom_call_target="tpu_custom_call" | custom-call | bytes 3686400 | tf_op jit(solution)/shard_map/exchange_1/pallas_call | solution.py:229
  130.9 3.7 %combine_holders.1 = bf16[2,3,192,128]{3,2,1,0:T(8,128)(2,1)} custom-call(f32[4,2,3,200,128]{4,3,2,1,0:T(8,128)} %exchange_1.1.part_ref), custom_call_target="tpu_custom_call" | custom-call | tf_op jit(solution)/shard_map/combine_holders/pallas_call | solution.py:278
  135.9 1.7 copy.84
  137.7 2.1 reshape.172
  142.3 17.3 %exchange_2.1 = bf16[4,2,64,1152]{3,2,1,0:T(8,128)(2,1)} custom-call(bf16[1,2,64,1152]{3,2,1,0:T(8,128)(2,1)} %bitcast.80), custom_call_target="tpu_custom_call" | custom-call | bytes 1769472 | tf_op jit(solution)/shard_map/exchange_2/pallas_call | solution.py:229
  159.6 3.2 %fusion.58 = f32[512,384]{1,0:T(8,128)} fusion(bf16[512,1152]{1,0:T(8,128)(2,1)} %bitcast.78, bf16[1152,384]{1,0:T(8,128)(2,1)} %param.19), kind=kOutput, calls=%fused_computation.106 | convolution fusion | flops 452984832 | bytes 2850816 | tf_op jit(solution)/shard_map/dot_general | solution.py:390
  162.8 5.0 %fusion.9 = f32[512,1152]{1,0:T(8,128)} fusion(bf16[384,1152]{1,0:T(8,128)(2,1)} %param.21, bf16[512,1152]{1,0:T(8,128)(2,1)} %bitcast.79, bf16[1152,384]{1,0:T(8,128)(2,1)} %param.20, f32[512,384]{1,0:T(8,128)} %fusion.58), kind=kOutput, calls=%fused_computation.15 | convolution fusion | flops 907149312 | bytes 6094848 | tf_op jit(solution)/shard_map/dot_general | solution.py:393
  167.8 29.4 %exchange_3.1 = f32[4,2,64,1152]{3,2,1,0:T(8,128)} custom-call(f32[4,2,64,1152]{3,2,1,0:T(8,128)} %bitcast.73), custom_call_target="tpu_custom_call" | custom-call | bytes 3538944 | tf_op jit(solution)/shard_map/exchange_3/pallas_call | solution.py:229
  197.2 2.7 %reduce_sum.39 = f32[2,64,1152]{2,1,0:T(8,128)} reduce(f32[4,2,64,1152]{3,2,1,0:T(8,128)} %exchange_3.1, f32[]{:T(128)} %constant.61.clone.1), dimensions={0}, to_apply=%region_3.4 | reduce | flops 442368 | bytes 2949124 | tf_op jit(solution)/shard_map/reduce_sum | solution.py:398
  202.1 11.8 %all-to-all-start.1 = ((bf16[2,64,1152]{2,0,1:T(2,128)(2,1)}), bf16[2,64,1152]{2,0,1:T(2,128)(2,1)S(1)}, u32[]{:S(2)}, u32[]{:S(2)}) async-start(bf16[2,64,1152]{2,0,1:T(2,128)(2,1)} %copy.86), calls=%async_computation.1 | async-start | bytes 589824 | tf_op jit(solution)/shard_map/all_to_all | solution.py:401
  216.3 10.2 %all-to-all-done.1 = bf16[2,64,1152]{2,0,1:T(2,128)(2,1)S(1)} async-done(((bf16[2,64,1152]{2,0,1:T(2,128)(2,1)}), bf16[2,64,1152]{2,0,1:T(2,128)(2,1)S(1)}, u32[]{:S(2)}, u32[]{:S(2)}) %all-to-all-start.1) | async-done | bytes 294944 | tf_op jit(solution)/shard_map/all_to_all | solution.py:401
  (74 shorter events, 26.8 us)
Async XLA Ops:
  7.2 132.6 %copy-start = (bf16[1152,1152]{1,0:T(8,128)(2,1)S(1)}, bf16[1152,1152]{1,0:T(8,128)(2,1)}, u32[]{:S(2)}) copy-start(bf16[1152,1152]{1,0:T(8,128)(2,1)} %param.17) | copy-start | bytes 7962628
  9.3 25.8 %all-to-all-start = ((bf16[2,64,1152]{2,0,1:T(2,128)(2,1)}), bf16[2,64,1152]{2,0,1:T(2,128)(2,1)S(1)}, u32[]{:S(2)}, u32[]{:S(2)}) async-start(bf16[2,64,1152]{2,0,1:T(2,128)(2,1)} %copy.76), calls=%async_computation | async-start | bytes 589824 | tf_op jit(solution)/shard_map/all_to_all | solution.py:345
  22.5 35.1 %all-gather.2.cloned.1.call-start = ((), (), s32[]{:S(2)}) async-start(), calls=%async_computation.2 | async-start | bytes 1474560 | tf_op jit(solution)/shard_map/all_gather | solution.py:346
  23.8 12.1 %copy-start.9 = (s32[8,1,5]{0,1,2:T(1,128)S(1)}, s32[8,1,5]{0,1,2:T(1,128)}, u32[]{:S(2)}) copy-start(s32[8,1,5]{0,1,2:T(1,128)} %param.23) | copy-start | bytes 484
  24.2 13.6 %copy-start.10 = (s32[8]{0:T(128)S(1)}, s32[8]{0:T(128)}, u32[]{:S(2)}) copy-start(s32[8]{0:T(128)} %param.24) | copy-start | bytes 100
  38.3 4.8 %copy-start.5 = (f32[512,64]{0,1:T(8,128)}, f32[512,64]{0,1:T(8,128)S(1)}, u32[]{:S(2)}) copy-start(f32[512,64]{0,1:T(8,128)S(1)} %get-tuple-element.34) | copy-start | bytes 393220
  48.0 6.7 %copy-start.11 = (s32[8]{0:T(128)S(1)}, s32[8]{0:T(128)}, u32[]{:S(2)}) copy-start(s32[8]{0:T(128)} %param.26) | copy-start | bytes 100
  49.0 10.1 %copy-start.7 = (f32[1152]{0:T(1024)S(1)}, f32[1152]{0:T(1024)}, u32[]{:S(2)}) copy-start(f32[1152]{0:T(1024)} %param.15) | copy-start | bytes 13828
  67.0 1.9 copy-start.2
  67.1 2.6 %copy-start.1 = (f32[512,1152]{1,0:T(8,128)S(1)}, f32[512,1152]{1,0:T(8,128)}, u32[]{:S(2)}) copy-start(f32[512,1152]{1,0:T(8,128)} %copy.81) | copy-start | bytes 7077892
  69.6 2.1 copy-start.3
  130.9 8.8 %copy-start.4 = (bf16[2,64,1152]{2,1,0:T(8,128)(2,1)S(1)}, bf16[2,64,1152]{2,1,0:T(8,128)(2,1)}, u32[]{:S(2)}) copy-start(bf16[2,64,1152]{2,1,0:T(8,128)(2,1)} %copy.77) | copy-start | bytes 884740
  137.7 3.8 %copy-start.8 = (f32[1152]{0:T(1024)S(1)}, f32[1152]{0:T(1024)}, u32[]{:S(2)}) copy-start(f32[1152]{0:T(1024)} %param.18) | copy-start | bytes 13828
  197.2 16.7 %copy-start.6 = (f32[8,64,64]{2,1,0:T(8,128)S(1)}, f32[8,64,64]{2,1,0:T(8,128)}, u32[]{:S(2)}) copy-start(f32[8,64,64]{2,1,0:T(8,128)} %get-tuple-element.31) | copy-start | bytes 393220
  200.0 15.5 %copy-start.12 = (s32[8]{0:T(128)S(1)}, s32[8]{0:T(128)}, u32[]{:S(2)}) copy-start(s32[8]{0:T(128)} %param.27) | copy-start | bytes 100
  202.1 24.4 %all-to-all-start.1 = ((bf16[2,64,1152]{2,0,1:T(2,128)(2,1)}), bf16[2,64,1152]{2,0,1:T(2,128)(2,1)S(1)}, u32[]{:S(2)}, u32[]{:S(2)}) async-start(bf16[2,64,1152]{2,0,1:T(2,128)(2,1)} %copy.86), calls=%async_computation.1 | async-start | bytes 589824 | tf_op jit(solution)/shard_map/all_to_all | solution.py:401
Sparse Core Ops, SparseCore 0:
  36.0 21.4 all-gather.1

commit v5 on v4

--- a/solution.py
+++ b/solution.py
@@ -114,6 +114,9 @@
         peak = jnp.max(sd, axis=-1, keepdims=True)
         for sc in parts:
             peak = jnp.maximum(peak, jnp.max(sc, axis=-1, keepdims=True))
+        peak_hi = peak.astype(jnp.bfloat16).astype(jnp.float32)
+        peak_lo = (peak - peak_hi).astype(jnp.bfloat16).astype(jnp.float32)
+        peak = peak_hi + peak_lo
         wd = jnp.exp(sd - peak)
         total = jnp.sum(wd, axis=-1, keepdims=True)
         acc = jnp.dot(
@@ -127,12 +130,16 @@
                 page_refs[s][0, 1, :, lanes],
                 preferred_element_type=jnp.float32,
             )
-        part_ref[0, c, 0:half, :] = jnp.where(low_h, acc[:half], acc[half:])
-        stats = jnp.where(stat_lanes == 0, total, jnp.where(stat_lanes == 1, peak, 0.0))
+        part_ref[0, c, 0:half, :] = jnp.where(low_h, acc[:half], acc[half:]).astype(part_ref.dtype)
+        stats = jnp.where(
+            stat_lanes == 0,
+            total,
+            jnp.where(stat_lanes == 1, peak_hi, jnp.where(stat_lanes == 2, peak_lo, 0.0)),
+        )
         flipped = jnp.transpose(stats)
-        pieces = [flipped[j : j + 1, 128 * p : 128 * (p + 1)] for j in range(2) for p in range(3)]
-        pieces.append(jnp.zeros((2, 128), jnp.float32))
-        part_ref[0, c, half : half + 8, :] = jnp.concatenate(pieces, axis=0)
+        pieces = [flipped[j : j + 1, 128 * p : 128 * (p + 1)] for j in range(3) for p in range(3)]
+        pieces.append(jnp.zeros((7, 128), jnp.float32))
+        part_ref[0, c, half : half + 16, :] = jnp.concatenate(pieces, axis=0).astype(part_ref.dtype)
 
 
 def paged_partials(queries, cache, page_list, limits, draft_keys, draft_values, draft_mask):
@@ -154,10 +161,10 @@
         pl.BlockSpec((1, tree_length, tree_length), lambda k, pages, limit: (k, 0, 0)),
     ]
     out_specs = [
-        pl.BlockSpec((1, chunks, rows // 2 + 8, 128), lambda k, pages, limit: (k, 0, 0, 0)),
+        pl.BlockSpec((1, chunks, rows // 2 + 16, 128), lambda k, pages, limit: (k, 0, 0, 0)),
     ]
     out_shape = [
-        jax.ShapeDtypeStruct((requests, chunks, rows // 2 + 8, 128), jnp.float32),
+        jax.ShapeDtypeStruct((requests, chunks, rows // 2 + 16, 128), jnp.bfloat16),
     ]
     keys_seen = slots * page_length + tree_length
     cost = pl.CostEstimate(
@@ -254,10 +261,13 @@
         return jnp.where(low_h, column[:half], column[half:])
 
     for c in range(chunks):
-        tails = [part_ref[h, 0, c, half : half + 8, :] for h in range(holders)]
+        tails = [
+            part_ref[h, 0, c, half : half + 16, :].astype(jnp.float32) for h in range(holders)
+        ]
         totals = [jnp.concatenate([t[p : p + 1] for p in range(pieces)], axis=1) for t in tails]
         peaks = [
             jnp.concatenate([t[pieces + p : pieces + p + 1] for p in range(pieces)], axis=1)
+            + jnp.concatenate([t[2 * pieces + p : 2 * pieces + p + 1] for p in range(pieces)], axis=1)
             for t in tails
         ]
         top = peaks[0]
@@ -268,13 +278,13 @@
         for h in range(holders):
             factor = jnp.exp(peaks[h] - top)
             total = total + totals[h] * factor
-            acc = acc + part_ref[h, 0, c, 0:half, :] * as_column(factor)
+            acc = acc + part_ref[h, 0, c, 0:half, :].astype(jnp.float32) * as_column(factor)
         out_ref[0, c] = (acc / as_column(total)).astype(out_ref.dtype)
 
 
 def combine(parts):
     holders, requests, chunks, rows_in, lanes = parts.shape
-    half = rows_in - 8
+    half = rows_in - 16
     return pl.pallas_call(
         combine_kernel,
         grid=(requests,),
@@ -393,9 +403,9 @@
     down = jnp.dot(activated, w_down, preferred_element_type=jnp.float32).reshape(
         rep_count, owner_page_count, tree_length, model_width
     )
-    ffn_terms = exchange(down, rep_count, False, 3)
+    ffn_terms = exchange(down.astype(jnp.bfloat16), rep_count, False, 3)
     out_own = (
-        jnp.sum(ffn_terms, axis=0)
+        jnp.sum(ffn_terms.astype(jnp.float32), axis=0)
         + residual_wide.reshape(owner_page_count, tree_length, model_width)
     ).astype(jnp.bfloat16)
     out = lax.all_to_all(out_own, "req", split_axis=1, concat_axis=1, tiled=True)

time: 235 us -> 207 us (0.88)
  Pallas kernels: 108 us -> 83.1 us
    pallas_call x3, Pallas kernels: 76 us -> 50.7 us  [exchange(): pl.pallas_call(functools.partial(exchange_kernel, count, same), in_specs=...]
  transfers between devices with their start and end apart: 3 -> 3, of which waited for: 3 -> 3; matrix products, arithmetic and copies ran while one was open for 11% -> 12% of each run, Pallas kernels for 0% -> 0%
where the time goes in v5:
time: 207 us; the launch traced here: 206 us
  Pallas kernels  83.1 us (40%)
  local copies, waits for them, and re-layouts  31 us (15%)
  starting transfers between devices  25 us (12%)
  waiting for transfers between devices  21.6 us (10%)
  matrix products  20.8 us (10%)
  between operations  14.4 us (7%)
  other arithmetic  10.3 us (5%)
    pallas_call x3, Pallas kernels, exchange(): pl.pallas_call(functools.partial(exchange_kernel, count, same), in_specs=...  50.7 us
    pallas_call x1, Pallas kernels, paged_partials(): pl.pallas_call(functools.partial(paged_kernel, slots, chunks), grid_spec=...  28.8 us
    all_to_all x1, starting transfers between devices, body(): lax.all_to_all(local_rows, 'req', split_axis=1, concat_axis=1, tiled=True)  13.1 us
    all_to_all x1, starting transfers between devices, body(): lax.all_to_all(out_own, 'req', split_axis=1, concat_axis=1, tiled=True)  11.8 us
    all_to_all x1, waiting for transfers between devices, body(): lax.all_to_all(out_own, 'req', split_axis=1, concat_axis=1, tiled=True)  10.2 us
    all_to_all x1, waiting for transfers between devices, body(): lax.all_to_all(local_rows, 'req', split_axis=1, concat_axis=1, tiled=True)  9.29 us
    another operation x4, local copies, waits for them, and re-layouts, rotate_flat(): cosine = jnp.tile(jnp.concatenate([cosine, cosine], axis=-1), (1, repeats))  9.11 us
    another operation x4, local copies, waits for them, and re-layouts, rotate_flat(): sines = jnp.tile(jnp.concatenate([-sines, sines], axis=-1), (1, repeats))  7.2 us
  transfers between devices with their start and end apart: 3, of which 3 were waited for; matrix products, arithmetic and copies ran while one was open for 12% of the time, Pallas kernels for 0%

profile of v5, /device:TPU:1, one launch (start us, length us, event | category | flops | bytes accessed | tf_op | source)
XLA Modules:
  0.0 206.2 jit_solution(6526717551016344622)
XLA Ops:
  7.2 2.1 %copy.76 = bf16[2,64,1152]{2,0,1:T(2,128)(2,1)} copy(bf16[2,64,1152]{2,1,0:T(8,128)(2,1)} %bitcast.81) | data formatting | bytes 589824 | tf_op jit(solution)/shard_map/reshape | solution.py:354
  9.3 13.1 %all-to-all-start = ((bf16[2,64,1152]{2,0,1:T(2,128)(2,1)}), bf16[2,64,1152]{2,0,1:T(2,128)(2,1)S(1)}, u32[]{:S(2)}, u32[]{:S(2)}) async-start(bf16[2,64,1152]{2,0,1:T(2,128)(2,1)} %copy.76), calls=%async_computation | async-start | bytes 589824 | tf_op jit(solution)/shard_map/all_to_all | solution.py:355
  25.8 9.3 %all-to-all-done = bf16[2,64,1152]{2,0,1:T(2,128)(2,1)S(1)} async-done(((bf16[2,64,1152]{2,0,1:T(2,128)(2,1)}), bf16[2,64,1152]{2,0,1:T(2,128)(2,1)S(1)}, u32[]{:S(2)}, u32[]{:S(2)}) %all-to-all-start) | async-done | bytes 294944 | tf_op jit(solution)/shard_map/all_to_all | solution.py:355
  38.3 1.7 tile.18
  40.0 3.1 %copy.81 = f32[512,1152]{1,0:T(8,128)} copy(f32[512,1152]{0,1:T(8,128)} %bitcast.64) | data formatting | bytes 4718592 | tf_op jit(solution)/shard_map/tile | solution.py:315
  43.1 1.7 tile.16
  44.8 3.1 %copy.80 = f32[512,1152]{1,0:T(8,128)} copy(f32[512,1152]{0,1:T(8,128)} %bitcast.65) | data formatting | bytes 4718592 | tf_op jit(solution)/shard_map/tile | solution.py:314
  50.4 1.9 tile.40
  52.3 2.3 %copy.82 = f32[512,384]{1,0:T(8,128)} copy(f32[512,384]{0,1:T(8,128)} %bitcast.71) | data formatting | bytes 1572864 | tf_op jit(solution)/shard_map/tile | solution.py:314
  55.4 2.1 %all-gather.2.cloned.1.call-done = bf16[8,64,1152]{2,1,0:T(8,128)(2,1)} async-done(((bf16[2,64,1152]{2,1,0:T(8,128)(2,1)}), bf16[8,64,1152]{2,1,0:T(8,128)(2,1)}) %all-gather.2.cloned.1.call-update) | async-done | bytes 1179664 | tf_op jit(solution)/shard_map/all_gather | solution.py:356
  60.7 5.1 %convolution_convert_fusion.1 = bf16[512,1920]{1,0:T(8,128)(2,1)S(1)} fusion(bf16[512,1152]{1,0:T(8,128)(2,1)S(1)} %bitcast.76, bf16[1152,1920]{1,0:T(8,128)(2,1)} %param.16), kind=kOutput, calls=%fused_computation.1 | convolution fusion | flops 2265907200 | bytes 7569408 | tf_op jit(solution)/shard_map/dot_general | solution.py:359
  69.6 2.1 fusion.7
  72.9 28.8 %paged_partials.1 = bf16[8,3,208,128]{3,2,1,0:T(8,128)(2,1)} custom-call(s32[8,5]{1,0:T(8,128)} %bitcast.83, s32[8,5]{1,0:T(8,128)} %broadcast_subtract_fusion.limit_ref, bf16[8,64,1152]{2,1,0:T(8,128)(2,1)} %bitcast.69, bf16[16,2,128,384]{3,2,1,0:T(8,128)(2,1)} %refs_5_.1, bf16[16,2,128,384]{3,2,1,0:T(8,128)(2,1)} %refs_5_.1, ...), custom_call_target="tpu_custom_call" | custom-call | flops 3321888768 | bytes 11403264 | tf_op jit(solution)/shard_map/paged_partials/pallas_call | solution.py:181
  101.7 16.7 %exchange_1.1.part_ref = bf16[4,2,3,208,128]{4,3,2,1,0:T(8,128)(2,1)} custom-call(bf16[4,2,3,208,128]{4,3,2,1,0:T(8,128)(2,1)} %bitcast.68), custom_call_target="tpu_custom_call" | custom-call | bytes 1916928 | tf_op jit(solution)/shard_map/exchange_1/pallas_call | solution.py:236
  118.4 3.6 %combine_holders.1 = bf16[2,3,192,128]{3,2,1,0:T(8,128)(2,1)} custom-call(bf16[4,2,3,208,128]{4,3,2,1,0:T(8,128)(2,1)} %exchange_1.1.part_ref), custom_call_target="tpu_custom_call" | custom-call | tf_op jit(solution)/shard_map/combine_holders/pallas_call | solution.py:288
  123.2 1.7 copy.84
  124.9 2.1 %reshape.171 = bf16[128,1152]{0,1:T(8,128)(2,1)} reshape(bf16[2,64,3,2,3,64]{1,0,5,4,3,2:T(2,128)(2,1)} %bitcast.73) | data formatting | bytes 589824 | tf_op jit(solution)/shard_map/reshape | solution.py:304
  127.1 1.7 multiply_reduce_fusion
  129.6 17.3 %exchange_2.1 = bf16[4,2,64,1152]{3,2,1,0:T(8,128)(2,1)} custom-call(bf16[1,2,64,1152]{3,2,1,0:T(8,128)(2,1)} %bitcast.80), custom_call_target="tpu_custom_call" | custom-call | bytes 1769472 | tf_op jit(solution)/shard_map/exchange_2/pallas_call | solution.py:236
  146.9 3.2 %fusion.57 = f32[512,384]{1,0:T(8,128)} fusion(bf16[512,1152]{1,0:T(8,128)(2,1)} %bitcast.77, bf16[1152,384]{1,0:T(8,128)(2,1)} %param.19), kind=kOutput, calls=%fused_computation.107 | convolution fusion | flops 452984832 | bytes 2850816 | tf_op jit(solution)/shard_map/dot_general | solution.py:400
  150.1 4.6 %convolution_convert_fusion = bf16[512,1152]{1,0:T(8,128)(2,1)} fusion(bf16[384,1152]{1,0:T(8,128)(2,1)} %param.21, bf16[512,1152]{1,0:T(8,128)(2,1)} %bitcast.78, bf16[1152,384]{1,0:T(8,128)(2,1)} %param.20, f32[512,384]{1,0:T(8,128)} %fusion.57), kind=kOutput, calls=%fused_computation | convolution fusion | flops 907739136 | bytes 4915200 | tf_op jit(solution)/shard_map/dot_general | solution.py:403
  154.7 16.8 %exchange_3.1 = bf16[4,2,64,1152]{3,2,1,0:T(8,128)(2,1)} custom-call(bf16[4,2,64,1152]{3,2,1,0:T(8,128)(2,1)} %bitcast.79), custom_call_target="tpu_custom_call" | custom-call | bytes 1769472 | tf_op jit(solution)/shard_map/exchange_3/pallas_call | solution.py:236
  174.2 11.8 %all-to-all-start.1 = ((bf16[2,64,1152]{2,0,1:T(2,128)(2,1)}), bf16[2,64,1152]{2,0,1:T(2,128)(2,1)S(1)}, u32[]{:S(2)}, u32[]{:S(2)}) async-start(bf16[2,64,1152]{2,0,1:T(2,128)(2,1)} %copy.86), calls=%async_computation.1 | async-start | bytes 589824 | tf_op jit(solution)/shard_map/all_to_all | solution.py:411
  188.4 10.2 %all-to-all-done.1 = bf16[2,64,1152]{2,0,1:T(2,128)(2,1)S(1)} async-done(((bf16[2,64,1152]{2,0,1:T(2,128)(2,1)}), bf16[2,64,1152]{2,0,1:T(2,128)(2,1)S(1)}, u32[]{:S(2)}, u32[]{:S(2)}) %all-to-all-start.1) | async-done | bytes 294944 | tf_op jit(solution)/shard_map/all_to_all | solution.py:411
  (74 shorter events, 25.6 us)
Async XLA Ops:
  7.2 119.9 %copy-start = (bf16[1152,1152]{1,0:T(8,128)(2,1)S(1)}, bf16[1152,1152]{1,0:T(8,128)(2,1)}, u32[]{:S(2)}) copy-start(bf16[1152,1152]{1,0:T(8,128)(2,1)} %param.17) | copy-start | bytes 7962628
  9.3 25.8 %all-to-all-start = ((bf16[2,64,1152]{2,0,1:T(2,128)(2,1)}), bf16[2,64,1152]{2,0,1:T(2,128)(2,1)S(1)}, u32[]{:S(2)}, u32[]{:S(2)}) async-start(bf16[2,64,1152]{2,0,1:T(2,128)(2,1)} %copy.76), calls=%async_computation | async-start | bytes 589824 | tf_op jit(solution)/shard_map/all_to_all | solution.py:355
  22.5 35.1 %all-gather.2.cloned.1.call-start = ((), (), s32[]{:S(2)}) async-start(), calls=%async_computation.2 | async-start | bytes 1474560 | tf_op jit(solution)/shard_map/all_gather | solution.py:356
  23.8 12.1 %copy-start.9 = (s32[8,1,5]{0,1,2:T(1,128)S(1)}, s32[8,1,5]{0,1,2:T(1,128)}, u32[]{:S(2)}) copy-start(s32[8,1,5]{0,1,2:T(1,128)} %param.23) | copy-start | bytes 484
  24.2 13.6 %copy-start.10 = (s32[8]{0:T(128)S(1)}, s32[8]{0:T(128)}, u32[]{:S(2)}) copy-start(s32[8]{0:T(128)} %param.24) | copy-start | bytes 100
  38.3 4.8 %copy-start.5 = (f32[512,64]{0,1:T(8,128)}, f32[512,64]{0,1:T(8,128)S(1)}, u32[]{:S(2)}) copy-start(f32[512,64]{0,1:T(8,128)S(1)} %get-tuple-element.34) | copy-start | bytes 393220
  48.0 6.7 %copy-start.11 = (s32[8]{0:T(128)S(1)}, s32[8]{0:T(128)}, u32[]{:S(2)}) copy-start(s32[8]{0:T(128)} %param.26) | copy-start | bytes 100
  49.0 10.1 %copy-start.7 = (f32[1152]{0:T(1024)S(1)}, f32[1152]{0:T(1024)}, u32[]{:S(2)}) copy-start(f32[1152]{0:T(1024)} %param.15) | copy-start | bytes 13828
  67.0 1.9 copy-start.2
  67.1 2.6 %copy-start.1 = (f32[512,1152]{1,0:T(8,128)S(1)}, f32[512,1152]{1,0:T(8,128)}, u32[]{:S(2)}) copy-start(f32[512,1152]{1,0:T(8,128)} %copy.81) | copy-start | bytes 7077892
  69.6 2.1 %copy-start.3 = (f32[512,384]{1,0:T(8,128)S(1)}, f32[512,384]{1,0:T(8,128)}, u32[]{:S(2)}) copy-start(f32[512,384]{1,0:T(8,128)} %copy.82) | copy-start | bytes 2359300
  118.4 8.7 %copy-start.4 = (bf16[2,64,1152]{2,1,0:T(8,128)(2,1)S(1)}, bf16[2,64,1152]{2,1,0:T(8,128)(2,1)}, u32[]{:S(2)}) copy-start(bf16[2,64,1152]{2,1,0:T(8,128)(2,1)} %copy.77) | copy-start | bytes 884740
  124.9 3.8 %copy-start.8 = (f32[1152]{0:T(1024)S(1)}, f32[1152]{0:T(1024)}, u32[]{:S(2)}) copy-start(f32[1152]{0:T(1024)} %param.18) | copy-start | bytes 13828
  171.5 14.4 %copy-start.6 = (f32[8,64,64]{2,1,0:T(8,128)S(1)}, f32[8,64,64]{2,1,0:T(8,128)}, u32[]{:S(2)}) copy-start(f32[8,64,64]{2,1,0:T(8,128)} %get-tuple-element.31) | copy-start | bytes 393220
  173.1 14.5 %copy-start.12 = (s32[8]{0:T(128)S(1)}, s32[8]{0:T(128)}, u32[]{:S(2)}) copy-start(s32[8]{0:T(128)} %param.27) | copy-start | bytes 100
  174.2 24.4 %all-to-all-start.1 = ((bf16[2,64,1152]{2,0,1:T(2,128)(2,1)}), bf16[2,64,1152]{2,0,1:T(2,128)(2,1)S(1)}, u32[]{:S(2)}, u32[]{:S(2)}) async-start(bf16[2,64,1152]{2,0,1:T(2,128)(2,1)} %copy.86), calls=%async_computation.1 | async-start | bytes 589824 | tf_op jit(solution)/shard_map/all_to_all | solution.py:411
Sparse Core Ops, SparseCore 0:
  36.0 21.4 all-gather.1

commit v6 on v5

--- a/solution.py
+++ b/solution.py
@@ -84,7 +84,12 @@
     half = rows // 2
     low_t = lax.broadcasted_iota(jnp.int32, (tree_length, 128), 1) < 64
     low_h = lax.broadcasted_iota(jnp.int32, (half, 128), 1) < 64
-    key_lanes = lax.broadcasted_iota(jnp.int32, (rows, page_length), 1)
+    key_lanes = lax.broadcasted_iota(jnp.int32, (rows, slots * page_length), 1)
+    key_slots = key_lanes // page_length
+    limit_lanes = jnp.zeros_like(key_lanes)
+    for s in range(slots):
+        limit_lanes = jnp.where(key_slots == s, limit_ref[request, s], limit_lanes)
+    cache_open = (key_lanes % page_length) < limit_lanes
     stat_lanes = lax.broadcasted_iota(jnp.int32, (rows, 128), 1)
     draft_open = jnp.concatenate([dmask_ref[0]] * 6, axis=0) > 0.5
     nt = (((1,), (1,)), ((), ()))
@@ -102,34 +107,23 @@
             jnp.where(low_t, 0.0, tiles[2]),
         ]
         qc = jnp.concatenate(blocks, axis=0).astype(jnp.bfloat16)
-        parts = []
-        for s in range(slots):
-            kc = page_refs[s][0, 0, :, lanes]
-            sc = lax.dot_general(qc, kc, nt, preferred_element_type=jnp.float32) * SCALE
-            sc = jnp.where(key_lanes < limit_ref[request, s], sc, -jnp.inf)
-            parts.append(sc)
+        keys = jnp.concatenate([page_refs[s][0, 0, :, lanes] for s in range(slots)], axis=0)
+        values = jnp.concatenate([page_refs[s][0, 1, :, lanes] for s in range(slots)], axis=0)
+        sc = lax.dot_general(qc, keys, nt, preferred_element_type=jnp.float32) * SCALE
+        sc = jnp.where(cache_open, sc, -jnp.inf)
         kd = dk_ref[0, :, lanes]
         sd = lax.dot_general(qc, kd, nt, preferred_element_type=jnp.float32) * SCALE
         sd = jnp.where(draft_open, sd, -jnp.inf)
-        peak = jnp.max(sd, axis=-1, keepdims=True)
-        for sc in parts:
-            peak = jnp.maximum(peak, jnp.max(sc, axis=-1, keepdims=True))
+        peak = jnp.maximum(jnp.max(sd, axis=-1, keepdims=True), jnp.max(sc, axis=-1, keepdims=True))
         peak_hi = peak.astype(jnp.bfloat16).astype(jnp.float32)
         peak_lo = (peak - peak_hi).astype(jnp.bfloat16).astype(jnp.float32)
         peak = peak_hi + peak_lo
         wd = jnp.exp(sd - peak)
-        total = jnp.sum(wd, axis=-1, keepdims=True)
+        ws = jnp.exp(sc - peak)
+        total = jnp.sum(wd, axis=-1, keepdims=True) + jnp.sum(ws, axis=-1, keepdims=True)
         acc = jnp.dot(
             wd.astype(jnp.bfloat16), dv_ref[0, :, lanes], preferred_element_type=jnp.float32
-        )
-        for s in range(slots):
-            ws = jnp.exp(parts[s] - peak)
-            total = total + jnp.sum(ws, axis=-1, keepdims=True)
-            acc = acc + jnp.dot(
-                ws.astype(jnp.bfloat16),
-                page_refs[s][0, 1, :, lanes],
-                preferred_element_type=jnp.float32,
-            )
+        ) + jnp.dot(ws.astype(jnp.bfloat16), values, preferred_element_type=jnp.float32)
         part_ref[0, c, 0:half, :] = jnp.where(low_h, acc[:half], acc[half:]).astype(part_ref.dtype)
         stats = jnp.where(
             stat_lanes == 0,

time: 207 us -> 198 us (0.957)
  Pallas kernels: 83.1 us -> 73.9 us
    pallas_call x1, Pallas kernels: 28.8 us -> 19.6 us  [paged_partials(): pl.pallas_call(functools.partial(paged_kernel, slots, chunks), grid_spec=...]
  transfers between devices with their start and end apart: 3 -> 3, of which waited for: 3 -> 3; matrix products, arithmetic and copies ran while one was open for 12% -> 13% of each run, Pallas kernels for 0% -> 0%
where the time goes in v6:
time: 198 us; the launch traced here: 197 us
  Pallas kernels  73.9 us (37%)
  local copies, waits for them, and re-layouts  31 us (16%)
  starting transfers between devices  25 us (13%)
  waiting for transfers between devices  21.6 us (11%)
  matrix products  20.8 us (11%)
  between operations  14.4 us (7%)
  other arithmetic  10.3 us (5%)
    pallas_call x3, Pallas kernels, exchange(): pl.pallas_call(functools.partial(exchange_kernel, count, same), in_specs=...  50.7 us
    pallas_call x1, Pallas kernels, paged_partials(): pl.pallas_call(functools.partial(paged_kernel, slots, chunks), grid_spec=...  19.6 us
    all_to_all x1, starting transfers between devices, body(): lax.all_to_all(local_rows, 'req', split_axis=1, concat_axis=1, tiled=True)  13.1 us
    all_to_all x1, starting transfers between devices, body(): lax.all_to_all(out_own, 'req', split_axis=1, concat_axis=1, tiled=True)  11.8 us
    all_to_all x1, waiting for transfers between devices, body(): lax.all_to_all(out_own, 'req', split_axis=1, concat_axis=1, tiled=True)  10.2 us
    all_to_all x1, waiting for transfers between devices, body(): lax.all_to_all(local_rows, 'req', split_axis=1, concat_axis=1, tiled=True)  9.29 us
    another operation x4, local copies, waits for them, and re-layouts, rotate_flat(): cosine = jnp.tile(jnp.concatenate([cosine, cosine], axis=-1), (1, repeats))  9.11 us
    another operation x4, local copies, waits for them, and re-layouts, rotate_flat(): sines = jnp.tile(jnp.concatenate([-sines, sines], axis=-1), (1, repeats))  7.2 us
  transfers between devices with their start and end apart: 3, of which 3 were waited for; matrix products, arithmetic and copies ran while one was open for 13% of the time, Pallas kernels for 0%

profile of v6, /device:TPU:1, one launch (start us, length us, event | category | flops | bytes accessed | tf_op | source)
XLA Modules:
  0.0 197.0 jit_solution(13015270923974952334)
XLA Ops:
  7.2 2.1 %copy.76 = bf16[2,64,1152]{2,0,1:T(2,128)(2,1)} copy(bf16[2,64,1152]{2,1,0:T(8,128)(2,1)} %bitcast.81) | data formatting | bytes 589824 | tf_op jit(solution)/shard_map/reshape | solution.py:348
  9.3 13.1 %all-to-all-start = ((bf16[2,64,1152]{2,0,1:T(2,128)(2,1)}), bf16[2,64,1152]{2,0,1:T(2,128)(2,1)S(1)}, u32[]{:S(2)}, u32[]{:S(2)}) async-start(bf16[2,64,1152]{2,0,1:T(2,128)(2,1)} %copy.76), calls=%async_computation | async-start | bytes 589824 | tf_op jit(solution)/shard_map/all_to_all | solution.py:349
  25.8 9.3 %all-to-all-done = bf16[2,64,1152]{2,0,1:T(2,128)(2,1)S(1)} async-done(((bf16[2,64,1152]{2,0,1:T(2,128)(2,1)}), bf16[2,64,1152]{2,0,1:T(2,128)(2,1)S(1)}, u32[]{:S(2)}, u32[]{:S(2)}) %all-to-all-start) | async-done | bytes 294944 | tf_op jit(solution)/shard_map/all_to_all | solution.py:349
  38.3 1.7 tile.18
  40.0 3.1 %copy.81 = f32[512,1152]{1,0:T(8,128)} copy(f32[512,1152]{0,1:T(8,128)} %bitcast.64) | data formatting | bytes 4718592 | tf_op jit(solution)/shard_map/tile | solution.py:309
  43.1 1.7 tile.16
  44.8 3.1 %copy.80 = f32[512,1152]{1,0:T(8,128)} copy(f32[512,1152]{0,1:T(8,128)} %bitcast.65) | data formatting | bytes 4718592 | tf_op jit(solution)/shard_map/tile | solution.py:308
  50.4 1.9 tile.40
  52.3 2.3 %copy.82 = f32[512,384]{1,0:T(8,128)} copy(f32[512,384]{0,1:T(8,128)} %bitcast.71) | data formatting | bytes 1572864 | tf_op jit(solution)/shard_map/tile | solution.py:308
  55.4 2.1 %all-gather.2.cloned.1.call-done = bf16[8,64,1152]{2,1,0:T(8,128)(2,1)} async-done(((bf16[2,64,1152]{2,1,0:T(8,128)(2,1)}), bf16[8,64,1152]{2,1,0:T(8,128)(2,1)}) %all-gather.2.cloned.1.call-update) | async-done | bytes 1179664 | tf_op jit(solution)/shard_map/all_gather | solution.py:350
  60.7 5.1 %convolution_convert_fusion.1 = bf16[512,1920]{1,0:T(8,128)(2,1)S(1)} fusion(bf16[512,1152]{1,0:T(8,128)(2,1)S(1)} %bitcast.76, bf16[1152,1920]{1,0:T(8,128)(2,1)} %param.16), kind=kOutput, calls=%fused_computation.1 | convolution fusion | flops 2265907200 | bytes 7569408 | tf_op jit(solution)/shard_map/dot_general | solution.py:353
  69.6 2.1 %fusion.7 = bf16[512,1152]{1,0:T(8,128)(2,1)} fusion(f32[512,1152]{1,0:T(8,128)S(1)} %copy-done.1, f32[512,32]{1,0:T(8,128)S(1)} %get-tuple-element.15, f32[512,1120]{1,0:T(8,128)S(1)} %get-tuple-element.17, f32[512,1120]{1,0:T(8,128)S(1)} %get-tuple-element.16, f32[512,32]{1,0:T(8,128)S(1)} %get-tuple-element.14, f32[512,1152]{1,0:T(8,128)S(1)} %copy-done.2, ...), kind=kLoop, calls=%fused_computation.13 | loop fusion | flops 4718592 | bytes 11797632 | tf_op jit(solution)/shard_map/convert_element_type | solution.py:365
  72.9 19.6 %paged_partials.1 = bf16[8,3,208,128]{3,2,1,0:T(8,128)(2,1)} custom-call(s32[8,5]{1,0:T(8,128)} %bitcast.83, s32[8,5]{1,0:T(8,128)} %broadcast_subtract_fusion.limit_ref, bf16[8,64,1152]{2,1,0:T(8,128)(2,1)} %bitcast.69, bf16[16,2,128,384]{3,2,1,0:T(8,128)(2,1)} %refs_5_.1, bf16[16,2,128,384]{3,2,1,0:T(8,128)(2,1)} %refs_5_.1, ...), custom_call_target="tpu_custom_call" | custom-call | flops 3321888768 | bytes 11403264 | tf_op jit(solution)/shard_map/paged_partials/pallas_call | solution.py:175
  92.5 16.7 %exchange_1.1.part_ref = bf16[4,2,3,208,128]{4,3,2,1,0:T(8,128)(2,1)} custom-call(bf16[4,2,3,208,128]{4,3,2,1,0:T(8,128)(2,1)} %bitcast.68), custom_call_target="tpu_custom_call" | custom-call | bytes 1916928 | tf_op jit(solution)/shard_map/exchange_1/pallas_call | solution.py:230
  109.2 3.6 %combine_holders.1 = bf16[2,3,192,128]{3,2,1,0:T(8,128)(2,1)} custom-call(bf16[4,2,3,208,128]{4,3,2,1,0:T(8,128)(2,1)} %exchange_1.1.part_ref), custom_call_target="tpu_custom_call" | custom-call | tf_op jit(solution)/shard_map/combine_holders/pallas_call | solution.py:282
  114.0 1.7 copy.84
  115.7 2.1 %reshape.171 = bf16[128,1152]{0,1:T(8,128)(2,1)} reshape(bf16[2,64,3,2,3,64]{1,0,5,4,3,2:T(2,128)(2,1)} %bitcast.73) | data formatting | bytes 589824 | tf_op jit(solution)/shard_map/reshape | solution.py:298
  117.9 1.7 multiply_reduce_fusion
  120.4 17.3 %exchange_2.1 = bf16[4,2,64,1152]{3,2,1,0:T(8,128)(2,1)} custom-call(bf16[1,2,64,1152]{3,2,1,0:T(8,128)(2,1)} %bitcast.80), custom_call_target="tpu_custom_call" | custom-call | bytes 1769472 | tf_op jit(solution)/shard_map/exchange_2/pallas_call | solution.py:230
  137.7 3.2 %fusion.57 = f32[512,384]{1,0:T(8,128)} fusion(bf16[512,1152]{1,0:T(8,128)(2,1)} %bitcast.77, bf16[1152,384]{1,0:T(8,128)(2,1)} %param.19), kind=kOutput, calls=%fused_computation.107 | convolution fusion | flops 452984832 | bytes 2850816 | tf_op jit(solution)/shard_map/dot_general | solution.py:394
  140.9 4.6 %convolution_convert_fusion = bf16[512,1152]{1,0:T(8,128)(2,1)} fusion(bf16[384,1152]{1,0:T(8,128)(2,1)} %param.21, bf16[512,1152]{1,0:T(8,128)(2,1)} %bitcast.78, bf16[1152,384]{1,0:T(8,128)(2,1)} %param.20, f32[512,384]{1,0:T(8,128)} %fusion.57), kind=kOutput, calls=%fused_computation | convolution fusion | flops 907739136 | bytes 4915200 | tf_op jit(solution)/shard_map/dot_general | solution.py:397
  145.5 16.8 %exchange_3.1 = bf16[4,2,64,1152]{3,2,1,0:T(8,128)(2,1)} custom-call(bf16[4,2,64,1152]{3,2,1,0:T(8,128)(2,1)} %bitcast.79), custom_call_target="tpu_custom_call" | custom-call | bytes 1769472 | tf_op jit(solution)/shard_map/exchange_3/pallas_call | solution.py:230
  165.0 11.8 %all-to-all-start.1 = ((bf16[2,64,1152]{2,0,1:T(2,128)(2,1)}), bf16[2,64,1152]{2,0,1:T(2,128)(2,1)S(1)}, u32[]{:S(2)}, u32[]{:S(2)}) async-start(bf16[2,64,1152]{2,0,1:T(2,128)(2,1)} %copy.86), calls=%async_computation.1 | async-start | bytes 589824 | tf_op jit(solution)/shard_map/all_to_all | solution.py:405
  179.2 10.2 %all-to-all-done.1 = bf16[2,64,1152]{2,0,1:T(2,128)(2,1)S(1)} async-done(((bf16[2,64,1152]{2,0,1:T(2,128)(2,1)}), bf16[2,64,1152]{2,0,1:T(2,128)(2,1)S(1)}, u32[]{:S(2)}, u32[]{:S(2)}) %all-to-all-start.1) | async-done | bytes 294944 | tf_op jit(solution)/shard_map/all_to_all | solution.py:405
  (74 shorter events, 25.6 us)
Async XLA Ops:
  7.2 110.7 %copy-start = (bf16[1152,1152]{1,0:T(8,128)(2,1)S(1)}, bf16[1152,1152]{1,0:T(8,128)(2,1)}, u32[]{:S(2)}) copy-start(bf16[1152,1152]{1,0:T(8,128)(2,1)} %param.17) | copy-start | bytes 7962628
  9.3 25.8 %all-to-all-start = ((bf16[2,64,1152]{2,0,1:T(2,128)(2,1)}), bf16[2,64,1152]{2,0,1:T(2,128)(2,1)S(1)}, u32[]{:S(2)}, u32[]{:S(2)}) async-start(bf16[2,64,1152]{2,0,1:T(2,128)(2,1)} %copy.76), calls=%async_computation | async-start | bytes 589824 | tf_op jit(solution)/shard_map/all_to_all | solution.py:349
  22.5 35.1 %all-gather.2.cloned.1.call-start = ((), (), s32[]{:S(2)}) async-start(), calls=%async_computation.2 | async-start | bytes 1474560 | tf_op jit(solution)/shard_map/all_gather | solution.py:350
  23.8 12.1 %copy-start.9 = (s32[8,1,5]{0,1,2:T(1,128)S(1)}, s32[8,1,5]{0,1,2:T(1,128)}, u32[]{:S(2)}) copy-start(s32[8,1,5]{0,1,2:T(1,128)} %param.23) | copy-start | bytes 484
  24.2 13.6 %copy-start.10 = (s32[8]{0:T(128)S(1)}, s32[8]{0:T(128)}, u32[]{:S(2)}) copy-start(s32[8]{0:T(128)} %param.24) | copy-start | bytes 100
  38.3 4.8 %copy-start.5 = (f32[512,64]{0,1:T(8,128)}, f32[512,64]{0,1:T(8,128)S(1)}, u32[]{:S(2)}) copy-start(f32[512,64]{0,1:T(8,128)S(1)} %get-tuple-element.34) | copy-start | bytes 393220
  48.0 6.7 %copy-start.11 = (s32[8]{0:T(128)S(1)}, s32[8]{0:T(128)}, u32[]{:S(2)}) copy-start(s32[8]{0:T(128)} %param.26) | copy-start | bytes 100
  49.0 10.1 %copy-start.7 = (f32[1152]{0:T(1024)S(1)}, f32[1152]{0:T(1024)}, u32[]{:S(2)}) copy-start(f32[1152]{0:T(1024)} %param.15) | copy-start | bytes 13828
  67.0 1.9 copy-start.2
  67.1 2.6 %copy-start.1 = (f32[512,1152]{1,0:T(8,128)S(1)}, f32[512,1152]{1,0:T(8,128)}, u32[]{:S(2)}) copy-start(f32[512,1152]{1,0:T(8,128)} %copy.81) | copy-start | bytes 7077892
  69.6 2.1 %copy-start.3 = (f32[512,384]{1,0:T(8,128)S(1)}, f32[512,384]{1,0:T(8,128)}, u32[]{:S(2)}) copy-start(f32[512,384]{1,0:T(8,128)} %copy.82) | copy-start | bytes 2359300
  109.2 8.7 %copy-start.4 = (bf16[2,64,1152]{2,1,0:T(8,128)(2,1)S(1)}, bf16[2,64,1152]{2,1,0:T(8,128)(2,1)}, u32[]{:S(2)}) copy-start(bf16[2,64,1152]{2,1,0:T(8,128)(2,1)} %copy.77) | copy-start | bytes 884740
  115.7 3.8 %copy-start.8 = (f32[1152]{0:T(1024)S(1)}, f32[1152]{0:T(1024)}, u32[]{:S(2)}) copy-start(f32[1152]{0:T(1024)} %param.18) | copy-start | bytes 13828
  162.3 14.4 %copy-start.6 = (f32[8,64,64]{2,1,0:T(8,128)S(1)}, f32[8,64,64]{2,1,0:T(8,128)}, u32[]{:S(2)}) copy-start(f32[8,64,64]{2,1,0:T(8,128)} %get-tuple-element.31) | copy-start | bytes 393220
  163.9 14.5 %copy-start.12 = (s32[8]{0:T(128)S(1)}, s32[8]{0:T(128)}, u32[]{:S(2)}) copy-start(s32[8]{0:T(128)} %param.27) | copy-start | bytes 100
  165.0 24.4 %all-to-all-start.1 = ((bf16[2,64,1152]{2,0,1:T(2,128)(2,1)}), bf16[2,64,1152]{2,0,1:T(2,128)(2,1)S(1)}, u32[]{:S(2)}, u32[]{:S(2)}) async-start(bf16[2,64,1152]{2,0,1:T(2,128)(2,1)} %copy.86), calls=%async_computation.1 | async-start | bytes 589824 | tf_op jit(solution)/shard_map/all_to_all | solution.py:405
Sparse Core Ops, SparseCore 0:
  36.0 21.4 all-gather.1

commit v7 on v6

--- a/solution.py
+++ b/solution.py
@@ -106,13 +106,13 @@
             jnp.where(low_t, 0.0, turned2),
             jnp.where(low_t, 0.0, tiles[2]),
         ]
-        qc = jnp.concatenate(blocks, axis=0).astype(jnp.bfloat16)
+        qc = (jnp.concatenate(blocks, axis=0) * SCALE).astype(jnp.bfloat16)
         keys = jnp.concatenate([page_refs[s][0, 0, :, lanes] for s in range(slots)], axis=0)
         values = jnp.concatenate([page_refs[s][0, 1, :, lanes] for s in range(slots)], axis=0)
-        sc = lax.dot_general(qc, keys, nt, preferred_element_type=jnp.float32) * SCALE
+        sc = lax.dot_general(qc, keys, nt, preferred_element_type=jnp.float32)
         sc = jnp.where(cache_open, sc, -jnp.inf)
         kd = dk_ref[0, :, lanes]
-        sd = lax.dot_general(qc, kd, nt, preferred_element_type=jnp.float32) * SCALE
+        sd = lax.dot_general(qc, kd, nt, preferred_element_type=jnp.float32)
         sd = jnp.where(draft_open, sd, -jnp.inf)
         peak = jnp.maximum(jnp.max(sd, axis=-1, keepdims=True), jnp.max(sc, axis=-1, keepdims=True))
         peak_hi = peak.astype(jnp.bfloat16).astype(jnp.float32)

time: 198 us -> 198 us (level)
  no operation moved by 1% of the time
where the time goes in v7:
time: 198 us; the launch traced here: 197 us
  Pallas kernels  73.9 us (37%)
  local copies, waits for them, and re-layouts  31 us (16%)
  starting transfers between devices  25 us (13%)
  waiting for transfers between devices  21.6 us (11%)
  matrix products  20.8 us (11%)
  between operations  14.4 us (7%)
  other arithmetic  10.3 us (5%)
    pallas_call x3, Pallas kernels, exchange(): pl.pallas_call(functools.partial(exchange_kernel, count, same), in_specs=...  50.7 us
    pallas_call x1, Pallas kernels, paged_partials(): pl.pallas_call(functools.partial(paged_kernel, slots, chunks), grid_spec=...  19.6 us
    all_to_all x1, starting transfers between devices, body(): lax.all_to_all(local_rows, 'req', split_axis=1, concat_axis=1, tiled=True)  13.1 us
    all_to_all x1, starting transfers between devices, body(): lax.all_to_all(out_own, 'req', split_axis=1, concat_axis=1, tiled=True)  11.8 us
    all_to_all x1, waiting for transfers between devices, body(): lax.all_to_all(out_own, 'req', split_axis=1, concat_axis=1, tiled=True)  10.2 us
    all_to_all x1, waiting for transfers between devices, body(): lax.all_to_all(local_rows, 'req', split_axis=1, concat_axis=1, tiled=True)  9.29 us
    another operation x4, local copies, waits for them, and re-layouts, rotate_flat(): cosine = jnp.tile(jnp.concatenate([cosine, cosine], axis=-1), (1, repeats))  9.11 us
    another operation x4, local copies, waits for them, and re-layouts, rotate_flat(): sines = jnp.tile(jnp.concatenate([-sines, sines], axis=-1), (1, repeats))  7.2 us
  transfers between devices with their start and end apart: 3, of which 3 were waited for; matrix products, arithmetic and copies ran while one was open for 13% of the time, Pallas kernels for 0%

profile of v7, /device:TPU:1, one launch (start us, length us, event | category | flops | bytes accessed | tf_op | source)
XLA Modules:
  0.0 197.0 jit_solution(10075947973041292854)
XLA Ops:
  7.2 2.1 %copy.76 = bf16[2,64,1152]{2,0,1:T(2,128)(2,1)} copy(bf16[2,64,1152]{2,1,0:T(8,128)(2,1)} %bitcast.81) | data formatting | bytes 589824 | tf_op jit(solution)/shard_map/reshape | solution.py:348
  9.3 13.1 %all-to-all-start = ((bf16[2,64,1152]{2,0,1:T(2,128)(2,1)}), bf16[2,64,1152]{2,0,1:T(2,128)(2,1)S(1)}, u32[]{:S(2)}, u32[]{:S(2)}) async-start(bf16[2,64,1152]{2,0,1:T(2,128)(2,1)} %copy.76), calls=%async_computation | async-start | bytes 589824 | tf_op jit(solution)/shard_map/all_to_all | solution.py:349
  25.8 9.3 %all-to-all-done = bf16[2,64,1152]{2,0,1:T(2,128)(2,1)S(1)} async-done(((bf16[2,64,1152]{2,0,1:T(2,128)(2,1)}), bf16[2,64,1152]{2,0,1:T(2,128)(2,1)S(1)}, u32[]{:S(2)}, u32[]{:S(2)}) %all-to-all-start) | async-done | bytes 294944 | tf_op jit(solution)/shard_map/all_to_all | solution.py:349
  38.3 1.7 tile.18
  40.0 3.1 %copy.81 = f32[512,1152]{1,0:T(8,128)} copy(f32[512,1152]{0,1:T(8,128)} %bitcast.64) | data formatting | bytes 4718592 | tf_op jit(solution)/shard_map/tile | solution.py:309
  43.1 1.7 tile.16
  44.8 3.1 %copy.80 = f32[512,1152]{1,0:T(8,128)} copy(f32[512,1152]{0,1:T(8,128)} %bitcast.65) | data formatting | bytes 4718592 | tf_op jit(solution)/shard_map/tile | solution.py:308
  50.4 1.9 tile.40
  52.3 2.3 %copy.82 = f32[512,384]{1,0:T(8,128)} copy(f32[512,384]{0,1:T(8,128)} %bitcast.71) | data formatting | bytes 1572864 | tf_op jit(solution)/shard_map/tile | solution.py:308
  55.4 2.1 %all-gather.2.cloned.1.call-done = bf16[8,64,1152]{2,1,0:T(8,128)(2,1)} async-done(((bf16[2,64,1152]{2,1,0:T(8,128)(2,1)}), bf16[8,64,1152]{2,1,0:T(8,128)(2,1)}) %all-gather.2.cloned.1.call-update) | async-done | bytes 1179664 | tf_op jit(solution)/shard_map/all_gather | solution.py:350
  60.7 5.1 %convolution_convert_fusion.1 = bf16[512,1920]{1,0:T(8,128)(2,1)S(1)} fusion(bf16[512,1152]{1,0:T(8,128)(2,1)S(1)} %bitcast.76, bf16[1152,1920]{1,0:T(8,128)(2,1)} %param.16), kind=kOutput, calls=%fused_computation.1 | convolution fusion | flops 2265907200 | bytes 7569408 | tf_op jit(solution)/shard_map/dot_general | solution.py:353
  69.6 2.1 %fusion.7 = bf16[512,1152]{1,0:T(8,128)(2,1)} fusion(f32[512,1152]{1,0:T(8,128)S(1)} %copy-done.1, f32[512,32]{1,0:T(8,128)S(1)} %get-tuple-element.15, f32[512,1120]{1,0:T(8,128)S(1)} %get-tuple-element.17, f32[512,1120]{1,0:T(8,128)S(1)} %get-tuple-element.16, f32[512,32]{1,0:T(8,128)S(1)} %get-tuple-element.14, f32[512,1152]{1,0:T(8,128)S(1)} %copy-done.2, ...), kind=kLoop, calls=%fused_computation.13 | loop fusion | flops 4718592 | bytes 11797632 | tf_op jit(solution)/shard_map/convert_element_type | solution.py:365
  72.9 19.6 %paged_partials.1 = bf16[8,3,208,128]{3,2,1,0:T(8,128)(2,1)} custom-call(s32[8,5]{1,0:T(8,128)} %bitcast.83, s32[8,5]{1,0:T(8,128)} %broadcast_subtract_fusion.limit_ref, bf16[8,64,1152]{2,1,0:T(8,128)(2,1)} %bitcast.69, bf16[16,2,128,384]{3,2,1,0:T(8,128)(2,1)} %refs_5_.1, bf16[16,2,128,384]{3,2,1,0:T(8,128)(2,1)} %refs_5_.1, ...), custom_call_target="tpu_custom_call" | custom-call | flops 3321888768 | bytes 11403264 | tf_op jit(solution)/shard_map/paged_partials/pallas_call | solution.py:175
  92.5 16.7 %exchange_1.1.part_ref = bf16[4,2,3,208,128]{4,3,2,1,0:T(8,128)(2,1)} custom-call(bf16[4,2,3,208,128]{4,3,2,1,0:T(8,128)(2,1)} %bitcast.68), custom_call_target="tpu_custom_call" | custom-call | bytes 1916928 | tf_op jit(solution)/shard_map/exchange_1/pallas_call | solution.py:230
  109.2 3.6 %combine_holders.1 = bf16[2,3,192,128]{3,2,1,0:T(8,128)(2,1)} custom-call(bf16[4,2,3,208,128]{4,3,2,1,0:T(8,128)(2,1)} %exchange_1.1.part_ref), custom_call_target="tpu_custom_call" | custom-call | tf_op jit(solution)/shard_map/combine_holders/pallas_call | solution.py:282
  114.0 1.7 copy.84
  115.7 2.1 %reshape.171 = bf16[128,1152]{0,1:T(8,128)(2,1)} reshape(bf16[2,64,3,2,3,64]{1,0,5,4,3,2:T(2,128)(2,1)} %bitcast.73) | data formatting | bytes 589824 | tf_op jit(solution)/shard_map/reshape | solution.py:298
  117.8 1.7 multiply_reduce_fusion
  120.4 17.3 %exchange_2.1 = bf16[4,2,64,1152]{3,2,1,0:T(8,128)(2,1)} custom-call(bf16[1,2,64,1152]{3,2,1,0:T(8,128)(2,1)} %bitcast.80), custom_call_target="tpu_custom_call" | custom-call | bytes 1769472 | tf_op jit(solution)/shard_map/exchange_2/pallas_call | solution.py:230
  137.7 3.2 %fusion.57 = f32[512,384]{1,0:T(8,128)} fusion(bf16[512,1152]{1,0:T(8,128)(2,1)} %bitcast.77, bf16[1152,384]{1,0:T(8,128)(2,1)} %param.19), kind=kOutput, calls=%fused_computation.107 | convolution fusion | flops 452984832 | bytes 2850816 | tf_op jit(solution)/shard_map/dot_general | solution.py:394
  140.9 4.6 %convolution_convert_fusion = bf16[512,1152]{1,0:T(8,128)(2,1)} fusion(bf16[384,1152]{1,0:T(8,128)(2,1)} %param.21, bf16[512,1152]{1,0:T(8,128)(2,1)} %bitcast.78, bf16[1152,384]{1,0:T(8,128)(2,1)} %param.20, f32[512,384]{1,0:T(8,128)} %fusion.57), kind=kOutput, calls=%fused_computation | convolution fusion | flops 907739136 | bytes 4915200 | tf_op jit(solution)/shard_map/dot_general | solution.py:397
  145.5 16.8 %exchange_3.1 = bf16[4,2,64,1152]{3,2,1,0:T(8,128)(2,1)} custom-call(bf16[4,2,64,1152]{3,2,1,0:T(8,128)(2,1)} %bitcast.79), custom_call_target="tpu_custom_call" | custom-call | bytes 1769472 | tf_op jit(solution)/shard_map/exchange_3/pallas_call | solution.py:230
  164.9 11.8 %all-to-all-start.1 = ((bf16[2,64,1152]{2,0,1:T(2,128)(2,1)}), bf16[2,64,1152]{2,0,1:T(2,128)(2,1)S(1)}, u32[]{:S(2)}, u32[]{:S(2)}) async-start(bf16[2,64,1152]{2,0,1:T(2,128)(2,1)} %copy.86), calls=%async_computation.1 | async-start | bytes 589824 | tf_op jit(solution)/shard_map/all_to_all | solution.py:405
  179.2 10.2 %all-to-all-done.1 = bf16[2,64,1152]{2,0,1:T(2,128)(2,1)S(1)} async-done(((bf16[2,64,1152]{2,0,1:T(2,128)(2,1)}), bf16[2,64,1152]{2,0,1:T(2,128)(2,1)S(1)}, u32[]{:S(2)}, u32[]{:S(2)}) %all-to-all-start.1) | async-done | bytes 294944 | tf_op jit(solution)/shard_map/all_to_all | solution.py:405
  (74 shorter events, 25.6 us)
Async XLA Ops:
  7.2 110.7 %copy-start = (bf16[1152,1152]{1,0:T(8,128)(2,1)S(1)}, bf16[1152,1152]{1,0:T(8,128)(2,1)}, u32[]{:S(2)}) copy-start(bf16[1152,1152]{1,0:T(8,128)(2,1)} %param.17) | copy-start | bytes 7962628
  9.3 25.8 %all-to-all-start = ((bf16[2,64,1152]{2,0,1:T(2,128)(2,1)}), bf16[2,64,1152]{2,0,1:T(2,128)(2,1)S(1)}, u32[]{:S(2)}, u32[]{:S(2)}) async-start(bf16[2,64,1152]{2,0,1:T(2,128)(2,1)} %copy.76), calls=%async_computation | async-start | bytes 589824 | tf_op jit(solution)/shard_map/all_to_all | solution.py:349
  22.5 35.1 %all-gather.2.cloned.1.call-start = ((), (), s32[]{:S(2)}) async-start(), calls=%async_computation.2 | async-start | bytes 1474560 | tf_op jit(solution)/shard_map/all_gather | solution.py:350
  23.8 12.1 %copy-start.9 = (s32[8,1,5]{0,1,2:T(1,128)S(1)}, s32[8,1,5]{0,1,2:T(1,128)}, u32[]{:S(2)}) copy-start(s32[8,1,5]{0,1,2:T(1,128)} %param.23) | copy-start | bytes 484
  24.2 13.6 %copy-start.10 = (s32[8]{0:T(128)S(1)}, s32[8]{0:T(128)}, u32[]{:S(2)}) copy-start(s32[8]{0:T(128)} %param.24) | copy-start | bytes 100
  38.3 4.8 %copy-start.5 = (f32[512,64]{0,1:T(8,128)}, f32[512,64]{0,1:T(8,128)S(1)}, u32[]{:S(2)}) copy-start(f32[512,64]{0,1:T(8,128)S(1)} %get-tuple-element.34) | copy-start | bytes 393220
  48.0 6.7 %copy-start.11 = (s32[8]{0:T(128)S(1)}, s32[8]{0:T(128)}, u32[]{:S(2)}) copy-start(s32[8]{0:T(128)} %param.26) | copy-start | bytes 100
  49.0 10.1 %copy-start.7 = (f32[1152]{0:T(1024)S(1)}, f32[1152]{0:T(1024)}, u32[]{:S(2)}) copy-start(f32[1152]{0:T(1024)} %param.15) | copy-start | bytes 13828
  67.0 1.9 copy-start.2
  67.1 2.6 %copy-start.1 = (f32[512,1152]{1,0:T(8,128)S(1)}, f32[512,1152]{1,0:T(8,128)}, u32[]{:S(2)}) copy-start(f32[512,1152]{1,0:T(8,128)} %copy.81) | copy-start | bytes 7077892
  69.6 2.1 %copy-start.3 = (f32[512,384]{1,0:T(8,128)S(1)}, f32[512,384]{1,0:T(8,128)}, u32[]{:S(2)}) copy-start(f32[512,384]{1,0:T(8,128)} %copy.82) | copy-start | bytes 2359300
  109.2 8.7 %copy-start.4 = (bf16[2,64,1152]{2,1,0:T(8,128)(2,1)S(1)}, bf16[2,64,1152]{2,1,0:T(8,128)(2,1)}, u32[]{:S(2)}) copy-start(bf16[2,64,1152]{2,1,0:T(8,128)(2,1)} %copy.77) | copy-start | bytes 884740
  115.7 3.8 %copy-start.8 = (f32[1152]{0:T(1024)S(1)}, f32[1152]{0:T(1024)}, u32[]{:S(2)}) copy-start(f32[1152]{0:T(1024)} %param.18) | copy-start | bytes 13828
  162.3 14.4 %copy-start.6 = (f32[8,64,64]{2,1,0:T(8,128)S(1)}, f32[8,64,64]{2,1,0:T(8,128)}, u32[]{:S(2)}) copy-start(f32[8,64,64]{2,1,0:T(8,128)} %get-tuple-element.31) | copy-start | bytes 393220
  163.8 14.5 %copy-start.12 = (s32[8]{0:T(128)S(1)}, s32[8]{0:T(128)}, u32[]{:S(2)}) copy-start(s32[8]{0:T(128)} %param.27) | copy-start | bytes 100
  164.9 24.4 %all-to-all-start.1 = ((bf16[2,64,1152]{2,0,1:T(2,128)(2,1)}), bf16[2,64,1152]{2,0,1:T(2,128)(2,1)S(1)}, u32[]{:S(2)}, u32[]{:S(2)}) async-start(bf16[2,64,1152]{2,0,1:T(2,128)(2,1)} %copy.86), calls=%async_computation.1 | async-start | bytes 589824 | tf_op jit(solution)/shard_map/all_to_all | solution.py:405
Sparse Core Ops, SparseCore 0:
  36.0 21.4 all-gather.1

commit v8 on v7

--- a/solution.py
+++ b/solution.py
@@ -182,7 +182,7 @@
     )(page_list, limits, queries, *([cache] * slots), draft_keys, draft_values, draft_mask)
 
 
-def exchange_kernel(count, same, x_ref, out_ref, local_sem, send_sems, recv_sems):
+def exchange_kernel(count, same, x_ref, out_ref, send_sems, recv_sems):
     me = lax.axis_index("rep")
     row = lax.axis_index("req")
     mesh_ids = pl.DeviceIdType.MESH
@@ -191,9 +191,6 @@
         peer = lax.rem(me + step, count)
         pl.semaphore_signal(barrier, inc=1, device_id=(row, peer), device_id_type=mesh_ids)
     pl.semaphore_wait(barrier, count - 1)
-    own = x_ref.at[0] if same else x_ref.at[me]
-    local = pltpu.make_async_copy(own, out_ref.at[me], local_sem)
-    local.start()
     sends = []
     for step in range(1, count):
         peer = lax.rem(me + step, count)
@@ -208,7 +205,6 @@
         )
         copy.start()
         sends.append(copy)
-    local.wait()
     for copy in sends:
         copy.wait_send()
     for step in range(1, count):
@@ -227,13 +223,12 @@
 def exchange(blocks, count, same, collective_id):
     out_shape = jax.ShapeDtypeStruct((count,) + blocks.shape[1:], blocks.dtype)
     moved = blocks[0].size * blocks.dtype.itemsize * (count - 1)
-    return pl.pallas_call(
+    moved_in = pl.pallas_call(
         functools.partial(exchange_kernel, count, same),
         in_specs=[pl.BlockSpec(memory_space=pl.ANY)],
         out_specs=pl.BlockSpec(memory_space=pl.ANY),
         out_shape=out_shape,
         scratch_shapes=[
-            pltpu.SemaphoreType.DMA(()),
             pltpu.SemaphoreType.DMA((count,)),
             pltpu.SemaphoreType.DMA((count,)),
         ],
@@ -241,6 +236,9 @@
         cost_estimate=pl.CostEstimate(flops=0, bytes_accessed=2 * moved, transcendentals=0),
         name=f"exchange_{collective_id}",
     )(blocks)
+    me = lax.axis_index("rep")
+    own = blocks[0] if same else lax.dynamic_index_in_dim(blocks, me, 0, keepdims=False)
+    return lax.dynamic_update_index_in_dim(moved_in, own, me, 0)
 
 
 def combine_kernel(part_ref, out_ref):

time: 198 us -> 203 us (1.025)
  local copies, waits for them, and re-layouts: 31 us -> 36.2 us
    dynamic_update_slice x0 -> x3, local copies, waits for them, and re-layouts: none -> 5.15 us  [exchange(): return lax.dynamic_update_index_in_dim(moved_in, own, me, 0)]
  transfers between devices with their start and end apart: 3 -> 3, of which waited for: 3 -> 3; matrix products, arithmetic and copies ran while one was open for 13% -> 12% of each run, Pallas kernels for 0% -> 0%
where the time goes in v8:
time: 203 us; the launch traced here: 202 us
  Pallas kernels  73.8 us (36%)
  local copies, waits for them, and re-layouts  36.2 us (18%)
  starting transfers between devices  25 us (12%)
  waiting for transfers between devices  21.6 us (11%)
  matrix products  20.8 us (10%)
  between operations  14.4 us (7%)
  other arithmetic  10.3 us (5%)
    pallas_call x3, Pallas kernels, exchange(): pl.pallas_call(functools.partial(exchange_kernel, count, same), in_specs=...  50.7 us
    pallas_call x1, Pallas kernels, paged_partials(): pl.pallas_call(functools.partial(paged_kernel, slots, chunks), grid_spec=...  19.6 us
    all_to_all x1, starting transfers between devices, body(): lax.all_to_all(local_rows, 'req', split_axis=1, concat_axis=1, tiled=True)  13.1 us
    all_to_all x1, starting transfers between devices, body(): lax.all_to_all(out_own, 'req', split_axis=1, concat_axis=1, tiled=True)  11.8 us
    all_to_all x1, waiting for transfers between devices, body(): lax.all_to_all(out_own, 'req', split_axis=1, concat_axis=1, tiled=True)  10.2 us
    all_to_all x1, waiting for transfers between devices, body(): lax.all_to_all(local_rows, 'req', split_axis=1, concat_axis=1, tiled=True)  9.29 us
    another operation x4, local copies, waits for them, and re-layouts, rotate_flat(): cosine = jnp.tile(jnp.concatenate([cosine, cosine], axis=-1), (1, repeats))  9.11 us
    another operation x4, local copies, waits for them, and re-layouts, rotate_flat(): sines = jnp.tile(jnp.concatenate([-sines, sines], axis=-1), (1, repeats))  7.2 us
  transfers between devices with their start and end apart: 3, of which 3 were waited for; matrix products, arithmetic and copies ran while one was open for 12% of the time, Pallas kernels for 0%

profile of v8, /device:TPU:1, one launch (start us, length us, event | category | flops | bytes accessed | tf_op | source)
XLA Modules:
  0.0 202.0 jit_solution(8018483386989383555)
XLA Ops:
  7.2 2.1 %copy.76 = bf16[2,64,1152]{2,0,1:T(2,128)(2,1)} copy(bf16[2,64,1152]{2,1,0:T(8,128)(2,1)} %bitcast.84) | data formatting | bytes 589824 | tf_op jit(solution)/shard_map/reshape | solution.py:346
  9.3 13.1 %all-to-all-start = ((bf16[2,64,1152]{2,0,1:T(2,128)(2,1)}), bf16[2,64,1152]{2,0,1:T(2,128)(2,1)S(1)}, u32[]{:S(2)}, u32[]{:S(2)}) async-start(bf16[2,64,1152]{2,0,1:T(2,128)(2,1)} %copy.76), calls=%async_computation | async-start | bytes 589824 | tf_op jit(solution)/shard_map/all_to_all | solution.py:347
  25.8 9.3 %all-to-all-done = bf16[2,64,1152]{2,0,1:T(2,128)(2,1)S(1)} async-done(((bf16[2,64,1152]{2,0,1:T(2,128)(2,1)}), bf16[2,64,1152]{2,0,1:T(2,128)(2,1)S(1)}, u32[]{:S(2)}, u32[]{:S(2)}) %all-to-all-start) | async-done | bytes 294944 | tf_op jit(solution)/shard_map/all_to_all | solution.py:347
  40.0 3.1 %copy.81 = f32[512,1152]{1,0:T(8,128)} copy(f32[512,1152]{0,1:T(8,128)} %bitcast.64) | data formatting | bytes 4718592 | tf_op jit(solution)/shard_map/tile | solution.py:307
  43.1 1.7 tile.16
  44.8 3.1 %copy.80 = f32[512,1152]{1,0:T(8,128)} copy(f32[512,1152]{0,1:T(8,128)} %bitcast.65) | data formatting | bytes 4718592 | tf_op jit(solution)/shard_map/tile | solution.py:306
  50.4 1.9 tile.40
  52.3 2.3 %copy.82 = f32[512,384]{1,0:T(8,128)} copy(f32[512,384]{0,1:T(8,128)} %bitcast.72) | data formatting | bytes 1572864 | tf_op jit(solution)/shard_map/tile | solution.py:306
  55.4 2.1 %all-gather.2.cloned.1.call-done = bf16[8,64,1152]{2,1,0:T(8,128)(2,1)} async-done(((bf16[2,64,1152]{2,1,0:T(8,128)(2,1)}), bf16[8,64,1152]{2,1,0:T(8,128)(2,1)}) %all-gather.2.cloned.1.call-update) | async-done | bytes 1179664 | tf_op jit(solution)/shard_map/all_gather | solution.py:348
  60.7 5.1 %convolution_convert_fusion.1 = bf16[512,1920]{1,0:T(8,128)(2,1)S(1)} fusion(bf16[512,1152]{1,0:T(8,128)(2,1)S(1)} %bitcast.81, bf16[1152,1920]{1,0:T(8,128)(2,1)} %param.16), kind=kOutput, calls=%fused_computation.1 | convolution fusion | flops 2265907200 | bytes 7569408 | tf_op jit(solution)/shard_map/dot_general | solution.py:351
  69.6 2.1 %fusion.7 = bf16[512,1152]{1,0:T(8,128)(2,1)} fusion(f32[512,1152]{1,0:T(8,128)S(1)} %copy-done.1, f32[512,32]{1,0:T(8,128)S(1)} %get-tuple-element.15, f32[512,1120]{1,0:T(8,128)S(1)} %get-tuple-element.17, f32[512,1120]{1,0:T(8,128)S(1)} %get-tuple-element.16, f32[512,32]{1,0:T(8,128)S(1)} %get-tuple-element.14, f32[512,1152]{1,0:T(8,128)S(1)} %copy-done.2, ...), kind=kLoop, calls=%fused_computation.13 | loop fusion | flops 4718592 | bytes 11797632 | tf_op jit(solution)/shard_map/convert_element_type | solution.py:363
  72.9 19.6 %paged_partials.1 = bf16[8,3,208,128]{3,2,1,0:T(8,128)(2,1)} custom-call(s32[8,5]{1,0:T(8,128)} %bitcast.86, s32[8,5]{1,0:T(8,128)} %broadcast_subtract_fusion.limit_ref, bf16[8,64,1152]{2,1,0:T(8,128)(2,1)} %bitcast.70, bf16[16,2,128,384]{3,2,1,0:T(8,128)(2,1)} %refs_5_.1, bf16[16,2,128,384]{3,2,1,0:T(8,128)(2,1)} %refs_5_.1, ...), custom_call_target="tpu_custom_call" | custom-call | flops 3321888768 | bytes 11403264 | tf_op jit(solution)/shard_map/paged_partials/pallas_call | solution.py:175
  92.5 16.6 %exchange_1.1 = bf16[4,2,3,208,128]{4,3,2,1,0:T(8,128)(2,1)} custom-call(bf16[4,2,3,208,128]{4,3,2,1,0:T(8,128)(2,1)} %bitcast.66), custom_call_target="tpu_custom_call" | custom-call | bytes 1916928 | tf_op jit(solution)/shard_map/exchange_1/pallas_call | solution.py:226
  109.2 1.7 dynamic-slice_dynamic-update-slice_fusion.part_ref
  110.9 3.5 %combine_holders.1 = bf16[2,3,192,128]{3,2,1,0:T(8,128)(2,1)} custom-call(bf16[4,2,3,208,128]{4,3,2,1,0:T(8,128)(2,1)} %dynamic-slice_dynamic-update-slice_fusion.part_ref), custom_call_target="tpu_custom_call" | custom-call | tf_op jit(solution)/shard_map/combine_holders/pallas_call | solution.py:280
  115.7 1.7 copy.84
  117.4 2.1 %reshape.172 = bf16[128,1152]{0,1:T(8,128)(2,1)} reshape(bf16[2,64,3,2,3,64]{1,0,5,4,3,2:T(2,128)(2,1)} %bitcast.76) | data formatting | bytes 589824 | tf_op jit(solution)/shard_map/reshape | solution.py:296
  122.1 17.3 %exchange_2.1 = bf16[4,2,64,1152]{3,2,1,0:T(8,128)(2,1)} custom-call(bf16[1,2,64,1152]{3,2,1,0:T(8,128)(2,1)} %bitcast.74), custom_call_target="tpu_custom_call" | custom-call | bytes 1769472 | tf_op jit(solution)/shard_map/exchange_2/pallas_call | solution.py:226
  141.1 3.2 %fusion.57 = f32[512,384]{1,0:T(8,128)} fusion(bf16[512,1152]{1,0:T(8,128)(2,1)} %bitcast.82, bf16[1152,384]{1,0:T(8,128)(2,1)} %param.19), kind=kOutput, calls=%fused_computation.110 | convolution fusion | flops 452984832 | bytes 2850816 | tf_op jit(solution)/shard_map/dot_general | solution.py:392
  144.3 4.6 %convolution_convert_fusion = bf16[512,1152]{1,0:T(8,128)(2,1)} fusion(bf16[384,1152]{1,0:T(8,128)(2,1)} %param.21, bf16[512,1152]{1,0:T(8,128)(2,1)} %bitcast.83, bf16[1152,384]{1,0:T(8,128)(2,1)} %param.20, f32[512,384]{1,0:T(8,128)} %fusion.57), kind=kOutput, calls=%fused_computation | convolution fusion | flops 907739136 | bytes 4915200 | tf_op jit(solution)/shard_map/dot_general | solution.py:395
  148.9 16.7 %exchange_3.1 = bf16[4,2,64,1152]{3,2,1,0:T(8,128)(2,1)} custom-call(bf16[4,2,64,1152]{3,2,1,0:T(8,128)(2,1)} %bitcast.77), custom_call_target="tpu_custom_call" | custom-call | bytes 1769472 | tf_op jit(solution)/shard_map/exchange_3/pallas_call | solution.py:226
  165.7 1.7 dynamic-slice_dynamic-update-slice_fusion.1
  170.0 11.8 %all-to-all-start.1 = ((bf16[2,64,1152]{2,0,1:T(2,128)(2,1)}), bf16[2,64,1152]{2,0,1:T(2,128)(2,1)S(1)}, u32[]{:S(2)}, u32[]{:S(2)}) async-start(bf16[2,64,1152]{2,0,1:T(2,128)(2,1)} %copy.86), calls=%async_computation.1 | async-start | bytes 589824 | tf_op jit(solution)/shard_map/all_to_all | solution.py:403
  184.3 10.2 %all-to-all-done.1 = bf16[2,64,1152]{2,0,1:T(2,128)(2,1)S(1)} async-done(((bf16[2,64,1152]{2,0,1:T(2,128)(2,1)}), bf16[2,64,1152]{2,0,1:T(2,128)(2,1)S(1)}, u32[]{:S(2)}, u32[]{:S(2)}) %all-to-all-start.1) | async-done | bytes 294944 | tf_op jit(solution)/shard_map/all_to_all | solution.py:403
  (77 shorter events, 30.7 us)
Async XLA Ops:
  7.2 112.4 %copy-start = (bf16[1152,1152]{1,0:T(8,128)(2,1)S(1)}, bf16[1152,1152]{1,0:T(8,128)(2,1)}, u32[]{:S(2)}) copy-start(bf16[1152,1152]{1,0:T(8,128)(2,1)} %param.17) | copy-start | bytes 7962628
  9.3 25.8 %all-to-all-start = ((bf16[2,64,1152]{2,0,1:T(2,128)(2,1)}), bf16[2,64,1152]{2,0,1:T(2,128)(2,1)S(1)}, u32[]{:S(2)}, u32[]{:S(2)}) async-start(bf16[2,64,1152]{2,0,1:T(2,128)(2,1)} %copy.76), calls=%async_computation | async-start | bytes 589824 | tf_op jit(solution)/shard_map/all_to_all | solution.py:347
  22.5 35.1 %all-gather.2.cloned.1.call-start = ((), (), s32[]{:S(2)}) async-start(), calls=%async_computation.2 | async-start | bytes 1474560 | tf_op jit(solution)/shard_map/all_gather | solution.py:348
  23.8 12.1 %copy-start.9 = (s32[8,1,5]{0,1,2:T(1,128)S(1)}, s32[8,1,5]{0,1,2:T(1,128)}, u32[]{:S(2)}) copy-start(s32[8,1,5]{0,1,2:T(1,128)} %param.23) | copy-start | bytes 484
  24.2 13.6 %copy-start.10 = (s32[8]{0:T(128)S(1)}, s32[8]{0:T(128)}, u32[]{:S(2)}) copy-start(s32[8]{0:T(128)} %param.24) | copy-start | bytes 100
  38.3 4.8 %copy-start.5 = (f32[512,64]{0,1:T(8,128)}, f32[512,64]{0,1:T(8,128)S(1)}, u32[]{:S(2)}) copy-start(f32[512,64]{0,1:T(8,128)S(1)} %get-tuple-element.34) | copy-start | bytes 393220
  48.0 6.7 %copy-start.11 = (s32[8]{0:T(128)S(1)}, s32[8]{0:T(128)}, u32[]{:S(2)}) copy-start(s32[8]{0:T(128)} %param.26) | copy-start | bytes 100
  49.0 10.1 %copy-start.7 = (f32[1152]{0:T(1024)S(1)}, f32[1152]{0:T(1024)}, u32[]{:S(2)}) copy-start(f32[1152]{0:T(1024)} %param.15) | copy-start | bytes 13828
  67.0 1.9 copy-start.2
  67.1 2.6 %copy-start.1 = (f32[512,1152]{1,0:T(8,128)S(1)}, f32[512,1152]{1,0:T(8,128)}, u32[]{:S(2)}) copy-start(f32[512,1152]{1,0:T(8,128)} %copy.81) | copy-start | bytes 7077892
  69.6 2.1 %copy-start.3 = (f32[512,384]{1,0:T(8,128)S(1)}, f32[512,384]{1,0:T(8,128)}, u32[]{:S(2)}) copy-start(f32[512,384]{1,0:T(8,128)} %copy.82) | copy-start | bytes 2359300
  110.9 8.7 %copy-start.4 = (bf16[2,64,1152]{2,1,0:T(8,128)(2,1)S(1)}, bf16[2,64,1152]{2,1,0:T(8,128)(2,1)}, u32[]{:S(2)}) copy-start(bf16[2,64,1152]{2,1,0:T(8,128)(2,1)} %copy.77) | copy-start | bytes 884740
  117.4 3.8 %copy-start.8 = (f32[1152]{0:T(1024)S(1)}, f32[1152]{0:T(1024)}, u32[]{:S(2)}) copy-start(f32[1152]{0:T(1024)} %param.18) | copy-start | bytes 13828
  167.4 14.4 %copy-start.6 = (f32[8,64,64]{2,1,0:T(8,128)S(1)}, f32[8,64,64]{2,1,0:T(8,128)}, u32[]{:S(2)}) copy-start(f32[8,64,64]{2,1,0:T(8,128)} %get-tuple-element.31) | copy-start | bytes 393220
  168.9 14.5 %copy-start.12 = (s32[8]{0:T(128)S(1)}, s32[8]{0:T(128)}, u32[]{:S(2)}) copy-start(s32[8]{0:T(128)} %param.27) | copy-start | bytes 100
  170.0 24.4 %all-to-all-start.1 = ((bf16[2,64,1152]{2,0,1:T(2,128)(2,1)}), bf16[2,64,1152]{2,0,1:T(2,128)(2,1)S(1)}, u32[]{:S(2)}, u32[]{:S(2)}) async-start(bf16[2,64,1152]{2,0,1:T(2,128)(2,1)} %copy.86), calls=%async_computation.1 | async-start | bytes 589824 | tf_op jit(solution)/shard_map/all_to_all | solution.py:403
Sparse Core Ops, SparseCore 0:
  36.0 21.4 all-gather.1
